TPU v7x, 128 devices: a whole 4x4x4 slice. The times are simulated.
128 devices in a mesh: gx: 8 (over x_hi, z), gy: 4 (over x_lo, core), gz: 4 (over y).
Axes of the slice: x: 4 (x_hi: 2, x_lo: 2; x = x_hi * 2 + x_lo), y: 4, z: 4, core: 2. Of those that a mesh axis runs over, the one named last changes fastest.
Arguments:
- panel: float32 [128, 524288], P(None, ('gx', 'gy', 'gz')), may hold values from -3000 to 3000
- trailing: float32 [64, 524288], P(None, ('gx', 'gy', 'gz')), may hold values from -6 to 6
Outputs:
- basis: float32 [128, 524288], P(None, ('gx', 'gy', 'gz'))
- upper: float32 [128, 128], replicated
- coupling: float32 [128, 64], replicated
- updated: float32 [64, 524288], P(None, ('gx', 'gy', 'gz'))
All inputs are finite; a program needn't handle non-finite values.
Results may differ from a plain program's by a relative error of at most 0.0033.
Values sent between devices are 32-bit elements; how exact they have to be, the bound alone decides.
No kernel may reach another device: no remote copies, remote signals or barrier semaphores. Data moves between devices by JAX's collectives and lax.ppermute only.
A program may use at most 64 MiB of HBM per device.

v0:
```python
import jax
import jax.numpy as jnp
from jax import lax
from jax.experimental import pallas as pl
from jax.experimental.pallas import tpu as pltpu
from jax.sharding import PartitionSpec as P

AXES = ("gx", "gy", "gz")
HIGHEST = lax.Precision.HIGHEST
F32 = jnp.float32
BF16 = jnp.bfloat16
CHUNK = 1024
PANEL_COLS = 8
SMALL = 4e-3
MAGIC = 1.5 * 2.0**23


def round_int(x):
    return (x + MAGIC) - MAGIC


def two_sum(a, b):
    total = a + b
    part = total - a
    return total, (a - (total - part)) + (b - part)


def snap(x):
    c = x * 4097.0
    return c - (c - x)


def power_below(x):
    p = snap(jnp.exp2(jnp.floor(jnp.log2(jnp.maximum(x, 1e-30)))))
    return p, snap(1.0 / p)


def slices(hi, lo, count):
    digits = []
    for k in range(count):
        d = round_int(hi)
        digits.append(d)
        if k < count - 1:
            hi = (hi - d) * 256.0
            if lo is not None:
                lo = lo * 256.0
                new = hi + lo
                lo = lo - (new - hi)
                hi = new
    return digits


def nt(a, b, **kw):
    return lax.dot_general(a, b, (((1,), (1,)), ((), ())), preferred_element_type=F32, **kw)


def nn(a, b, **kw):
    return lax.dot_general(a, b, (((1,), (0,)), ((), ())), preferred_element_type=F32, **kw)


def iota(shape, axis):
    return lax.broadcasted_iota(jnp.int32, shape, axis)


def gram_kernel(core_ref, panel_ref, trail_ref, keep_ref, send_ref, ops, hi_ref, lo_ref, ca_ref):
    step = pl.program_id(0)
    n, t = panel_ref.shape[0], trail_ref.shape[0]

    @pl.when(step == 0)
    def _():
        hi_ref[...] = jnp.zeros_like(hi_ref)
        lo_ref[...] = jnp.zeros_like(lo_ref)
        ca_ref[...] = jnp.zeros_like(ca_ref)

    x = panel_ref[...]
    p, inv = power_below(jnp.max(jnp.abs(x), axis=1, keepdims=True))
    a = x * (inv * 64.0)
    d1 = round_int(a)
    r1 = (a - d1) * 256.0
    d2 = round_int(r1)
    ops[0:n, :] = d1.astype(BF16)
    ops[n : 2 * n, :] = d2.astype(BF16)
    ops[2 * n : 3 * n, :] = ((r1 - d2) * 256.0).astype(BF16)
    c = trail_ref[...]
    c1 = c.astype(BF16)
    rc = c - c1.astype(F32)
    c2 = rc.astype(BF16)
    ops[3 * n : 3 * n + t, :] = c1
    ops[3 * n + t : 3 * n + 2 * t, :] = c2
    ops[3 * n + 2 * t : 3 * n + 3 * t, :] = (rc - c2.astype(F32)).astype(BF16)

    m = nt(ops[...], ops[0 : 3 * n, :])

    def blk(i, j):
        return m[i * n : (i + 1) * n, j * n : (j + 1) * n]

    def cblk(i, j):
        return m[3 * n + i * t : 3 * n + (i + 1) * t, j * n : (j + 1) * n]

    row = jnp.broadcast_to(p * (1.0 / 64.0), (n, n))
    col = row.T
    scale = row * col
    h, e = two_sum(blk(0, 0), (blk(0, 1) + blk(1, 0)) * 2.0**-8)
    rest = (blk(0, 2) + blk(2, 0) + blk(1, 1)) * 2.0**-16
    rest = rest + ((blk(1, 2) + blk(2, 1)) * 2.0**-24 + blk(2, 2) * 2.0**-32)
    hi, err = two_sum(hi_ref[...], h * scale)
    hi_ref[...] = hi
    lo_ref[...] += err + (e + rest) * scale
    ca = (cblk(2, 0) + cblk(1, 1) * 2.0**-8 + cblk(0, 2) * 2.0**-16) + (cblk(1, 0) + cblk(0, 1) * 2.0**-8)
    ca_ref[...] += (ca + cblk(0, 0)) * col[0:t, :]

    @pl.when(step == pl.num_programs(0) - 1)
    def _():
        core = core_ref[0]
        half = n // 2
        i, j = iota((half, n), 0), iota((half, n), 1)

        def fold(g):
            top, bottom = g[:half, :], g[half:, :]
            body = jnp.where((j >= half) & (i >= j - half), pltpu.roll(top, half, 1), bottom)
            diag = jnp.sum(jnp.where(i == j - half, bottom, 0.0), axis=0, keepdims=True)
            return body, jnp.broadcast_to(diag, (8, n))

        hi_body, hi_diag = fold(hi_ref[...])
        lo_body, lo_diag = fold(lo_ref[...])
        ca = ca_ref[...]
        q = half // 2
        tq = t // 2

        def put(ref, first):
            def pick(v, size):
                return jnp.where(first, v[:size, :], v[size:, :])

            ref[0:q, :] = pick(hi_body, q)
            ref[q : q + 8, :] = hi_diag
            ref[q + 8 : 2 * q + 8, :] = pick(lo_body, q)
            ref[2 * q + 8 : 2 * q + 16, :] = lo_diag
            ref[2 * q + 16 :, :] = pick(ca, tq)

        put(keep_ref, core == 0)
        put(send_ref, core == 1)


def local_gram(core, panel, trailing):
    n, rows = panel.shape
    t = trailing.shape[0]
    out = jax.ShapeDtypeStruct((n // 2 + 16 + t // 2, n), F32)
    whole = pl.BlockSpec(out.shape, lambda i: (0, 0))
    return pl.pallas_call(
        gram_kernel,
        grid=(rows // CHUNK,),
        in_specs=[
            pl.BlockSpec(memory_space=pltpu.SMEM),
            pl.BlockSpec((n, CHUNK), lambda i: (0, i)),
            pl.BlockSpec((t, CHUNK), lambda i: (0, i)),
        ],
        out_specs=[whole, whole],
        out_shape=[out, out],
        scratch_shapes=[
            pltpu.VMEM((3 * (n + t), CHUNK), BF16),
            pltpu.VMEM((n, n), F32),
            pltpu.VMEM((n, n), F32),
            pltpu.VMEM((t, n), F32),
        ],
        compiler_params=pltpu.CompilerParams(vmem_limit_bytes=32 << 20),
        name="gram",
    )(core, panel, trailing)


def add_pair(a, b, words):
    hi, err = two_sum(a[:words, :], b[:words, :])
    return hi, (a[words : 2 * words, :] + b[words : 2 * words, :]) + err, a[2 * words :, :] + b[2 * words :, :]


def add_kernel(words, *refs):
    *ins, out = refs
    parts = [add_pair(ins[k][...], ins[k + 1][...], words) for k in range(0, len(ins), 2)]
    total = parts[0]
    if len(parts) == 2:
        hi, err = two_sum(parts[0][0], parts[1][0])
        total = (hi, (parts[0][1] + parts[1][1]) + err, parts[0][2] + parts[1][2])
    out[:words, :] = total[0]
    out[words : 2 * words, :] = total[1]
    out[2 * words :, :] = total[2]


def add_packed(words, *arrays):
    spec = pl.BlockSpec(memory_space=pltpu.VMEM)
    return pl.pallas_call(
        lambda *refs: add_kernel(words, *refs),
        in_specs=[spec] * len(arrays),
        out_specs=spec,
        out_shape=jax.ShapeDtypeStruct(arrays[0].shape, F32),
        name="add_packed",
    )(*arrays)


def exchange(value, mask):
    size = lax.axis_size(AXES)
    return lax.ppermute(value, AXES, [(s, s ^ mask) for s in range(size)])


def chol_inv(s):
    blocks = len(s)
    n = 8 * blocks
    rid, lid = iota((8, n), 0), iota((8, n), 1)
    w = [jnp.where(lid == rid + 8 * r, 1.0, 0.0) for r in range(blocks)]
    s = list(s)
    for first in range(0, n, PANEL_COLS):
        r0 = first // 8
        cols = [
            [jnp.broadcast_to(s[r][:, first + k : first + k + 1], (8, n)) for r in range(r0, blocks)]
            for k in range(PANEL_COLS)
        ]
        scales = []
        for k in range(PANEL_COLS):
            pivot = cols[k][0][k : k + 1, :]
            inv = 1.0 / pivot
            mult = [c * inv for c in cols[k]]
            mult[0] = jnp.where(rid > k, mult[0], 0.0)
            for later in range(k + 1, PANEL_COLS):
                e = cols[later][0][k : k + 1, :]
                cols[later] = [c - m * e for c, m in zip(cols[later], mult)]
            srow, wrow = s[r0][k : k + 1, :], w[r0][k : k + 1, :]
            for i, m in enumerate(mult):
                s[r0 + i] = s[r0 + i] - m * srow
                w[r0 + i] = w[r0 + i] - m * wrow
            scales.append(lax.rsqrt(pivot))
        for k, d in enumerate(scales):
            w[r0] = jnp.where(rid == k, w[r0] * d, w[r0])
    return w


def factor_kernel(rows_all, core_ref, own_ref, other_ref, wz_ref, upper_ref, coup_ref, wcat, gcat, tcat, v_ref):
    n = upper_ref.shape[0]
    t = coup_ref.shape[1]
    half, q, tq = n // 2, n // 4, t // 2
    first = core_ref[0] == 0
    own, other = own_ref[...], other_ref[...]
    a, b = jnp.where(first, own, other), jnp.where(first, other, own)
    i, j = iota((n, n), 0), iota((n, n), 1)
    hi_, hj_ = iota((half, n), 0), iota((half, n), 1)

    def unfold(start):
        body = jnp.concatenate([a[start : start + q, :], b[start : start + q, :]], axis=0)
        diag = jnp.broadcast_to(a[start + q : start + q + 1, :], (half, n))
        top = jnp.where((hj_ < half) & (hi_ >= hj_), pltpu.roll(body, half, 1), 0.0)
        keep = jnp.where((hj_ < half) | (hi_ < hj_ - half), body, 0.0)
        bottom = jnp.where(hi_ == hj_ - half, diag, keep)
        part = jnp.concatenate([top, bottom], axis=0)
        return jnp.where(i == j, part, part + part.T)

    g_hi, g_lo = unfold(0), unfold(q + 8)
    ca = jnp.concatenate([a[2 * q + 16 :, :], b[2 * q + 16 :, :]], axis=0)
    g_hi, g_lo = two_sum(g_hi, g_lo)

    diag = jnp.sum(jnp.where(i == j, g_hi, 0.0), axis=0, keepdims=True)
    pc, inv_pc = power_below(jnp.sqrt(diag))
    ic = jnp.broadcast_to(inv_pc, (n, n))
    eq = ic * ic.T
    s_hi, s_lo = g_hi * eq, g_lo * eq

    w = jnp.concatenate(chol_inv([s_hi[8 * r : 8 * r + 8, :] for r in range(n // 8)]), axis=0)

    qr, inv_qr = power_below(jnp.max(jnp.abs(w), axis=1, keepdims=True))
    wd = slices(w * (inv_qr * 64.0), None, 3)
    qs = qr * (1.0 / 64.0)
    wt = (wd[0] + wd[1] * 2.0**-8 + wd[2] * 2.0**-16) * qs
    for k in range(3):
        wcat[:, k * n : (k + 1) * n] = wd[k].astype(BF16)
    gd = slices(s_hi * 32.0, s_lo * 32.0, 6)
    for k in range(6):
        gcat[(5 - k) * n : (6 - k) * n, :] = gd[k].astype(BF16)

    def weigh(parts):
        hi, lo = parts[0], None
        for k, part in enumerate(parts[1:]):
            hi, err = two_sum(hi, part * 2.0 ** (-8 * (k + 1)))
            lo = err if lo is None else lo + err
        return two_sum(hi, lo)

    def t_level(k):
        width = min(k + 1, 3) * n
        return nn(wcat[:, 0:width], gcat[(5 - k) * n : (5 - k) * n + width, :])

    t_hi, t_lo = weigh([t_level(k) for k in range(6)])
    tau, inv_tau = power_below(jnp.max(jnp.abs(t_hi), axis=1, keepdims=True))
    td = slices(t_hi * (inv_tau * 64.0), t_lo * (inv_tau * 64.0), 4)
    for k in range(4):
        tcat[:, (3 - k) * n : (4 - k) * n] = td[k].astype(BF16)

    def m_level(k):
        width = min(k + 1, 3) * n
        return nt(tcat[:, (3 - k) * n : (3 - k) * n + width], wcat[:, 0:width])

    m_hi, m_lo = weigh([m_level(k) for k in range(4)])
    qb = jnp.broadcast_to(qs, (n, n))
    scale = qb.T * (qb * (tau * (1.0 / 2048.0)))
    e = (m_hi * scale - jnp.where(i == j, 1.0, 0.0)) + m_lo * scale

    def phi(x):
        return jnp.where(i > j, x, jnp.where(i == j, 0.5 * x, 0.0))

    f = phi(e)
    size = jnp.sum(f * f)

    @pl.when(size <= SMALL * SMALL)
    def _():
        fb = f.astype(BF16)
        v_ref[...] = (jnp.where(i == j, 1.0, 0.0) - f) + (phi(nt(fb, fb)) + nn(fb, fb))

    @pl.when(jnp.logical_not(size <= SMALL * SMALL))
    def _():
        lower = jnp.where(i >= j, e, 0.0)
        full = jnp.where(i == j, e + 1.0, lower + lower.T)
        blocks = chol_inv([full[8 * r : 8 * r + 8, :] for r in range(n // 8)])
        for r in range(n // 8):
            v_ref[8 * r : 8 * r + 8, :] = blocks[r]

    v = v_ref[...]
    w_new = nn(v, wt, precision=HIGHEST) * ic
    t_true = t_hi * (qs * (1.0 / 32.0)) * jnp.broadcast_to(pc, (n, n))
    root = jnp.sqrt(jnp.float32(rows_all))
    upper_ref[...] = jnp.where(i <= j, nn(v, t_true, precision=HIGHEST) / root, 0.0)
    coupling = nt(w_new, ca, precision=HIGHEST)
    coup_ref[...] = coupling
    wz_ref[:n, :] = w_new * root
    wz_ref[n:, :] = lax.dot_general(coupling, w_new, (((0,), (0,)), ((), ())), preferred_element_type=F32, precision=HIGHEST)


def factor(core, own, other, n, t, rows_all):
    spec = pl.BlockSpec(memory_space=pltpu.VMEM)
    return pl.pallas_call(
        lambda *refs: factor_kernel(rows_all, *refs),
        in_specs=[pl.BlockSpec(memory_space=pltpu.SMEM), spec, spec],
        out_specs=[spec] * 3,
        out_shape=[
            jax.ShapeDtypeStruct((n + t, n), F32),
            jax.ShapeDtypeStruct((n, n), F32),
            jax.ShapeDtypeStruct((n, t), F32),
        ],
        scratch_shapes=[
            pltpu.VMEM((n, 3 * n), BF16),
            pltpu.VMEM((6 * n, n), BF16),
            pltpu.VMEM((n, 4 * n), BF16),
            pltpu.VMEM((n, n), F32),
        ],
        compiler_params=pltpu.CompilerParams(vmem_limit_bytes=32 << 20),
        name="factor",
    )(core, own, other)


def shards(panel, trailing):
    n, t = panel.shape[0], trailing.shape[0]
    rows_all = panel.shape[1] * lax.axis_size(AXES)
    core = jnp.reshape(lax.axis_index("gy") % 2, (1,)).astype(jnp.int32)
    words = n // 4 + 8
    keep, send = local_gram(core, panel, trailing)
    total = add_packed(words, keep, exchange(send, 4))
    for masks in ((1, 3, 2), (8, 72, 64), (16, 48, 32)):
        near, wrap, far = (exchange(total, m) for m in masks)
        total = add_packed(words, total, near, far, wrap)
    other = exchange(total, 4)
    wz, upper, coupling = factor(core, total, other, n, t, rows_all)
    basis_t = nn(wz[:n], panel, precision=HIGHEST)
    updated = trailing - nn(wz[n:], panel, precision=HIGHEST)
    return basis_t, upper, coupling, updated


def solution(mesh):
    placed = (P(None, AXES), P(None, AXES))
    return jax.shard_map(
        shards,
        mesh=mesh,
        in_specs=placed,
        out_specs=(P(None, AXES), P(), P(), P(None, AXES)),
        check_vma=False,
    )
```

profile of v0, /device:TPU:1, one launch (start us, length us, event | category | flops | bytes accessed | tf_op | source)
XLA Modules:
  0.0 63.9 jit_solution(9131871977511172129)
XLA Ops:
  0.7 1.6 %copy-done = f32[128,4096]{1,0:T(8,128)S(1)} copy-done((f32[128,4096]{1,0:T(8,128)S(1)}, f32[128,4096]{1,0:T(8,128)}, u32[]{:S(2)}) %copy-start) | copy-done | bytes 2097176
  2.2 1.2 %copy-done.2 = f32[64,4096]{1,0:T(8,128)S(1)} copy-done((f32[64,4096]{1,0:T(8,128)S(1)}, f32[64,4096]{1,0:T(8,128)}, u32[]{:S(2)}) %copy-start.2) | copy-done | bytes 1048600
  3.5 4.2 %gram.1 = (f32[112,128]{1,0:T(8,128)S(1)}, f32[112,128]{1,0:T(8,128)S(1)}) custom-call(s32[1]{0:T(128)} %bitcast.core_ref.refs_0_, f32[128,4096]{1,0:T(8,128)S(1)} %copy-done, f32[64,4096]{1,0:T(8,128)S(1)} %copy-done.2), custom_call_target="tpu_custom_call" | custom-call | tf_op jit(solution)/shard_map/gram/pallas_call | solution.py:149
  8.3 1.4 %collective-permute-start = (f32[112,128]{1,0:T(8,128)S(1)}, f32[112,128]{1,0:T(8,128)S(1)}, u32[]{:S(2)}, u32[]{:S(2)}) collective-permute-start(f32[112,128]{1,0:T(8,128)S(1)} %get-tuple-element.10), channel_id=1, source_target_pairs={{0,4},{1,5},{2,6},{3,7},{4,0},{5,1},{6,2},{7,3},{8,12},{9,13},{10,... | collective-permute-start | bytes 172040 | tf_op jit(solution)/shard_map/ppermute | solution.py:200
  9.7 0.9 %collective-permute-done.refs_1_ = f32[112,128]{1,0:T(8,128)S(1)} collective-permute-done((f32[112,128]{1,0:T(8,128)S(1)}, f32[112,128]{1,0:T(8,128)S(1)}, u32[]{:S(2)}, u32[]{:S(2)}) %collective-permute-start) | collective-permute-done | bytes 57376 | tf_op jit(solution)/shard_map/ppermute | solution.py:200
  11.2 1.5 %add_packed.4.refs_0_ = f32[112,128]{1,0:T(8,128)} custom-call(f32[112,128]{1,0:T(8,128)} %copy-done.5, f32[112,128]{1,0:T(8,128)} %copy-done.15), custom_call_target="tpu_custom_call" | custom-call | tf_op jit(solution)/shard_map/add_packed/pallas_call | solution.py:189
  12.7 2.8 %collective-permute-start.3 = (f32[112,128]{1,0:T(8,128)}, f32[112,128]{1,0:T(8,128)S(1)}, u32[]{:S(2)}, u32[]{:S(2)}) collective-permute-start(f32[112,128]{1,0:T(8,128)} %add_packed.4.refs_0_), channel_id=1, source_target_pairs={{0,3},{1,2},{2,1},{3,0},{4,7},{5,6},{6,5},{7,4},{8,11},{9,10},{10,... | collective-permute-start | bytes 172040 | tf_op jit(solution)/shard_map/ppermute | solution.py:200
  16.1 1.6 %collective-permute-done.3.refs_3_ = f32[112,128]{1,0:T(8,128)S(1)} collective-permute-done((f32[112,128]{1,0:T(8,128)}, f32[112,128]{1,0:T(8,128)S(1)}, u32[]{:S(2)}, u32[]{:S(2)}) %collective-permute-start.3) | collective-permute-done | bytes 57376 | tf_op jit(solution)/shard_map/ppermute | solution.py:200
  17.7 2.6 %collective-permute-done.2.refs_2_ = f32[112,128]{1,0:T(8,128)S(1)} collective-permute-done((f32[112,128]{1,0:T(8,128)}, f32[112,128]{1,0:T(8,128)S(1)}, u32[]{:S(2)}, u32[]{:S(2)}) %collective-permute-start.2) | collective-permute-done | bytes 57376 | tf_op jit(solution)/shard_map/ppermute | solution.py:200
  21.5 1.5 %add_packed.5.refs_0_ = f32[112,128]{1,0:T(8,128)} custom-call(f32[112,128]{1,0:T(8,128)} %add_packed.4.refs_0_, f32[112,128]{1,0:T(8,128)} %copy-done.12, f32[112,128]{1,0:T(8,128)} %copy-done.9, f32[112,128]{1,0:T(8,128)} %copy-done.6), custom_call_target="tpu_custom_call" | custom-call | tf_op jit(solution)/shard_map/add_packed/pallas_call | solution.py:189
  23.0 2.5 %collective-permute-start.6 = (f32[112,128]{1,0:T(8,128)}, f32[112,128]{1,0:T(8,128)S(1)}, u32[]{:S(2)}, u32[]{:S(2)}) collective-permute-start(f32[112,128]{1,0:T(8,128)} %add_packed.5.refs_0_), channel_id=1, source_target_pairs={{0,72},{1,73},{2,74},{3,75},{4,76},{5,77},{6,78},{7,79},{8,64},{9,... | collective-permute-start | bytes 172040 | tf_op jit(solution)/shard_map/ppermute | solution.py:200
  26.3 1.2 %collective-permute-done.6.refs_3_ = f32[112,128]{1,0:T(8,128)S(1)} collective-permute-done((f32[112,128]{1,0:T(8,128)}, f32[112,128]{1,0:T(8,128)S(1)}, u32[]{:S(2)}, u32[]{:S(2)}) %collective-permute-start.6) | collective-permute-done | bytes 57376 | tf_op jit(solution)/shard_map/ppermute | solution.py:200
  27.5 2.9 %collective-permute-done.5.refs_2_ = f32[112,128]{1,0:T(8,128)S(1)} collective-permute-done((f32[112,128]{1,0:T(8,128)}, f32[112,128]{1,0:T(8,128)S(1)}, u32[]{:S(2)}, u32[]{:S(2)}) %collective-permute-start.5) | collective-permute-done | bytes 57376 | tf_op jit(solution)/shard_map/ppermute | solution.py:200
  31.6 1.6 %add_packed.6.refs_0_ = f32[112,128]{1,0:T(8,128)} custom-call(f32[112,128]{1,0:T(8,128)} %add_packed.5.refs_0_, f32[112,128]{1,0:T(8,128)} %copy-done.13, f32[112,128]{1,0:T(8,128)} %copy-done.10, f32[112,128]{1,0:T(8,128)} %copy-done.7), custom_call_target="tpu_custom_call" | custom-call | tf_op jit(solution)/shard_map/add_packed/pallas_call | solution.py:189
  33.2 3.8 %collective-permute-start.9 = (f32[112,128]{1,0:T(8,128)}, f32[112,128]{1,0:T(8,128)S(1)}, u32[]{:S(2)}, u32[]{:S(2)}) collective-permute-start(f32[112,128]{1,0:T(8,128)} %add_packed.6.refs_0_), channel_id=1, source_target_pairs={{0,48},{1,49},{2,50},{3,51},{4,52},{5,53},{6,54},{7,55},{8,56},{9,... | collective-permute-start | bytes 172040 | tf_op jit(solution)/shard_map/ppermute | solution.py:200
  37.5 1.5 %collective-permute-done.9.refs_3_ = f32[112,128]{1,0:T(8,128)S(1)} collective-permute-done((f32[112,128]{1,0:T(8,128)}, f32[112,128]{1,0:T(8,128)S(1)}, u32[]{:S(2)}, u32[]{:S(2)}) %collective-permute-start.9) | collective-permute-done | bytes 57376 | tf_op jit(solution)/shard_map/ppermute | solution.py:200
  39.0 2.7 %collective-permute-done.8.refs_2_ = f32[112,128]{1,0:T(8,128)S(1)} collective-permute-done((f32[112,128]{1,0:T(8,128)}, f32[112,128]{1,0:T(8,128)S(1)}, u32[]{:S(2)}, u32[]{:S(2)}) %collective-permute-start.8) | collective-permute-done | bytes 57376 | tf_op jit(solution)/shard_map/ppermute | solution.py:200
  43.0 1.5 %add_packed.7.refs_1_ = f32[112,128]{1,0:T(8,128)} custom-call(f32[112,128]{1,0:T(8,128)} %add_packed.6.refs_0_, f32[112,128]{1,0:T(8,128)} %copy-done.14, f32[112,128]{1,0:T(8,128)} %copy-done.11, f32[112,128]{1,0:T(8,128)} %copy-done.8), custom_call_target="tpu_custom_call" | custom-call | tf_op jit(solution)/shard_map/add_packed/pallas_call | solution.py:189
  44.5 4.7 %collective-permute-start.10 = (f32[112,128]{1,0:T(8,128)}, f32[112,128]{1,0:T(8,128)S(1)}, u32[]{:S(2)}, u32[]{:S(2)}) collective-permute-start(f32[112,128]{1,0:T(8,128)} %add_packed.7.refs_1_), channel_id=1, source_target_pairs={{0,4},{1,5},{2,6},{3,7},{4,0},{5,1},{6,2},{7,3},{8,12},{9,13},{10,... | collective-permute-start | bytes 172040 | tf_op jit(solution)/shard_map/ppermute | solution.py:200
  49.1 1.1 %collective-permute-done.10.refs_2_ = f32[112,128]{1,0:T(8,128)S(1)} collective-permute-done((f32[112,128]{1,0:T(8,128)}, f32[112,128]{1,0:T(8,128)S(1)}, u32[]{:S(2)}, u32[]{:S(2)}) %collective-permute-start.10) | collective-permute-done | bytes 57376 | tf_op jit(solution)/shard_map/ppermute | solution.py:200
  50.2 0.8 %copy-done.4 = f32[112,128]{1,0:T(8,128)S(1)} copy-done((f32[112,128]{1,0:T(8,128)S(1)}, f32[112,128]{1,0:T(8,128)}, u32[]{:S(2)}) %copy-start.4) | copy-done | bytes 57368
  51.1 6.7 %factor.1 = (f32[192,128]{1,0:T(8,128)S(1)}, f32[128,128]{1,0:T(8,128)}, f32[128,64]{1,0:T(8,128)S(1)}) custom-call(s32[1]{0:T(128)} %bitcast.core_ref.refs_0_, f32[112,128]{1,0:T(8,128)S(1)} %copy-done.4, f32[112,128]{1,0:T(8,128)S(1)} %collective-permute-done.10.refs_2_), custom_call_target="tpu_custom_call" | custom-call | tf_op jit(solution)/shard_map/factor/pallas_call | solution.py:333
  57.8 2.2 %convolution_subtract_fusion = f32[64,4096]{1,0:T(8,128)} fusion(f32[64,4096]{1,0:T(8,128)S(1)} %copy-done.3, f32[128,4096]{1,0:T(8,128)S(1)} %copy-done.1, f32[192,128]{1,0:T(8,128)S(1)} %get-tuple-element.11), kind=kOutput, calls=%fused_computation | convolution fusion | flops 402915328 | bytes 4227072 | tf_op jit(solution)/shard_map/dot_general | solution.py:58
  60.0 3.2 %fusion = f32[128,4096]{1,0:T(8,128)} fusion(f32[128,4096]{1,0:T(8,128)S(1)} %copy-done.1, f32[192,128]{1,0:T(8,128)S(1)} %get-tuple-element.11), kind=kOutput, calls=%fused_computation.1 | convolution fusion | flops 805306368 | bytes 4259840 | tf_op jit(solution)/shard_map/dot_general | solution.py:58
  (39 shorter events, 7.6 us)
Async XLA Ops:
  0.6 1.6 %copy-start = (f32[128,4096]{1,0:T(8,128)S(1)}, f32[128,4096]{1,0:T(8,128)}, u32[]{:S(2)}) copy-start(f32[128,4096]{1,0:T(8,128)} %panel_ref.1) | copy-start | bytes 6291460
  2.2 1.2 %copy-start.2 = (f32[64,4096]{1,0:T(8,128)S(1)}, f32[64,4096]{1,0:T(8,128)}, u32[]{:S(2)}) copy-start(f32[64,4096]{1,0:T(8,128)} %trail_ref.1) | copy-start | bytes 3145732
  3.5 54.3 %copy-start.1 = (f32[128,4096]{1,0:T(8,128)S(1)}, f32[128,4096]{1,0:T(8,128)}, u32[]{:S(2)}) copy-start(f32[128,4096]{1,0:T(8,128)} %panel_ref.1) | copy-start | bytes 6291460
  3.5 54.3 %copy-start.3 = (f32[64,4096]{1,0:T(8,128)S(1)}, f32[64,4096]{1,0:T(8,128)}, u32[]{:S(2)}) copy-start(f32[64,4096]{1,0:T(8,128)} %trail_ref.1) | copy-start | bytes 3145732
  7.7 0.6 copy-start.5
  8.3 2.3 %collective-permute-start = (f32[112,128]{1,0:T(8,128)S(1)}, f32[112,128]{1,0:T(8,128)S(1)}, u32[]{:S(2)}, u32[]{:S(2)}) collective-permute-start(f32[112,128]{1,0:T(8,128)S(1)} %get-tuple-element.10), channel_id=1, source_target_pairs={{0,4},{1,5},{2,6},{3,7},{4,0},{5,1},{6,2},{7,3},{8,12},{9,13},{10,... | collective-permute-start | bytes 172040 | tf_op jit(solution)/shard_map/ppermute | solution.py:200
  10.6 0.6 copy-start.15
  12.7 5.0 %collective-permute-start.3 = (f32[112,128]{1,0:T(8,128)}, f32[112,128]{1,0:T(8,128)S(1)}, u32[]{:S(2)}, u32[]{:S(2)}) collective-permute-start(f32[112,128]{1,0:T(8,128)} %add_packed.4.refs_0_), channel_id=1, source_target_pairs={{0,3},{1,2},{2,1},{3,0},{4,7},{5,6},{6,5},{7,4},{8,11},{9,10},{10,... | collective-permute-start | bytes 172040 | tf_op jit(solution)/shard_map/ppermute | solution.py:200
  15.5 4.7 %collective-permute-start.2 = (f32[112,128]{1,0:T(8,128)}, f32[112,128]{1,0:T(8,128)S(1)}, u32[]{:S(2)}, u32[]{:S(2)}) collective-permute-start(f32[112,128]{1,0:T(8,128)} %add_packed.4.refs_0_), channel_id=1, source_target_pairs={{0,2},{1,3},{2,0},{3,1},{4,6},{5,7},{6,4},{7,5},{8,10},{9,11},{10,... | collective-permute-start | bytes 172040 | tf_op jit(solution)/shard_map/ppermute | solution.py:200
  15.9 4.4 %collective-permute-start.1 = (f32[112,128]{1,0:T(8,128)}, f32[112,128]{1,0:T(8,128)S(1)}, u32[]{:S(2)}, u32[]{:S(2)}) collective-permute-start(f32[112,128]{1,0:T(8,128)} %add_packed.4.refs_0_), channel_id=1, source_target_pairs={{0,1},{1,0},{2,3},{3,2},{4,5},{5,4},{6,7},{7,6},{8,9},{9,8},{10,11... | collective-permute-start | bytes 172040 | tf_op jit(solution)/shard_map/ppermute | solution.py:200
  17.7 2.6 %copy-start.6 = (f32[112,128]{1,0:T(8,128)}, f32[112,128]{1,0:T(8,128)S(1)}, u32[]{:S(2)}) copy-start(f32[112,128]{1,0:T(8,128)S(1)} %collective-permute-done.3.refs_3_) | copy-start | bytes 172036
  20.3 0.6 copy-start.9
  23.0 4.4 %collective-permute-start.6 = (f32[112,128]{1,0:T(8,128)}, f32[112,128]{1,0:T(8,128)S(1)}, u32[]{:S(2)}, u32[]{:S(2)}) collective-permute-start(f32[112,128]{1,0:T(8,128)} %add_packed.5.refs_0_), channel_id=1, source_target_pairs={{0,72},{1,73},{2,74},{3,75},{4,76},{5,77},{6,78},{7,79},{8,64},{9,... | collective-permute-start | bytes 172040 | tf_op jit(solution)/shard_map/ppermute | solution.py:200
  25.5 4.8 %collective-permute-start.5 = (f32[112,128]{1,0:T(8,128)}, f32[112,128]{1,0:T(8,128)S(1)}, u32[]{:S(2)}, u32[]{:S(2)}) collective-permute-start(f32[112,128]{1,0:T(8,128)} %add_packed.5.refs_0_), channel_id=1, source_target_pairs={{0,64},{1,65},{2,66},{3,67},{4,68},{5,69},{6,70},{7,71},{8,72},{9,... | collective-permute-start | bytes 172040 | tf_op jit(solution)/shard_map/ppermute | solution.py:200
  26.0 4.3 %collective-permute-start.4 = (f32[112,128]{1,0:T(8,128)}, f32[112,128]{1,0:T(8,128)S(1)}, u32[]{:S(2)}, u32[]{:S(2)}) collective-permute-start(f32[112,128]{1,0:T(8,128)} %add_packed.5.refs_0_), channel_id=1, source_target_pairs={{0,8},{1,9},{2,10},{3,11},{4,12},{5,13},{6,14},{7,15},{8,0},{9,1},... | collective-permute-start | bytes 172040 | tf_op jit(solution)/shard_map/ppermute | solution.py:200
  27.5 2.9 %copy-start.7 = (f32[112,128]{1,0:T(8,128)}, f32[112,128]{1,0:T(8,128)S(1)}, u32[]{:S(2)}) copy-start(f32[112,128]{1,0:T(8,128)S(1)} %collective-permute-done.6.refs_3_) | copy-start | bytes 172036
  30.4 0.6 copy-start.10
  33.2 5.9 %collective-permute-start.9 = (f32[112,128]{1,0:T(8,128)}, f32[112,128]{1,0:T(8,128)S(1)}, u32[]{:S(2)}, u32[]{:S(2)}) collective-permute-start(f32[112,128]{1,0:T(8,128)} %add_packed.6.refs_0_), channel_id=1, source_target_pairs={{0,48},{1,49},{2,50},{3,51},{4,52},{5,53},{6,54},{7,55},{8,56},{9,... | collective-permute-start | bytes 172040 | tf_op jit(solution)/shard_map/ppermute | solution.py:200
  36.9 4.8 %collective-permute-start.8 = (f32[112,128]{1,0:T(8,128)}, f32[112,128]{1,0:T(8,128)S(1)}, u32[]{:S(2)}, u32[]{:S(2)}) collective-permute-start(f32[112,128]{1,0:T(8,128)} %add_packed.6.refs_0_), channel_id=1, source_target_pairs={{0,32},{1,33},{2,34},{3,35},{4,36},{5,37},{6,38},{7,39},{8,40},{9,... | collective-permute-start | bytes 172040 | tf_op jit(solution)/shard_map/ppermute | solution.py:200
  37.0 4.8 %collective-permute-start.7 = (f32[112,128]{1,0:T(8,128)}, f32[112,128]{1,0:T(8,128)S(1)}, u32[]{:S(2)}, u32[]{:S(2)}) collective-permute-start(f32[112,128]{1,0:T(8,128)} %add_packed.6.refs_0_), channel_id=1, source_target_pairs={{0,16},{1,17},{2,18},{3,19},{4,20},{5,21},{6,22},{7,23},{8,24},{9,... | collective-permute-start | bytes 172040 | tf_op jit(solution)/shard_map/ppermute | solution.py:200
  39.0 2.7 %copy-start.8 = (f32[112,128]{1,0:T(8,128)}, f32[112,128]{1,0:T(8,128)S(1)}, u32[]{:S(2)}) copy-start(f32[112,128]{1,0:T(8,128)S(1)} %collective-permute-done.9.refs_3_) | copy-start | bytes 172036
  41.7 0.6 copy-start.11
  44.5 5.8 %collective-permute-start.10 = (f32[112,128]{1,0:T(8,128)}, f32[112,128]{1,0:T(8,128)S(1)}, u32[]{:S(2)}, u32[]{:S(2)}) collective-permute-start(f32[112,128]{1,0:T(8,128)} %add_packed.7.refs_1_), channel_id=1, source_target_pairs={{0,4},{1,5},{2,6},{3,7},{4,0},{5,1},{6,2},{7,3},{8,12},{9,13},{10,... | collective-permute-start | bytes 172040 | tf_op jit(solution)/shard_map/ppermute | solution.py:200
  50.2 0.8 %copy-start.4 = (f32[112,128]{1,0:T(8,128)S(1)}, f32[112,128]{1,0:T(8,128)}, u32[]{:S(2)}) copy-start(f32[112,128]{1,0:T(8,128)} %add_packed.7.refs_1_) | copy-start | bytes 172036
  (3 other events, 1.9 us)
where the time goes:
time: 64.3 us; the launch traced here: 63.9 us
  starting transfers between devices  17.1 us (27%)
  Pallas kernels  17 us (26%)
  waiting for transfers between devices  14.4 us (22%)
  local copies, waits for them, and re-layouts  9.29 us (14%)
  matrix products  5.4 us (8%)
  between operations  0.7 us (1%)
    ppermute x11, starting transfers between devices, exchange(): return lax.ppermute(value, AXES, [(s, s ^ mask) for s in range(size)])  17.1 us
    ppermute x11, waiting for transfers between devices, exchange(): return lax.ppermute(value, AXES, [(s, s ^ mask) for s in range(size)])  14.4 us
    unnamed x33, local copies, waits for them, and re-layouts  9.29 us
    pallas_call x1, Pallas kernels, factor(): pl.pallas_call(lambda *refs: factor_kernel(rows_all, *refs), in_specs=[pl...  6.71 us
    pallas_call x4, Pallas kernels, add_packed(): pl.pallas_call(lambda *refs: add_kernel(words, *refs), in_specs=[spec] *...  6.11 us
    dot_general x2, matrix products, nn(): lax.dot_general(a, b, (((1,), (0,)), ((), ())), preferred_element_type=F3...  5.4 us
    pallas_call x1, Pallas kernels, local_gram(): pl.pallas_call(gram_kernel, grid=(rows // CHUNK,), in_specs=[pl.BlockSpec...  4.19 us
  transfers between devices with their start and end apart: 11, of which 8 were waited for; matrix products, arithmetic and copies ran while one was open for 0% of the time, Pallas kernels for 0%

commit v1 on v0

--- a/solution.py
+++ b/solution.py
@@ -10,6 +10,7 @@
 F32 = jnp.float32
 BF16 = jnp.bfloat16
 CHUNK = 1024
+OUT_CHUNK = 512
 PANEL_COLS = 8
 SMALL = 4e-3
 MAGIC = 1.5 * 2.0**23
@@ -167,32 +168,17 @@
     )(core, panel, trailing)
 
 
-def add_pair(a, b, words):
-    hi, err = two_sum(a[:words, :], b[:words, :])
-    return hi, (a[words : 2 * words, :] + b[words : 2 * words, :]) + err, a[2 * words :, :] + b[2 * words :, :]
-
-
-def add_kernel(words, *refs):
-    *ins, out = refs
-    parts = [add_pair(ins[k][...], ins[k + 1][...], words) for k in range(0, len(ins), 2)]
-    total = parts[0]
-    if len(parts) == 2:
-        hi, err = two_sum(parts[0][0], parts[1][0])
-        total = (hi, (parts[0][1] + parts[1][1]) + err, parts[0][2] + parts[1][2])
-    out[:words, :] = total[0]
-    out[words : 2 * words, :] = total[1]
-    out[2 * words :, :] = total[2]
-
-
 def add_packed(words, *arrays):
-    spec = pl.BlockSpec(memory_space=pltpu.VMEM)
-    return pl.pallas_call(
-        lambda *refs: add_kernel(words, *refs),
-        in_specs=[spec] * len(arrays),
-        out_specs=spec,
-        out_shape=jax.ShapeDtypeStruct(arrays[0].shape, F32),
-        name="add_packed",
-    )(*arrays)
+    parts, errors = list(arrays), []
+    while len(parts) > 1:
+        pairs = []
+        for a, b in zip(parts[::2], parts[1::2]):
+            errors.append(two_sum(a[:words], b[:words])[1])
+            pairs.append(a + b)
+        parts = pairs
+    error = errors[0] if len(errors) == 1 else (errors[0] + errors[1]) + errors[2]
+    rest = parts[0].shape[0] - 2 * words
+    return parts[0] + jnp.pad(error, ((words, rest), (0, 0)))
 
 
 def exchange(value, mask):
@@ -233,7 +219,7 @@
 
 def factor_kernel(rows_all, core_ref, own_ref, other_ref, wz_ref, upper_ref, coup_ref, wcat, gcat, tcat, v_ref):
     n = upper_ref.shape[0]
-    t = coup_ref.shape[1]
+    t = coup_ref.shape[0]
     half, q, tq = n // 2, n // 4, t // 2
     first = core_ref[0] == 0
     own, other = own_ref[...], other_ref[...]
@@ -318,14 +304,16 @@
             v_ref[8 * r : 8 * r + 8, :] = blocks[r]
 
     v = v_ref[...]
-    w_new = nn(v, wt, precision=HIGHEST) * ic
+    y = nt(wt, ca * inv_pc, precision=HIGHEST)
     t_true = t_hi * (qs * (1.0 / 32.0)) * jnp.broadcast_to(pc, (n, n))
+    wide = nn(v, jnp.concatenate([wt, t_true, y], axis=1), precision=HIGHEST)
+    w_new = wide[:, :n] * ic
     root = jnp.sqrt(jnp.float32(rows_all))
-    upper_ref[...] = jnp.where(i <= j, nn(v, t_true, precision=HIGHEST) / root, 0.0)
-    coupling = nt(w_new, ca, precision=HIGHEST)
-    coup_ref[...] = coupling
-    wz_ref[:n, :] = w_new * root
-    wz_ref[n:, :] = lax.dot_general(coupling, w_new, (((0,), (0,)), ((), ())), preferred_element_type=F32, precision=HIGHEST)
+    upper_ref[...] = jnp.where(i <= j, wide[:, n : 2 * n] / root, 0.0)
+    coupling_t = wide[:, 2 * n :].T
+    coup_ref[...] = coupling_t
+    wz_ref[:n, :] = w_new
+    wz_ref[n:, :] = nn(coupling_t, w_new, precision=HIGHEST)
 
 
 def factor(core, own, other, n, t, rows_all):
@@ -337,7 +325,7 @@
         out_shape=[
             jax.ShapeDtypeStruct((n + t, n), F32),
             jax.ShapeDtypeStruct((n, n), F32),
-            jax.ShapeDtypeStruct((n, t), F32),
+            jax.ShapeDtypeStruct((t, n), F32),
         ],
         scratch_shapes=[
             pltpu.VMEM((n, 3 * n), BF16),
@@ -350,21 +338,45 @@
     )(core, own, other)
 
 
+def apply_kernel(rows_all, wz_ref, panel_ref, trail_ref, basis_ref, updated_ref):
+    n = panel_ref.shape[0]
+    width = basis_ref.shape[1]
+    at = pl.multiple_of(pl.program_id(0) * width, width)
+    out = nn(wz_ref[...], panel_ref[:, pl.ds(at, width)], precision=HIGHEST)
+    basis_ref[...] = out[:n, :] * jnp.sqrt(jnp.float32(rows_all))
+    updated_ref[...] = trail_ref[:, pl.ds(at, width)] - out[n:, :]
+
+
+def apply_factors(wz, panel, trailing, rows_all):
+    n, rows = panel.shape
+    t = trailing.shape[0]
+    spec = pl.BlockSpec(memory_space=pltpu.VMEM)
+    return pl.pallas_call(
+        lambda *refs: apply_kernel(rows_all, *refs),
+        grid=(rows // OUT_CHUNK,),
+        in_specs=[spec, spec, spec],
+        out_specs=[pl.BlockSpec((n, OUT_CHUNK), lambda i: (0, i)), pl.BlockSpec((t, OUT_CHUNK), lambda i: (0, i))],
+        out_shape=[jax.ShapeDtypeStruct((n, rows), F32), jax.ShapeDtypeStruct((t, rows), F32)],
+        compiler_params=pltpu.CompilerParams(vmem_limit_bytes=32 << 20),
+        name="apply",
+    )(wz, panel, trailing)
+
+
 def shards(panel, trailing):
     n, t = panel.shape[0], trailing.shape[0]
     rows_all = panel.shape[1] * lax.axis_size(AXES)
     core = jnp.reshape(lax.axis_index("gy") % 2, (1,)).astype(jnp.int32)
     words = n // 4 + 8
-    keep, send = local_gram(core, panel, trailing)
+    streamed = (pltpu.with_memory_space_constraint(a, pltpu.HBM) for a in (panel, trailing))
+    keep, send = local_gram(core, *streamed)
     total = add_packed(words, keep, exchange(send, 4))
     for masks in ((1, 3, 2), (8, 72, 64), (16, 48, 32)):
         near, wrap, far = (exchange(total, m) for m in masks)
         total = add_packed(words, total, near, far, wrap)
     other = exchange(total, 4)
-    wz, upper, coupling = factor(core, total, other, n, t, rows_all)
-    basis_t = nn(wz[:n], panel, precision=HIGHEST)
-    updated = trailing - nn(wz[n:], panel, precision=HIGHEST)
-    return basis_t, upper, coupling, updated
+    wz, upper, coupling_t = factor(core, total, other, n, t, rows_all)
+    basis_t, updated = apply_factors(wz, panel, trailing, rows_all)
+    return basis_t, upper, coupling_t.T, updated
 
 
 def solution(mesh):

time: 64.3 us -> 51.2 us (0.80)
  local copies, waits for them, and re-layouts: 9.29 us -> 0.01 us
  matrix products: 5.4 us -> 0 us
  starting transfers between devices: 17.1 us -> 19.5 us
  waiting for transfers between devices: 14.4 us -> 13.4 us
    unnamed x33 -> x4, local copies, waits for them, and re-layouts: 9.29 us -> 0.01 us
    dot_general x2 -> x0, matrix products: 5.4 us -> none  [nn(): lax.dot_general(a, b, (((1,), (0,)), ((), ())), preferred_element_type=F3...]
    ppermute x11, starting transfers between devices: 17.1 us -> 19.5 us  [exchange(): return lax.ppermute(value, AXES, [(s, s ^ mask) for s in range(size)])]
    pallas_call x1, Pallas kernels: 4.19 us -> 5.41 us  [local_gram(): pl.pallas_call(gram_kernel, grid=(rows // CHUNK,), in_specs=[pl.BlockSpec...]
    ppermute x11, waiting for transfers between devices: 14.4 us -> 13.4 us  [exchange(): return lax.ppermute(value, AXES, [(s, s ^ mask) for s in range(size)])]
    pallas_call x4 -> x1, Pallas kernels: 6.11 us -> 5.31 us  [apply_factors(): pl.pallas_call(lambda *refs: apply_kernel(rows_all, *refs), grid=(rows //...]
where the time goes in v1:
time: 51.2 us; the launch traced here: 51 us
  starting transfers between devices  19.5 us (38%)
  Pallas kernels  17.3 us (34%)
  waiting for transfers between devices  13.4 us (26%)
  between operations  0.74 us (1%)
    ppermute x11, starting transfers between devices, exchange(): return lax.ppermute(value, AXES, [(s, s ^ mask) for s in range(size)])  19.5 us
    ppermute x11, waiting for transfers between devices, exchange(): return lax.ppermute(value, AXES, [(s, s ^ mask) for s in range(size)])  13.4 us
    pallas_call x1, Pallas kernels, factor(): pl.pallas_call(lambda *refs: factor_kernel(rows_all, *refs), in_specs=[pl...  6.57 us
    pallas_call x1, Pallas kernels, local_gram(): pl.pallas_call(gram_kernel, grid=(rows // CHUNK,), in_specs=[pl.BlockSpec...  5.41 us
    pallas_call x1, Pallas kernels, apply_factors(): pl.pallas_call(lambda *refs: apply_kernel(rows_all, *refs), grid=(rows //...  5.31 us
  transfers between devices with their start and end apart: 11, of which 8 were waited for; matrix products, arithmetic and copies ran while one was open for 0% of the time, Pallas kernels for 0%

profile of v1, /device:TPU:1, one launch (start us, length us, event | category | flops | bytes accessed | tf_op | source)
XLA Modules:
  0.0 51.0 jit_solution(3266066381883819813)
XLA Ops:
  0.7 5.4 %gram.1 = (f32[112,128]{1,0:T(8,128)S(1)}, f32[112,128]{1,0:T(8,128)S(1)}) custom-call(s32[1]{0:T(128)} %bitcast.core_ref.refs_0_, f32[128,4096]{1,0:T(8,128)} %refs_1_.1, f32[64,4096]{1,0:T(8,128)} %refs_2_.1), custom_call_target="tpu_custom_call" | custom-call | tf_op jit(solution)/shard_map/gram/pallas_call | solution.py:150
  6.1 1.5 %collective-permute-start = (f32[112,128]{1,0:T(8,128)S(1)}, f32[112,128]{1,0:T(8,128)S(1)}, u32[]{:S(2)}, u32[]{:S(2)}) collective-permute-start(f32[112,128]{1,0:T(8,128)S(1)} %get-tuple-element.12), channel_id=1, source_target_pairs={{0,4},{1,5},{2,6},{3,7},{4,0},{5,1},{6,2},{7,3},{8,12},{9,13},{10,... | collective-permute-start | bytes 172040 | tf_op jit(solution)/shard_map/ppermute | solution.py:186
  7.6 0.9 %collective-permute-done = f32[112,128]{1,0:T(8,128)S(1)} collective-permute-done((f32[112,128]{1,0:T(8,128)S(1)}, f32[112,128]{1,0:T(8,128)S(1)}, u32[]{:S(2)}, u32[]{:S(2)}) %collective-permute-start) | collective-permute-done | bytes 57376 | tf_op jit(solution)/shard_map/ppermute | solution.py:186
  8.5 1.5 %collective-permute-start.1 = (f32[112,128]{1,0:T(8,128)S(1)}, f32[112,128]{1,0:T(8,128)S(1)}, u32[]{:S(2)}, u32[]{:S(2)}) collective-permute-start(f32[112,128]{1,0:T(8,128)S(1)} %pad_add_fusion.3), channel_id=1, source_target_pairs={{0,1},{1,0},{2,3},{3,2},{4,5},{5,4},{6,7},{7,6},{8,9},{9,8},{10,11... | collective-permute-start | bytes 172040 | tf_op jit(solution)/shard_map/ppermute | solution.py:186
  10.0 1.9 %collective-permute-start.3 = (f32[112,128]{1,0:T(8,128)S(1)}, f32[112,128]{1,0:T(8,128)S(1)}, u32[]{:S(2)}, u32[]{:S(2)}) collective-permute-start(f32[112,128]{1,0:T(8,128)S(1)} %pad_add_fusion.3), channel_id=1, source_target_pairs={{0,3},{1,2},{2,1},{3,0},{4,7},{5,6},{6,5},{7,4},{8,11},{9,10},{10,... | collective-permute-start | bytes 172040 | tf_op jit(solution)/shard_map/ppermute | solution.py:186
  11.9 0.7 %collective-permute-start.2 = (f32[112,128]{1,0:T(8,128)S(1)}, f32[112,128]{1,0:T(8,128)S(1)}, u32[]{:S(2)}, u32[]{:S(2)}) collective-permute-start(f32[112,128]{1,0:T(8,128)S(1)} %pad_add_fusion.3), channel_id=1, source_target_pairs={{0,2},{1,3},{2,0},{3,1},{4,6},{5,7},{6,4},{7,5},{8,10},{9,11},{10,... | collective-permute-start | bytes 172040 | tf_op jit(solution)/shard_map/ppermute | solution.py:186
  12.6 0.0 collective-permute-done.1
  12.6 1.6 %collective-permute-done.3 = f32[112,128]{1,0:T(8,128)S(1)} collective-permute-done((f32[112,128]{1,0:T(8,128)S(1)}, f32[112,128]{1,0:T(8,128)S(1)}, u32[]{:S(2)}, u32[]{:S(2)}) %collective-permute-start.3) | collective-permute-done | bytes 57376 | tf_op jit(solution)/shard_map/ppermute | solution.py:186
  14.2 2.2 %collective-permute-done.2 = f32[112,128]{1,0:T(8,128)S(1)} collective-permute-done((f32[112,128]{1,0:T(8,128)S(1)}, f32[112,128]{1,0:T(8,128)S(1)}, u32[]{:S(2)}, u32[]{:S(2)}) %collective-permute-start.2) | collective-permute-done | bytes 57376 | tf_op jit(solution)/shard_map/ppermute | solution.py:186
  16.5 1.3 %collective-permute-start.4 = (f32[112,128]{1,0:T(8,128)S(1)}, f32[112,128]{1,0:T(8,128)S(1)}, u32[]{:S(2)}, u32[]{:S(2)}) collective-permute-start(f32[112,128]{1,0:T(8,128)S(1)} %pad_add_fusion.2), channel_id=1, source_target_pairs={{0,8},{1,9},{2,10},{3,11},{4,12},{5,13},{6,14},{7,15},{8,0},{9,1},... | collective-permute-start | bytes 172040 | tf_op jit(solution)/shard_map/ppermute | solution.py:186
  17.7 1.8 %collective-permute-start.6 = (f32[112,128]{1,0:T(8,128)S(1)}, f32[112,128]{1,0:T(8,128)S(1)}, u32[]{:S(2)}, u32[]{:S(2)}) collective-permute-start(f32[112,128]{1,0:T(8,128)S(1)} %pad_add_fusion.2), channel_id=1, source_target_pairs={{0,72},{1,73},{2,74},{3,75},{4,76},{5,77},{6,78},{7,79},{8,64},{9,... | collective-permute-start | bytes 172040 | tf_op jit(solution)/shard_map/ppermute | solution.py:186
  19.6 0.6 %collective-permute-start.5 = (f32[112,128]{1,0:T(8,128)S(1)}, f32[112,128]{1,0:T(8,128)S(1)}, u32[]{:S(2)}, u32[]{:S(2)}) collective-permute-start(f32[112,128]{1,0:T(8,128)S(1)} %pad_add_fusion.2), channel_id=1, source_target_pairs={{0,64},{1,65},{2,66},{3,67},{4,68},{5,69},{6,70},{7,71},{8,72},{9,... | collective-permute-start | bytes 172040 | tf_op jit(solution)/shard_map/ppermute | solution.py:186
  20.2 0.0 collective-permute-done.4
  20.2 1.8 %collective-permute-done.6 = f32[112,128]{1,0:T(8,128)S(1)} collective-permute-done((f32[112,128]{1,0:T(8,128)S(1)}, f32[112,128]{1,0:T(8,128)S(1)}, u32[]{:S(2)}, u32[]{:S(2)}) %collective-permute-start.6) | collective-permute-done | bytes 57376 | tf_op jit(solution)/shard_map/ppermute | solution.py:186
  22.0 2.5 %collective-permute-done.5 = f32[112,128]{1,0:T(8,128)S(1)} collective-permute-done((f32[112,128]{1,0:T(8,128)S(1)}, f32[112,128]{1,0:T(8,128)S(1)}, u32[]{:S(2)}, u32[]{:S(2)}) %collective-permute-start.5) | collective-permute-done | bytes 57376 | tf_op jit(solution)/shard_map/ppermute | solution.py:186
  24.6 1.7 %collective-permute-start.7 = (f32[112,128]{1,0:T(8,128)S(1)}, f32[112,128]{1,0:T(8,128)S(1)}, u32[]{:S(2)}, u32[]{:S(2)}) collective-permute-start(f32[112,128]{1,0:T(8,128)S(1)} %pad_add_fusion.1), channel_id=1, source_target_pairs={{0,16},{1,17},{2,18},{3,19},{4,20},{5,21},{6,22},{7,23},{8,24},{9,... | collective-permute-start | bytes 172040 | tf_op jit(solution)/shard_map/ppermute | solution.py:186
  26.3 2.2 %collective-permute-start.9 = (f32[112,128]{1,0:T(8,128)S(1)}, f32[112,128]{1,0:T(8,128)S(1)}, u32[]{:S(2)}, u32[]{:S(2)}) collective-permute-start(f32[112,128]{1,0:T(8,128)S(1)} %pad_add_fusion.1), channel_id=1, source_target_pairs={{0,48},{1,49},{2,50},{3,51},{4,52},{5,53},{6,54},{7,55},{8,56},{9,... | collective-permute-start | bytes 172040 | tf_op jit(solution)/shard_map/ppermute | solution.py:186
  28.5 1.1 %collective-permute-start.8 = (f32[112,128]{1,0:T(8,128)S(1)}, f32[112,128]{1,0:T(8,128)S(1)}, u32[]{:S(2)}, u32[]{:S(2)}) collective-permute-start(f32[112,128]{1,0:T(8,128)S(1)} %pad_add_fusion.1), channel_id=1, source_target_pairs={{0,32},{1,33},{2,34},{3,35},{4,36},{5,37},{6,38},{7,39},{8,40},{9,... | collective-permute-start | bytes 172040 | tf_op jit(solution)/shard_map/ppermute | solution.py:186
  29.6 0.9 %collective-permute-done.9 = f32[112,128]{1,0:T(8,128)S(1)} collective-permute-done((f32[112,128]{1,0:T(8,128)S(1)}, f32[112,128]{1,0:T(8,128)S(1)}, u32[]{:S(2)}, u32[]{:S(2)}) %collective-permute-start.9) | collective-permute-done | bytes 57376 | tf_op jit(solution)/shard_map/ppermute | solution.py:186
  30.5 2.5 %collective-permute-done.8 = f32[112,128]{1,0:T(8,128)S(1)} collective-permute-done((f32[112,128]{1,0:T(8,128)S(1)}, f32[112,128]{1,0:T(8,128)S(1)}, u32[]{:S(2)}, u32[]{:S(2)}) %collective-permute-start.8) | collective-permute-done | bytes 57376 | tf_op jit(solution)/shard_map/ppermute | solution.py:186
  33.1 5.1 %collective-permute-start.10 = (f32[112,128]{1,0:T(8,128)S(1)}, f32[112,128]{1,0:T(8,128)S(1)}, u32[]{:S(2)}, u32[]{:S(2)}) collective-permute-start(f32[112,128]{1,0:T(8,128)S(1)} %pad_add_fusion.refs_1_), channel_id=1, source_target_pairs={{0,4},{1,5},{2,6},{3,7},{4,0},{5,1},{6,2},{7,3},{8,12},{9,13},{10,... | collective-permute-start | bytes 172040 | tf_op jit(solution)/shard_map/ppermute | solution.py:186
  38.3 0.9 %collective-permute-done.10.refs_2_ = f32[112,128]{1,0:T(8,128)S(1)} collective-permute-done((f32[112,128]{1,0:T(8,128)S(1)}, f32[112,128]{1,0:T(8,128)S(1)}, u32[]{:S(2)}, u32[]{:S(2)}) %collective-permute-start.10) | collective-permute-done | bytes 57376 | tf_op jit(solution)/shard_map/ppermute | solution.py:186
  39.2 6.6 %factor.1 = (f32[192,128]{1,0:T(8,128)S(1)}, f32[128,128]{1,0:T(8,128)}, f32[64,128]{1,0:T(8,128)}) custom-call(s32[1]{0:T(128)} %bitcast.core_ref.refs_0_, f32[112,128]{1,0:T(8,128)S(1)} %pad_add_fusion.refs_1_, f32[112,128]{1,0:T(8,128)S(1)} %collective-permute-done.10.refs_2_), custom_call_target="tpu_custom_call" | custom-call | tf_op jit(solution)/shard_map/factor/pallas_call | solution.py:321
  45.7 5.3 %apply.1 = (f32[128,4096]{1,0:T(8,128)}, f32[64,4096]{1,0:T(8,128)}) custom-call(f32[192,128]{1,0:T(8,128)S(1)} %get-tuple-element.13.refs_0_, f32[128,4096]{1,0:T(8,128)S(1)} %copy-done, f32[64,4096]{1,0:T(8,128)S(1)} %copy-done.1), custom_call_target="tpu_custom_call" | custom-call | tf_op jit(solution)/shard_map/apply/pallas_call | solution.py:354
  (19 shorter events, 0.2 us)
Async XLA Ops:
  0.6 45.1 %copy-start = (f32[128,4096]{1,0:T(8,128)S(1)}, f32[128,4096]{1,0:T(8,128)}, u32[]{:S(2)}) copy-start(f32[128,4096]{1,0:T(8,128)} %refs_1_.1) | copy-start | bytes 6291460
  0.7 45.1 %copy-start.1 = (f32[64,4096]{1,0:T(8,128)S(1)}, f32[64,4096]{1,0:T(8,128)}, u32[]{:S(2)}) copy-start(f32[64,4096]{1,0:T(8,128)} %refs_2_.1) | copy-start | bytes 3145732
  6.1 2.4 %collective-permute-start = (f32[112,128]{1,0:T(8,128)S(1)}, f32[112,128]{1,0:T(8,128)S(1)}, u32[]{:S(2)}, u32[]{:S(2)}) collective-permute-start(f32[112,128]{1,0:T(8,128)S(1)} %get-tuple-element.12), channel_id=1, source_target_pairs={{0,4},{1,5},{2,6},{3,7},{4,0},{5,1},{6,2},{7,3},{8,12},{9,13},{10,... | collective-permute-start | bytes 172040 | tf_op jit(solution)/shard_map/ppermute | solution.py:186
  8.5 4.1 %collective-permute-start.1 = (f32[112,128]{1,0:T(8,128)S(1)}, f32[112,128]{1,0:T(8,128)S(1)}, u32[]{:S(2)}, u32[]{:S(2)}) collective-permute-start(f32[112,128]{1,0:T(8,128)S(1)} %pad_add_fusion.3), channel_id=1, source_target_pairs={{0,1},{1,0},{2,3},{3,2},{4,5},{5,4},{6,7},{7,6},{8,9},{9,8},{10,11... | collective-permute-start | bytes 172040 | tf_op jit(solution)/shard_map/ppermute | solution.py:186
  10.0 4.2 %collective-permute-start.3 = (f32[112,128]{1,0:T(8,128)S(1)}, f32[112,128]{1,0:T(8,128)S(1)}, u32[]{:S(2)}, u32[]{:S(2)}) collective-permute-start(f32[112,128]{1,0:T(8,128)S(1)} %pad_add_fusion.3), channel_id=1, source_target_pairs={{0,3},{1,2},{2,1},{3,0},{4,7},{5,6},{6,5},{7,4},{8,11},{9,10},{10,... | collective-permute-start | bytes 172040 | tf_op jit(solution)/shard_map/ppermute | solution.py:186
  11.9 4.5 %collective-permute-start.2 = (f32[112,128]{1,0:T(8,128)S(1)}, f32[112,128]{1,0:T(8,128)S(1)}, u32[]{:S(2)}, u32[]{:S(2)}) collective-permute-start(f32[112,128]{1,0:T(8,128)S(1)} %pad_add_fusion.3), channel_id=1, source_target_pairs={{0,2},{1,3},{2,0},{3,1},{4,6},{5,7},{6,4},{7,5},{8,10},{9,11},{10,... | collective-permute-start | bytes 172040 | tf_op jit(solution)/shard_map/ppermute | solution.py:186
  16.5 3.7 %collective-permute-start.4 = (f32[112,128]{1,0:T(8,128)S(1)}, f32[112,128]{1,0:T(8,128)S(1)}, u32[]{:S(2)}, u32[]{:S(2)}) collective-permute-start(f32[112,128]{1,0:T(8,128)S(1)} %pad_add_fusion.2), channel_id=1, source_target_pairs={{0,8},{1,9},{2,10},{3,11},{4,12},{5,13},{6,14},{7,15},{8,0},{9,1},... | collective-permute-start | bytes 172040 | tf_op jit(solution)/shard_map/ppermute | solution.py:186
  17.7 4.2 %collective-permute-start.6 = (f32[112,128]{1,0:T(8,128)S(1)}, f32[112,128]{1,0:T(8,128)S(1)}, u32[]{:S(2)}, u32[]{:S(2)}) collective-permute-start(f32[112,128]{1,0:T(8,128)S(1)} %pad_add_fusion.2), channel_id=1, source_target_pairs={{0,72},{1,73},{2,74},{3,75},{4,76},{5,77},{6,78},{7,79},{8,64},{9,... | collective-permute-start | bytes 172040 | tf_op jit(solution)/shard_map/ppermute | solution.py:186
  19.6 5.0 %collective-permute-start.5 = (f32[112,128]{1,0:T(8,128)S(1)}, f32[112,128]{1,0:T(8,128)S(1)}, u32[]{:S(2)}, u32[]{:S(2)}) collective-permute-start(f32[112,128]{1,0:T(8,128)S(1)} %pad_add_fusion.2), channel_id=1, source_target_pairs={{0,64},{1,65},{2,66},{3,67},{4,68},{5,69},{6,70},{7,71},{8,72},{9,... | collective-permute-start | bytes 172040 | tf_op jit(solution)/shard_map/ppermute | solution.py:186
  24.6 5.0 %collective-permute-start.7 = (f32[112,128]{1,0:T(8,128)S(1)}, f32[112,128]{1,0:T(8,128)S(1)}, u32[]{:S(2)}, u32[]{:S(2)}) collective-permute-start(f32[112,128]{1,0:T(8,128)S(1)} %pad_add_fusion.1), channel_id=1, source_target_pairs={{0,16},{1,17},{2,18},{3,19},{4,20},{5,21},{6,22},{7,23},{8,24},{9,... | collective-permute-start | bytes 172040 | tf_op jit(solution)/shard_map/ppermute | solution.py:186
  26.3 4.2 %collective-permute-start.9 = (f32[112,128]{1,0:T(8,128)S(1)}, f32[112,128]{1,0:T(8,128)S(1)}, u32[]{:S(2)}, u32[]{:S(2)}) collective-permute-start(f32[112,128]{1,0:T(8,128)S(1)} %pad_add_fusion.1), channel_id=1, source_target_pairs={{0,48},{1,49},{2,50},{3,51},{4,52},{5,53},{6,54},{7,55},{8,56},{9,... | collective-permute-start | bytes 172040 | tf_op jit(solution)/shard_map/ppermute | solution.py:186
  28.5 4.5 %collective-permute-start.8 = (f32[112,128]{1,0:T(8,128)S(1)}, f32[112,128]{1,0:T(8,128)S(1)}, u32[]{:S(2)}, u32[]{:S(2)}) collective-permute-start(f32[112,128]{1,0:T(8,128)S(1)} %pad_add_fusion.1), channel_id=1, source_target_pairs={{0,32},{1,33},{2,34},{3,35},{4,36},{5,37},{6,38},{7,39},{8,40},{9,... | collective-permute-start | bytes 172040 | tf_op jit(solution)/shard_map/ppermute | solution.py:186
  33.1 6.0 %collective-permute-start.10 = (f32[112,128]{1,0:T(8,128)S(1)}, f32[112,128]{1,0:T(8,128)S(1)}, u32[]{:S(2)}, u32[]{:S(2)}) collective-permute-start(f32[112,128]{1,0:T(8,128)S(1)} %pad_add_fusion.refs_1_), channel_id=1, source_target_pairs={{0,4},{1,5},{2,6},{3,7},{4,0},{5,1},{6,2},{7,3},{8,12},{9,13},{10,... | collective-permute-start | bytes 172040 | tf_op jit(solution)/shard_map/ppermute | solution.py:186

commit v2 on v1

--- a/solution.py
+++ b/solution.py
@@ -9,7 +9,7 @@
 HIGHEST = lax.Precision.HIGHEST
 F32 = jnp.float32
 BF16 = jnp.bfloat16
-CHUNK = 1024
+CHUNK = 2048
 OUT_CHUNK = 512
 PANEL_COLS = 8
 SMALL = 4e-3
@@ -63,105 +63,126 @@
     return lax.broadcasted_iota(jnp.int32, shape, axis)
 
 
-def gram_kernel(core_ref, panel_ref, trail_ref, keep_ref, send_ref, ops, hi_ref, lo_ref, ca_ref):
-    step = pl.program_id(0)
-    n, t = panel_ref.shape[0], trail_ref.shape[0]
-
-    @pl.when(step == 0)
-    def _():
-        hi_ref[...] = jnp.zeros_like(hi_ref)
-        lo_ref[...] = jnp.zeros_like(lo_ref)
-        ca_ref[...] = jnp.zeros_like(ca_ref)
-
-    x = panel_ref[...]
-    p, inv = power_below(jnp.max(jnp.abs(x), axis=1, keepdims=True))
-    a = x * (inv * 64.0)
-    d1 = round_int(a)
-    r1 = (a - d1) * 256.0
-    d2 = round_int(r1)
-    ops[0:n, :] = d1.astype(BF16)
-    ops[n : 2 * n, :] = d2.astype(BF16)
-    ops[2 * n : 3 * n, :] = ((r1 - d2) * 256.0).astype(BF16)
-    c = trail_ref[...]
-    c1 = c.astype(BF16)
-    rc = c - c1.astype(F32)
-    c2 = rc.astype(BF16)
-    ops[3 * n : 3 * n + t, :] = c1
-    ops[3 * n + t : 3 * n + 2 * t, :] = c2
-    ops[3 * n + 2 * t : 3 * n + 3 * t, :] = (rc - c2.astype(F32)).astype(BF16)
-
-    m = nt(ops[...], ops[0 : 3 * n, :])
-
-    def blk(i, j):
-        return m[i * n : (i + 1) * n, j * n : (j + 1) * n]
-
-    def cblk(i, j):
-        return m[3 * n + i * t : 3 * n + (i + 1) * t, j * n : (j + 1) * n]
-
-    row = jnp.broadcast_to(p * (1.0 / 64.0), (n, n))
-    col = row.T
-    scale = row * col
-    h, e = two_sum(blk(0, 0), (blk(0, 1) + blk(1, 0)) * 2.0**-8)
-    rest = (blk(0, 2) + blk(2, 0) + blk(1, 1)) * 2.0**-16
-    rest = rest + ((blk(1, 2) + blk(2, 1)) * 2.0**-24 + blk(2, 2) * 2.0**-32)
-    hi, err = two_sum(hi_ref[...], h * scale)
-    hi_ref[...] = hi
-    lo_ref[...] += err + (e + rest) * scale
-    ca = (cblk(2, 0) + cblk(1, 1) * 2.0**-8 + cblk(0, 2) * 2.0**-16) + (cblk(1, 0) + cblk(0, 1) * 2.0**-8)
-    ca_ref[...] += (ca + cblk(0, 0)) * col[0:t, :]
-
-    @pl.when(step == pl.num_programs(0) - 1)
-    def _():
-        core = core_ref[0]
-        half = n // 2
-        i, j = iota((half, n), 0), iota((half, n), 1)
-
-        def fold(g):
-            top, bottom = g[:half, :], g[half:, :]
-            body = jnp.where((j >= half) & (i >= j - half), pltpu.roll(top, half, 1), bottom)
-            diag = jnp.sum(jnp.where(i == j - half, bottom, 0.0), axis=0, keepdims=True)
-            return body, jnp.broadcast_to(diag, (8, n))
-
-        hi_body, hi_diag = fold(hi_ref[...])
-        lo_body, lo_diag = fold(lo_ref[...])
-        ca = ca_ref[...]
-        q = half // 2
-        tq = t // 2
-
-        def put(ref, first):
-            def pick(v, size):
-                return jnp.where(first, v[:size, :], v[size:, :])
-
-            ref[0:q, :] = pick(hi_body, q)
-            ref[q : q + 8, :] = hi_diag
-            ref[q + 8 : 2 * q + 8, :] = pick(lo_body, q)
-            ref[2 * q + 8 : 2 * q + 16, :] = lo_diag
-            ref[2 * q + 16 :, :] = pick(ca, tq)
-
-        put(keep_ref, core == 0)
-        put(send_ref, core == 1)
+def gram_kernel(core_ref, panel, trail, keep_ref, send_ref, pbuf, tbuf, ops, hi_ref, lo_ref, mix_ref, ca_ref, ac_ref, sems):
+    n, rows = panel.shape
+    t = trail.shape[0]
+    steps = rows // CHUNK
+    copies = []
+    for k in range(steps):
+        at = pl.ds(k * CHUNK, CHUNK)
+        pair = (
+            pltpu.make_async_copy(panel.at[:, at], pbuf.at[k], sems.at[0, k]),
+            pltpu.make_async_copy(trail.at[:, at], tbuf.at[k], sems.at[1, k]),
+        )
+        for copy in pair:
+            copy.start()
+        copies.append(pair)
+
+    def split(k):
+        copies[k][0].wait()
+        x = pbuf[k]
+        p, inv = power_below(jnp.max(jnp.abs(x), axis=1, keepdims=True))
+        a = x * (inv * 32.0)
+        d1 = round_int(a)
+        r1 = (a - d1) * 256.0
+        d2 = round_int(r1)
+        d3 = (r1 - d2) * 256.0
+        copies[k][1].wait()
+        c = tbuf[k]
+        c1 = c.astype(BF16)
+        rc = c - c1.astype(F32)
+        c2 = rc.astype(BF16)
+        c3 = rc - c2.astype(F32)
+        at = 0
+        for part in (c3, d1, d2, d3, c1, c2):
+            ops[k, at : at + part.shape[0], :] = part.astype(BF16)
+            at += part.shape[0]
+        return p
+
+    def product(k, p):
+        left = nt(ops[k, 0 : t + 2 * n, :], ops[k, t : t + 2 * n, :])
+        right = nt(ops[k, t : t + 3 * n, :], ops[k, t + 2 * n :, :])
+        c3d1, left = left[:t, :n], left[t:, :]
+        row = jnp.broadcast_to(p * (1.0 / 32.0), (n, n))
+        col = row.T
+        scale = row * col
+        h, e = two_sum(left[:n, :n], (left[:n, n:] + left[n:, :n]) * 2.0**-8)
+        e = e + (left[n:, n:] * 2.0**-16 + right[2 * n :, :n] * 2.0**-32)
+        mix = (right[:n, :n] * 2.0**-16 + right[n : 2 * n, :n] * 2.0**-24) * scale
+        ac = right[2 * n :, n : n + t] * 2.0**-16 + right[n : 2 * n, n + t :] * 2.0**-8
+        ac = ac + (right[n : 2 * n, n : n + t] * 2.0**-8 + right[:n, n + t :])
+        ac = (ac + right[:n, n : n + t]) * row[:, :t]
+        ca = c3d1 * col[:t, :]
+        if k == 0:
+            hi_ref[...], lo_ref[...] = h * scale, e * scale
+            mix_ref[...], ca_ref[...], ac_ref[...] = mix, ca, ac
+        else:
+            hi, err = two_sum(hi_ref[...], h * scale)
+            hi_ref[...] = hi
+            lo_ref[...] += err + e * scale
+            mix_ref[...] += mix
+            ca_ref[...] += ca
+            ac_ref[...] += ac
+
+    p = split(0)
+    for k in range(steps):
+        following = split(k + 1) if k + 1 < steps else None
+        product(k, p)
+        p = following
+
+    core = core_ref[0]
+    half = n // 2
+    i, j = iota((half, n), 0), iota((half, n), 1)
+
+    def fold(g):
+        top, bottom = g[:half, :], g[half:, :]
+        body = jnp.where((j >= half) & (i >= j - half), pltpu.roll(top, half, 1), bottom)
+        diag = jnp.sum(jnp.where(i == j - half, bottom, 0.0), axis=0, keepdims=True)
+        return body, jnp.broadcast_to(diag, (8, n))
+
+    mix = mix_ref[...]
+    hi, lo = two_sum(hi_ref[...], lo_ref[...] + (mix + mix.T))
+    hi_body, hi_diag = fold(hi)
+    lo_body, lo_diag = fold(lo)
+    ca = ca_ref[...] + ac_ref[...].T
+    q = half // 2
+    tq = t // 2
+
+    def put(ref, first):
+        def pick(v, size):
+            return jnp.where(first, v[:size, :], v[size:, :])
+
+        ref[0:q, :] = pick(hi_body, q)
+        ref[q : q + 8, :] = hi_diag
+        ref[q + 8 : 2 * q + 8, :] = pick(lo_body, q)
+        ref[2 * q + 8 : 2 * q + 16, :] = lo_diag
+        ref[2 * q + 16 :, :] = pick(ca, tq)
+
+    put(keep_ref, core == 0)
+    put(send_ref, core == 1)
 
 
 def local_gram(core, panel, trailing):
     n, rows = panel.shape
     t = trailing.shape[0]
+    steps = rows // CHUNK
     out = jax.ShapeDtypeStruct((n // 2 + 16 + t // 2, n), F32)
-    whole = pl.BlockSpec(out.shape, lambda i: (0, 0))
+    vmem, hbm = pl.BlockSpec(memory_space=pltpu.VMEM), pl.BlockSpec(memory_space=pltpu.HBM)
     return pl.pallas_call(
         gram_kernel,
-        grid=(rows // CHUNK,),
-        in_specs=[
-            pl.BlockSpec(memory_space=pltpu.SMEM),
-            pl.BlockSpec((n, CHUNK), lambda i: (0, i)),
-            pl.BlockSpec((t, CHUNK), lambda i: (0, i)),
-        ],
-        out_specs=[whole, whole],
+        in_specs=[pl.BlockSpec(memory_space=pltpu.SMEM), hbm, hbm],
+        out_specs=[vmem, vmem],
         out_shape=[out, out],
         scratch_shapes=[
-            pltpu.VMEM((3 * (n + t), CHUNK), BF16),
+            pltpu.VMEM((steps, n, CHUNK), F32),
+            pltpu.VMEM((steps, t, CHUNK), F32),
+            pltpu.VMEM((steps, 3 * (n + t), CHUNK), BF16),
+            pltpu.VMEM((n, n), F32),
             pltpu.VMEM((n, n), F32),
             pltpu.VMEM((n, n), F32),
             pltpu.VMEM((t, n), F32),
+            pltpu.VMEM((n, t), F32),
+            pltpu.SemaphoreType.DMA((2, steps)),
         ],
         compiler_params=pltpu.CompilerParams(vmem_limit_bytes=32 << 20),
         name="gram",
@@ -338,25 +359,52 @@
     )(core, own, other)
 
 
-def apply_kernel(rows_all, wz_ref, panel_ref, trail_ref, basis_ref, updated_ref):
-    n = panel_ref.shape[0]
-    width = basis_ref.shape[1]
-    at = pl.multiple_of(pl.program_id(0) * width, width)
-    out = nn(wz_ref[...], panel_ref[:, pl.ds(at, width)], precision=HIGHEST)
-    basis_ref[...] = out[:n, :] * jnp.sqrt(jnp.float32(rows_all))
-    updated_ref[...] = trail_ref[:, pl.ds(at, width)] - out[n:, :]
+def apply_kernel(rows_all, wz_ref, panel_ref, trail_ref, basis, updated, words, basis_buf, updated_buf, sems):
+    n, rows = panel_ref.shape
+    root = jnp.sqrt(jnp.float32(rows_all))
+
+    def split(x):
+        x1 = x.astype(BF16)
+        rest = x - x1.astype(F32)
+        x2 = rest.astype(BF16)
+        return x1, x2, (rest - x2.astype(F32)).astype(BF16)
+
+    w1, w2, w3 = split(wz_ref[...])
+    for k, w in enumerate((w1, w2, w1, w2, w1, w3)):
+        words[:, k * n : (k + 1) * n] = w
+    copies = []
+    for k in range(rows // OUT_CHUNK):
+        at = pl.ds(k * OUT_CHUNK, OUT_CHUNK)
+        a1, a2, a3 = split(panel_ref[:, at])
+        out = nn(words[...], jnp.concatenate([a1, a2, a2, a1, a3, a1], axis=0))
+        basis_buf[k] = out[:n, :] * root
+        updated_buf[k] = trail_ref[:, at] - out[n:, :]
+        for copy in (
+            pltpu.make_async_copy(basis_buf.at[k], basis.at[:, at], sems.at[0, k]),
+            pltpu.make_async_copy(updated_buf.at[k], updated.at[:, at], sems.at[1, k]),
+        ):
+            copy.start()
+            copies.append(copy)
+    for copy in copies:
+        copy.wait()
 
 
 def apply_factors(wz, panel, trailing, rows_all):
     n, rows = panel.shape
     t = trailing.shape[0]
-    spec = pl.BlockSpec(memory_space=pltpu.VMEM)
+    steps = rows // OUT_CHUNK
+    vmem, hbm = pl.BlockSpec(memory_space=pltpu.VMEM), pl.BlockSpec(memory_space=pltpu.HBM)
     return pl.pallas_call(
         lambda *refs: apply_kernel(rows_all, *refs),
-        grid=(rows // OUT_CHUNK,),
-        in_specs=[spec, spec, spec],
-        out_specs=[pl.BlockSpec((n, OUT_CHUNK), lambda i: (0, i)), pl.BlockSpec((t, OUT_CHUNK), lambda i: (0, i))],
+        in_specs=[vmem] * 3,
+        out_specs=[hbm] * 2,
         out_shape=[jax.ShapeDtypeStruct((n, rows), F32), jax.ShapeDtypeStruct((t, rows), F32)],
+        scratch_shapes=[
+            pltpu.VMEM((n + t, 6 * n), BF16),
+            pltpu.VMEM((steps, n, OUT_CHUNK), F32),
+            pltpu.VMEM((steps, t, OUT_CHUNK), F32),
+            pltpu.SemaphoreType.DMA((2, steps)),
+        ],
         compiler_params=pltpu.CompilerParams(vmem_limit_bytes=32 << 20),
         name="apply",
     )(wz, panel, trailing)

time: 51.2 us -> 47.7 us (0.932)
  Pallas kernels: 17.3 us -> 13.6 us
    pallas_call x2, Pallas kernels: 10.7 us -> 6.89 us  [the longest x1 4.43 us: local_gram(): pl.pallas_call(gram_kernel, in_specs=[pl.BlockSpec(memory_space=pltpu.SME...]
where the time goes in v2:
time: 47.7 us; the launch traced here: 47.6 us
  starting transfers between devices  19.5 us (41%)
  Pallas kernels  13.6 us (29%)
  waiting for transfers between devices  13.4 us (28%)
  between operations  0.9 us (2%)
    ppermute x11, starting transfers between devices, exchange(): return lax.ppermute(value, AXES, [(s, s ^ mask) for s in range(size)])  19.5 us
    ppermute x11, waiting for transfers between devices, exchange(): return lax.ppermute(value, AXES, [(s, s ^ mask) for s in range(size)])  13.4 us
    pallas_call x1, Pallas kernels, factor(): pl.pallas_call(lambda *refs: factor_kernel(rows_all, *refs), in_specs=[pl...  6.75 us
    pallas_call x1, Pallas kernels, local_gram(): pl.pallas_call(gram_kernel, in_specs=[pl.BlockSpec(memory_space=pltpu.SME...  4.43 us
    pallas_call x1, Pallas kernels, apply_factors(): pl.pallas_call(lambda *refs: apply_kernel(rows_all, *refs), in_specs=[vme...  2.46 us
  transfers between devices with their start and end apart: 11, of which 8 were waited for; matrix products, arithmetic and copies ran while one was open for 0% of the time, Pallas kernels for 0%

profile of v2, /device:TPU:1, one launch (start us, length us, event | category | flops | bytes accessed | tf_op | source)
XLA Modules:
  0.0 47.6 jit_solution(16951114781221214057)
XLA Ops:
  0.7 4.4 %gram.1 = (f32[112,128]{1,0:T(8,128)S(1)}, f32[112,128]{1,0:T(8,128)S(1)}) custom-call(s32[1]{0:T(128)} %bitcast.core_ref.refs_0_, f32[128,4096]{1,0:T(8,128)} %refs_1_.1, f32[64,4096]{1,0:T(8,128)} %refs_2_.1), custom_call_target="tpu_custom_call" | custom-call | tf_op jit(solution)/shard_map/gram/pallas_call | solution.py:171
  5.1 1.5 %collective-permute-start = (f32[112,128]{1,0:T(8,128)S(1)}, f32[112,128]{1,0:T(8,128)S(1)}, u32[]{:S(2)}, u32[]{:S(2)}) collective-permute-start(f32[112,128]{1,0:T(8,128)S(1)} %get-tuple-element.12), channel_id=1, source_target_pairs={{0,4},{1,5},{2,6},{3,7},{4,0},{5,1},{6,2},{7,3},{8,12},{9,13},{10,... | collective-permute-start | bytes 172040 | tf_op jit(solution)/shard_map/ppermute | solution.py:207
  6.6 0.9 %collective-permute-done = f32[112,128]{1,0:T(8,128)S(1)} collective-permute-done((f32[112,128]{1,0:T(8,128)S(1)}, f32[112,128]{1,0:T(8,128)S(1)}, u32[]{:S(2)}, u32[]{:S(2)}) %collective-permute-start) | collective-permute-done | bytes 57376 | tf_op jit(solution)/shard_map/ppermute | solution.py:207
  7.5 1.5 %collective-permute-start.1 = (f32[112,128]{1,0:T(8,128)S(1)}, f32[112,128]{1,0:T(8,128)S(1)}, u32[]{:S(2)}, u32[]{:S(2)}) collective-permute-start(f32[112,128]{1,0:T(8,128)S(1)} %pad_add_fusion.3), channel_id=1, source_target_pairs={{0,1},{1,0},{2,3},{3,2},{4,5},{5,4},{6,7},{7,6},{8,9},{9,8},{10,11... | collective-permute-start | bytes 172040 | tf_op jit(solution)/shard_map/ppermute | solution.py:207
  9.0 1.9 %collective-permute-start.3 = (f32[112,128]{1,0:T(8,128)S(1)}, f32[112,128]{1,0:T(8,128)S(1)}, u32[]{:S(2)}, u32[]{:S(2)}) collective-permute-start(f32[112,128]{1,0:T(8,128)S(1)} %pad_add_fusion.3), channel_id=1, source_target_pairs={{0,3},{1,2},{2,1},{3,0},{4,7},{5,6},{6,5},{7,4},{8,11},{9,10},{10,... | collective-permute-start | bytes 172040 | tf_op jit(solution)/shard_map/ppermute | solution.py:207
  10.9 0.7 %collective-permute-start.2 = (f32[112,128]{1,0:T(8,128)S(1)}, f32[112,128]{1,0:T(8,128)S(1)}, u32[]{:S(2)}, u32[]{:S(2)}) collective-permute-start(f32[112,128]{1,0:T(8,128)S(1)} %pad_add_fusion.3), channel_id=1, source_target_pairs={{0,2},{1,3},{2,0},{3,1},{4,6},{5,7},{6,4},{7,5},{8,10},{9,11},{10,... | collective-permute-start | bytes 172040 | tf_op jit(solution)/shard_map/ppermute | solution.py:207
  11.6 0.0 collective-permute-done.1
  11.6 1.6 %collective-permute-done.3 = f32[112,128]{1,0:T(8,128)S(1)} collective-permute-done((f32[112,128]{1,0:T(8,128)S(1)}, f32[112,128]{1,0:T(8,128)S(1)}, u32[]{:S(2)}, u32[]{:S(2)}) %collective-permute-start.3) | collective-permute-done | bytes 57376 | tf_op jit(solution)/shard_map/ppermute | solution.py:207
  13.2 2.2 %collective-permute-done.2 = f32[112,128]{1,0:T(8,128)S(1)} collective-permute-done((f32[112,128]{1,0:T(8,128)S(1)}, f32[112,128]{1,0:T(8,128)S(1)}, u32[]{:S(2)}, u32[]{:S(2)}) %collective-permute-start.2) | collective-permute-done | bytes 57376 | tf_op jit(solution)/shard_map/ppermute | solution.py:207
  15.5 1.3 %collective-permute-start.4 = (f32[112,128]{1,0:T(8,128)S(1)}, f32[112,128]{1,0:T(8,128)S(1)}, u32[]{:S(2)}, u32[]{:S(2)}) collective-permute-start(f32[112,128]{1,0:T(8,128)S(1)} %pad_add_fusion.2), channel_id=1, source_target_pairs={{0,8},{1,9},{2,10},{3,11},{4,12},{5,13},{6,14},{7,15},{8,0},{9,1},... | collective-permute-start | bytes 172040 | tf_op jit(solution)/shard_map/ppermute | solution.py:207
  16.8 1.8 %collective-permute-start.6 = (f32[112,128]{1,0:T(8,128)S(1)}, f32[112,128]{1,0:T(8,128)S(1)}, u32[]{:S(2)}, u32[]{:S(2)}) collective-permute-start(f32[112,128]{1,0:T(8,128)S(1)} %pad_add_fusion.2), channel_id=1, source_target_pairs={{0,72},{1,73},{2,74},{3,75},{4,76},{5,77},{6,78},{7,79},{8,64},{9,... | collective-permute-start | bytes 172040 | tf_op jit(solution)/shard_map/ppermute | solution.py:207
  18.6 0.6 %collective-permute-start.5 = (f32[112,128]{1,0:T(8,128)S(1)}, f32[112,128]{1,0:T(8,128)S(1)}, u32[]{:S(2)}, u32[]{:S(2)}) collective-permute-start(f32[112,128]{1,0:T(8,128)S(1)} %pad_add_fusion.2), channel_id=1, source_target_pairs={{0,64},{1,65},{2,66},{3,67},{4,68},{5,69},{6,70},{7,71},{8,72},{9,... | collective-permute-start | bytes 172040 | tf_op jit(solution)/shard_map/ppermute | solution.py:207
  19.2 0.0 collective-permute-done.4
  19.2 1.8 %collective-permute-done.6 = f32[112,128]{1,0:T(8,128)S(1)} collective-permute-done((f32[112,128]{1,0:T(8,128)S(1)}, f32[112,128]{1,0:T(8,128)S(1)}, u32[]{:S(2)}, u32[]{:S(2)}) %collective-permute-start.6) | collective-permute-done | bytes 57376 | tf_op jit(solution)/shard_map/ppermute | solution.py:207
  21.0 2.5 %collective-permute-done.5 = f32[112,128]{1,0:T(8,128)S(1)} collective-permute-done((f32[112,128]{1,0:T(8,128)S(1)}, f32[112,128]{1,0:T(8,128)S(1)}, u32[]{:S(2)}, u32[]{:S(2)}) %collective-permute-start.5) | collective-permute-done | bytes 57376 | tf_op jit(solution)/shard_map/ppermute | solution.py:207
  23.6 1.7 %collective-permute-start.7 = (f32[112,128]{1,0:T(8,128)S(1)}, f32[112,128]{1,0:T(8,128)S(1)}, u32[]{:S(2)}, u32[]{:S(2)}) collective-permute-start(f32[112,128]{1,0:T(8,128)S(1)} %pad_add_fusion.1), channel_id=1, source_target_pairs={{0,16},{1,17},{2,18},{3,19},{4,20},{5,21},{6,22},{7,23},{8,24},{9,... | collective-permute-start | bytes 172040 | tf_op jit(solution)/shard_map/ppermute | solution.py:207
  25.3 2.3 %collective-permute-start.9 = (f32[112,128]{1,0:T(8,128)S(1)}, f32[112,128]{1,0:T(8,128)S(1)}, u32[]{:S(2)}, u32[]{:S(2)}) collective-permute-start(f32[112,128]{1,0:T(8,128)S(1)} %pad_add_fusion.1), channel_id=1, source_target_pairs={{0,48},{1,49},{2,50},{3,51},{4,52},{5,53},{6,54},{7,55},{8,56},{9,... | collective-permute-start | bytes 172040 | tf_op jit(solution)/shard_map/ppermute | solution.py:207
  27.6 1.1 %collective-permute-start.8 = (f32[112,128]{1,0:T(8,128)S(1)}, f32[112,128]{1,0:T(8,128)S(1)}, u32[]{:S(2)}, u32[]{:S(2)}) collective-permute-start(f32[112,128]{1,0:T(8,128)S(1)} %pad_add_fusion.1), channel_id=1, source_target_pairs={{0,32},{1,33},{2,34},{3,35},{4,36},{5,37},{6,38},{7,39},{8,40},{9,... | collective-permute-start | bytes 172040 | tf_op jit(solution)/shard_map/ppermute | solution.py:207
  28.6 0.9 %collective-permute-done.9 = f32[112,128]{1,0:T(8,128)S(1)} collective-permute-done((f32[112,128]{1,0:T(8,128)S(1)}, f32[112,128]{1,0:T(8,128)S(1)}, u32[]{:S(2)}, u32[]{:S(2)}) %collective-permute-start.9) | collective-permute-done | bytes 57376 | tf_op jit(solution)/shard_map/ppermute | solution.py:207
  29.5 2.6 %collective-permute-done.8 = f32[112,128]{1,0:T(8,128)S(1)} collective-permute-done((f32[112,128]{1,0:T(8,128)S(1)}, f32[112,128]{1,0:T(8,128)S(1)}, u32[]{:S(2)}, u32[]{:S(2)}) %collective-permute-start.8) | collective-permute-done | bytes 57376 | tf_op jit(solution)/shard_map/ppermute | solution.py:207
  32.2 5.1 %collective-permute-start.10 = (f32[112,128]{1,0:T(8,128)S(1)}, f32[112,128]{1,0:T(8,128)S(1)}, u32[]{:S(2)}, u32[]{:S(2)}) collective-permute-start(f32[112,128]{1,0:T(8,128)S(1)} %pad_add_fusion.refs_1_), channel_id=1, source_target_pairs={{0,4},{1,5},{2,6},{3,7},{4,0},{5,1},{6,2},{7,3},{8,12},{9,13},{10,... | collective-permute-start | bytes 172040 | tf_op jit(solution)/shard_map/ppermute | solution.py:207
  37.3 0.9 %collective-permute-done.10.refs_2_ = f32[112,128]{1,0:T(8,128)S(1)} collective-permute-done((f32[112,128]{1,0:T(8,128)S(1)}, f32[112,128]{1,0:T(8,128)S(1)}, u32[]{:S(2)}, u32[]{:S(2)}) %collective-permute-start.10) | collective-permute-done | bytes 57376 | tf_op jit(solution)/shard_map/ppermute | solution.py:207
  38.2 6.7 %factor.1 = (f32[192,128]{1,0:T(8,128)S(1)}, f32[128,128]{1,0:T(8,128)}, f32[64,128]{1,0:T(8,128)}) custom-call(s32[1]{0:T(128)} %bitcast.core_ref.refs_0_, f32[112,128]{1,0:T(8,128)S(1)} %pad_add_fusion.refs_1_, f32[112,128]{1,0:T(8,128)S(1)} %collective-permute-done.10.refs_2_), custom_call_target="tpu_custom_call" | custom-call | tf_op jit(solution)/shard_map/factor/pallas_call | solution.py:342
  44.9 2.5 %apply.1 = (f32[128,4096]{1,0:T(8,128)}, f32[64,4096]{1,0:T(8,128)}) custom-call(f32[192,128]{1,0:T(8,128)S(1)} %get-tuple-element.13.refs_0_, f32[128,4096]{1,0:T(8,128)S(1)} %copy-done, f32[64,4096]{1,0:T(8,128)S(1)} %copy-done.1), custom_call_target="tpu_custom_call" | custom-call | tf_op jit(solution)/shard_map/apply/pallas_call | solution.py:397
  (19 shorter events, 0.2 us)
Async XLA Ops:
  0.6 44.3 %copy-start = (f32[128,4096]{1,0:T(8,128)S(1)}, f32[128,4096]{1,0:T(8,128)}, u32[]{:S(2)}) copy-start(f32[128,4096]{1,0:T(8,128)} %refs_1_.1) | copy-start | bytes 6291460
  0.7 44.3 %copy-start.1 = (f32[64,4096]{1,0:T(8,128)S(1)}, f32[64,4096]{1,0:T(8,128)}, u32[]{:S(2)}) copy-start(f32[64,4096]{1,0:T(8,128)} %refs_2_.1) | copy-start | bytes 3145732
  5.1 2.4 %collective-permute-start = (f32[112,128]{1,0:T(8,128)S(1)}, f32[112,128]{1,0:T(8,128)S(1)}, u32[]{:S(2)}, u32[]{:S(2)}) collective-permute-start(f32[112,128]{1,0:T(8,128)S(1)} %get-tuple-element.12), channel_id=1, source_target_pairs={{0,4},{1,5},{2,6},{3,7},{4,0},{5,1},{6,2},{7,3},{8,12},{9,13},{10,... | collective-permute-start | bytes 172040 | tf_op jit(solution)/shard_map/ppermute | solution.py:207
  7.5 4.1 %collective-permute-start.1 = (f32[112,128]{1,0:T(8,128)S(1)}, f32[112,128]{1,0:T(8,128)S(1)}, u32[]{:S(2)}, u32[]{:S(2)}) collective-permute-start(f32[112,128]{1,0:T(8,128)S(1)} %pad_add_fusion.3), channel_id=1, source_target_pairs={{0,1},{1,0},{2,3},{3,2},{4,5},{5,4},{6,7},{7,6},{8,9},{9,8},{10,11... | collective-permute-start | bytes 172040 | tf_op jit(solution)/shard_map/ppermute | solution.py:207
  9.0 4.2 %collective-permute-start.3 = (f32[112,128]{1,0:T(8,128)S(1)}, f32[112,128]{1,0:T(8,128)S(1)}, u32[]{:S(2)}, u32[]{:S(2)}) collective-permute-start(f32[112,128]{1,0:T(8,128)S(1)} %pad_add_fusion.3), channel_id=1, source_target_pairs={{0,3},{1,2},{2,1},{3,0},{4,7},{5,6},{6,5},{7,4},{8,11},{9,10},{10,... | collective-permute-start | bytes 172040 | tf_op jit(solution)/shard_map/ppermute | solution.py:207
  10.9 4.5 %collective-permute-start.2 = (f32[112,128]{1,0:T(8,128)S(1)}, f32[112,128]{1,0:T(8,128)S(1)}, u32[]{:S(2)}, u32[]{:S(2)}) collective-permute-start(f32[112,128]{1,0:T(8,128)S(1)} %pad_add_fusion.3), channel_id=1, source_target_pairs={{0,2},{1,3},{2,0},{3,1},{4,6},{5,7},{6,4},{7,5},{8,10},{9,11},{10,... | collective-permute-start | bytes 172040 | tf_op jit(solution)/shard_map/ppermute | solution.py:207
  15.5 3.7 %collective-permute-start.4 = (f32[112,128]{1,0:T(8,128)S(1)}, f32[112,128]{1,0:T(8,128)S(1)}, u32[]{:S(2)}, u32[]{:S(2)}) collective-permute-start(f32[112,128]{1,0:T(8,128)S(1)} %pad_add_fusion.2), channel_id=1, source_target_pairs={{0,8},{1,9},{2,10},{3,11},{4,12},{5,13},{6,14},{7,15},{8,0},{9,1},... | collective-permute-start | bytes 172040 | tf_op jit(solution)/shard_map/ppermute | solution.py:207
  16.8 4.2 %collective-permute-start.6 = (f32[112,128]{1,0:T(8,128)S(1)}, f32[112,128]{1,0:T(8,128)S(1)}, u32[]{:S(2)}, u32[]{:S(2)}) collective-permute-start(f32[112,128]{1,0:T(8,128)S(1)} %pad_add_fusion.2), channel_id=1, source_target_pairs={{0,72},{1,73},{2,74},{3,75},{4,76},{5,77},{6,78},{7,79},{8,64},{9,... | collective-permute-start | bytes 172040 | tf_op jit(solution)/shard_map/ppermute | solution.py:207
  18.6 5.0 %collective-permute-start.5 = (f32[112,128]{1,0:T(8,128)S(1)}, f32[112,128]{1,0:T(8,128)S(1)}, u32[]{:S(2)}, u32[]{:S(2)}) collective-permute-start(f32[112,128]{1,0:T(8,128)S(1)} %pad_add_fusion.2), channel_id=1, source_target_pairs={{0,64},{1,65},{2,66},{3,67},{4,68},{5,69},{6,70},{7,71},{8,72},{9,... | collective-permute-start | bytes 172040 | tf_op jit(solution)/shard_map/ppermute | solution.py:207
  23.6 5.0 %collective-permute-start.7 = (f32[112,128]{1,0:T(8,128)S(1)}, f32[112,128]{1,0:T(8,128)S(1)}, u32[]{:S(2)}, u32[]{:S(2)}) collective-permute-start(f32[112,128]{1,0:T(8,128)S(1)} %pad_add_fusion.1), channel_id=1, source_target_pairs={{0,16},{1,17},{2,18},{3,19},{4,20},{5,21},{6,22},{7,23},{8,24},{9,... | collective-permute-start | bytes 172040 | tf_op jit(solution)/shard_map/ppermute | solution.py:207
  25.3 4.2 %collective-permute-start.9 = (f32[112,128]{1,0:T(8,128)S(1)}, f32[112,128]{1,0:T(8,128)S(1)}, u32[]{:S(2)}, u32[]{:S(2)}) collective-permute-start(f32[112,128]{1,0:T(8,128)S(1)} %pad_add_fusion.1), channel_id=1, source_target_pairs={{0,48},{1,49},{2,50},{3,51},{4,52},{5,53},{6,54},{7,55},{8,56},{9,... | collective-permute-start | bytes 172040 | tf_op jit(solution)/shard_map/ppermute | solution.py:207
  27.6 4.5 %collective-permute-start.8 = (f32[112,128]{1,0:T(8,128)S(1)}, f32[112,128]{1,0:T(8,128)S(1)}, u32[]{:S(2)}, u32[]{:S(2)}) collective-permute-start(f32[112,128]{1,0:T(8,128)S(1)} %pad_add_fusion.1), channel_id=1, source_target_pairs={{0,32},{1,33},{2,34},{3,35},{4,36},{5,37},{6,38},{7,39},{8,40},{9,... | collective-permute-start | bytes 172040 | tf_op jit(solution)/shard_map/ppermute | solution.py:207
  32.2 6.0 %collective-permute-start.10 = (f32[112,128]{1,0:T(8,128)S(1)}, f32[112,128]{1,0:T(8,128)S(1)}, u32[]{:S(2)}, u32[]{:S(2)}) collective-permute-start(f32[112,128]{1,0:T(8,128)S(1)} %pad_add_fusion.refs_1_), channel_id=1, source_target_pairs={{0,4},{1,5},{2,6},{3,7},{4,0},{5,1},{6,2},{7,3},{8,12},{9,13},{10,... | collective-permute-start | bytes 172040 | tf_op jit(solution)/shard_map/ppermute | solution.py:207

commit v3 on v2

--- a/solution.py
+++ b/solution.py
@@ -238,7 +238,45 @@
     return w
 
 
-def factor_kernel(rows_all, core_ref, own_ref, other_ref, wz_ref, upper_ref, coup_ref, wcat, gcat, tcat, v_ref):
+def split3(x):
+    x1 = x.astype(BF16)
+    rest = x - x1.astype(F32)
+    x2 = rest.astype(BF16)
+    return x1, x2, (rest - x2.astype(F32)).astype(BF16)
+
+
+def apply_factors(wz, scale, panel, trailing, basis, updated, words, basis_buf, updated_buf, sems):
+    n, rows = panel.shape
+    w1, w2, w3 = split3(wz)
+    for k, w in enumerate((w1, w2, w1, w2, w1, w3)):
+        words[:, k * n : (k + 1) * n] = w
+    copies = []
+    for k in range(rows // OUT_CHUNK):
+        at = pl.ds(k * OUT_CHUNK, OUT_CHUNK)
+        a1, a2, a3 = split3(panel[:, at])
+        out = nn(words[...], jnp.concatenate([a1, a2, a2, a1, a3, a1], axis=0))
+        basis_buf[k] = out[:n, :] * scale
+        updated_buf[k] = trailing[:, at] - out[n:, :]
+        for copy in (
+            pltpu.make_async_copy(basis_buf.at[k], basis.at[:, at], sems.at[0, k]),
+            pltpu.make_async_copy(updated_buf.at[k], updated.at[:, at], sems.at[1, k]),
+        ):
+            copy.start()
+            copies.append(copy)
+    for copy in copies:
+        copy.wait()
+
+
+def factor_kernel(
+    rows_all, core_ref, own_ref, other_ref, panel, trailing, basis, updated, upper_ref, coup_ref,
+    wcat, gcat, tcat, v_ref, panel_buf, trail_buf, in_sems, words, basis_buf, updated_buf, out_sems,
+):
+    loads = (
+        pltpu.make_async_copy(panel, panel_buf, in_sems.at[0]),
+        pltpu.make_async_copy(trailing, trail_buf, in_sems.at[1]),
+    )
+    for load in loads:
+        load.start()
     n = upper_ref.shape[0]
     t = coup_ref.shape[0]
     half, q, tq = n // 2, n // 4, t // 2
@@ -333,18 +371,24 @@
     upper_ref[...] = jnp.where(i <= j, wide[:, n : 2 * n] / root, 0.0)
     coupling_t = wide[:, 2 * n :].T
     coup_ref[...] = coupling_t
-    wz_ref[:n, :] = w_new
-    wz_ref[n:, :] = nn(coupling_t, w_new, precision=HIGHEST)
-
-
-def factor(core, own, other, n, t, rows_all):
-    spec = pl.BlockSpec(memory_space=pltpu.VMEM)
+    wz = jnp.concatenate([w_new, nn(coupling_t, w_new, precision=HIGHEST)], axis=0)
+    for load in loads:
+        load.wait()
+    apply_factors(wz, root, panel_buf, trail_buf, basis, updated, words, basis_buf, updated_buf, out_sems)
+
+
+def factor(core, own, other, panel, trailing, rows_all):
+    n, rows = panel.shape
+    t = trailing.shape[0]
+    steps = rows // OUT_CHUNK
+    vmem, hbm = pl.BlockSpec(memory_space=pltpu.VMEM), pl.BlockSpec(memory_space=pltpu.HBM)
     return pl.pallas_call(
         lambda *refs: factor_kernel(rows_all, *refs),
-        in_specs=[pl.BlockSpec(memory_space=pltpu.SMEM), spec, spec],
-        out_specs=[spec] * 3,
+        in_specs=[pl.BlockSpec(memory_space=pltpu.SMEM), vmem, vmem, hbm, hbm],
+        out_specs=[hbm, hbm, vmem, vmem],
         out_shape=[
-            jax.ShapeDtypeStruct((n + t, n), F32),
+            jax.ShapeDtypeStruct((n, rows), F32),
+            jax.ShapeDtypeStruct((t, rows), F32),
             jax.ShapeDtypeStruct((n, n), F32),
             jax.ShapeDtypeStruct((t, n), F32),
         ],
@@ -353,61 +397,17 @@
             pltpu.VMEM((6 * n, n), BF16),
             pltpu.VMEM((n, 4 * n), BF16),
             pltpu.VMEM((n, n), F32),
-        ],
-        compiler_params=pltpu.CompilerParams(vmem_limit_bytes=32 << 20),
-        name="factor",
-    )(core, own, other)
-
-
-def apply_kernel(rows_all, wz_ref, panel_ref, trail_ref, basis, updated, words, basis_buf, updated_buf, sems):
-    n, rows = panel_ref.shape
-    root = jnp.sqrt(jnp.float32(rows_all))
-
-    def split(x):
-        x1 = x.astype(BF16)
-        rest = x - x1.astype(F32)
-        x2 = rest.astype(BF16)
-        return x1, x2, (rest - x2.astype(F32)).astype(BF16)
-
-    w1, w2, w3 = split(wz_ref[...])
-    for k, w in enumerate((w1, w2, w1, w2, w1, w3)):
-        words[:, k * n : (k + 1) * n] = w
-    copies = []
-    for k in range(rows // OUT_CHUNK):
-        at = pl.ds(k * OUT_CHUNK, OUT_CHUNK)
-        a1, a2, a3 = split(panel_ref[:, at])
-        out = nn(words[...], jnp.concatenate([a1, a2, a2, a1, a3, a1], axis=0))
-        basis_buf[k] = out[:n, :] * root
-        updated_buf[k] = trail_ref[:, at] - out[n:, :]
-        for copy in (
-            pltpu.make_async_copy(basis_buf.at[k], basis.at[:, at], sems.at[0, k]),
-            pltpu.make_async_copy(updated_buf.at[k], updated.at[:, at], sems.at[1, k]),
-        ):
-            copy.start()
-            copies.append(copy)
-    for copy in copies:
-        copy.wait()
-
-
-def apply_factors(wz, panel, trailing, rows_all):
-    n, rows = panel.shape
-    t = trailing.shape[0]
-    steps = rows // OUT_CHUNK
-    vmem, hbm = pl.BlockSpec(memory_space=pltpu.VMEM), pl.BlockSpec(memory_space=pltpu.HBM)
-    return pl.pallas_call(
-        lambda *refs: apply_kernel(rows_all, *refs),
-        in_specs=[vmem] * 3,
-        out_specs=[hbm] * 2,
-        out_shape=[jax.ShapeDtypeStruct((n, rows), F32), jax.ShapeDtypeStruct((t, rows), F32)],
-        scratch_shapes=[
+            pltpu.VMEM((n, rows), F32),
+            pltpu.VMEM((t, rows), F32),
+            pltpu.SemaphoreType.DMA((2,)),
             pltpu.VMEM((n + t, 6 * n), BF16),
             pltpu.VMEM((steps, n, OUT_CHUNK), F32),
             pltpu.VMEM((steps, t, OUT_CHUNK), F32),
             pltpu.SemaphoreType.DMA((2, steps)),
         ],
-        compiler_params=pltpu.CompilerParams(vmem_limit_bytes=32 << 20),
-        name="apply",
-    )(wz, panel, trailing)
+        compiler_params=pltpu.CompilerParams(vmem_limit_bytes=48 << 20),
+        name="factor",
+    )(core, own, other, panel, trailing)
 
 
 def shards(panel, trailing):
@@ -415,15 +415,14 @@
     rows_all = panel.shape[1] * lax.axis_size(AXES)
     core = jnp.reshape(lax.axis_index("gy") % 2, (1,)).astype(jnp.int32)
     words = n // 4 + 8
-    streamed = (pltpu.with_memory_space_constraint(a, pltpu.HBM) for a in (panel, trailing))
-    keep, send = local_gram(core, *streamed)
+    panel, trailing = (pltpu.with_memory_space_constraint(a, pltpu.HBM) for a in (panel, trailing))
+    keep, send = local_gram(core, panel, trailing)
     total = add_packed(words, keep, exchange(send, 4))
     for masks in ((1, 3, 2), (8, 72, 64), (16, 48, 32)):
         near, wrap, far = (exchange(total, m) for m in masks)
         total = add_packed(words, total, near, far, wrap)
     other = exchange(total, 4)
-    wz, upper, coupling_t = factor(core, total, other, n, t, rows_all)
-    basis_t, updated = apply_factors(wz, panel, trailing, rows_all)
+    basis_t, updated, upper, coupling_t = factor(core, total, other, panel, trailing, rows_all)
     return basis_t, upper, coupling_t.T, updated
 
 

time: 47.7 us -> 47.6 us (level)
    pallas_call x1, Pallas kernels: 6.75 us -> 9.35 us  [factor(): pl.pallas_call(lambda *refs: factor_kernel(rows_all, *refs), in_specs=[pl...]
    pallas_call x1 -> x0, Pallas kernels: 2.46 us -> none  [apply_factors(): pl.pallas_call(lambda *refs: apply_kernel(rows_all, *refs), in_specs=[vme...]
where the time goes in v3:
time: 47.6 us; the launch traced here: 47.5 us
  starting transfers between devices  19.5 us (41%)
  Pallas kernels  13.6 us (29%)
  waiting for transfers between devices  13.4 us (28%)
  between operations  0.88 us (2%)
    ppermute x11, starting transfers between devices, exchange(): return lax.ppermute(value, AXES, [(s, s ^ mask) for s in range(size)])  19.5 us
    ppermute x11, waiting for transfers between devices, exchange(): return lax.ppermute(value, AXES, [(s, s ^ mask) for s in range(size)])  13.4 us
    pallas_call x1, Pallas kernels, factor(): pl.pallas_call(lambda *refs: factor_kernel(rows_all, *refs), in_specs=[pl...  9.35 us
    pallas_call x1, Pallas kernels, local_gram(): pl.pallas_call(gram_kernel, in_specs=[pl.BlockSpec(memory_space=pltpu.SME...  4.28 us
  transfers between devices with their start and end apart: 11, of which 8 were waited for; matrix products, arithmetic and copies ran while one was open for 0% of the time, Pallas kernels for 0%

profile of v3, /device:TPU:1, one launch (start us, length us, event | category | flops | bytes accessed | tf_op | source)
XLA Modules:
  0.0 47.5 jit_solution(6963530999531142109)
XLA Ops:
  0.6 4.3 %gram.1 = (f32[112,128]{1,0:T(8,128)S(1)}, f32[112,128]{1,0:T(8,128)S(1)}) custom-call(s32[1]{0:T(128)} %bitcast.core_ref.refs_0_, f32[128,4096]{1,0:T(8,128)} %refs_3_.1, f32[64,4096]{1,0:T(8,128)} %refs_4_.1), custom_call_target="tpu_custom_call" | custom-call | tf_op jit(solution)/shard_map/gram/pallas_call | solution.py:171
  4.9 1.5 %collective-permute-start = (f32[112,128]{1,0:T(8,128)S(1)}, f32[112,128]{1,0:T(8,128)S(1)}, u32[]{:S(2)}, u32[]{:S(2)}) collective-permute-start(f32[112,128]{1,0:T(8,128)S(1)} %get-tuple-element.11), channel_id=1, source_target_pairs={{0,4},{1,5},{2,6},{3,7},{4,0},{5,1},{6,2},{7,3},{8,12},{9,13},{10,... | collective-permute-start | bytes 172040 | tf_op jit(solution)/shard_map/ppermute | solution.py:207
  6.4 0.9 %collective-permute-done = f32[112,128]{1,0:T(8,128)S(1)} collective-permute-done((f32[112,128]{1,0:T(8,128)S(1)}, f32[112,128]{1,0:T(8,128)S(1)}, u32[]{:S(2)}, u32[]{:S(2)}) %collective-permute-start) | collective-permute-done | bytes 57376 | tf_op jit(solution)/shard_map/ppermute | solution.py:207
  7.4 1.5 %collective-permute-start.1 = (f32[112,128]{1,0:T(8,128)S(1)}, f32[112,128]{1,0:T(8,128)S(1)}, u32[]{:S(2)}, u32[]{:S(2)}) collective-permute-start(f32[112,128]{1,0:T(8,128)S(1)} %pad_add_fusion.3), channel_id=1, source_target_pairs={{0,1},{1,0},{2,3},{3,2},{4,5},{5,4},{6,7},{7,6},{8,9},{9,8},{10,11... | collective-permute-start | bytes 172040 | tf_op jit(solution)/shard_map/ppermute | solution.py:207
  8.8 1.9 %collective-permute-start.3 = (f32[112,128]{1,0:T(8,128)S(1)}, f32[112,128]{1,0:T(8,128)S(1)}, u32[]{:S(2)}, u32[]{:S(2)}) collective-permute-start(f32[112,128]{1,0:T(8,128)S(1)} %pad_add_fusion.3), channel_id=1, source_target_pairs={{0,3},{1,2},{2,1},{3,0},{4,7},{5,6},{6,5},{7,4},{8,11},{9,10},{10,... | collective-permute-start | bytes 172040 | tf_op jit(solution)/shard_map/ppermute | solution.py:207
  10.7 0.7 %collective-permute-start.2 = (f32[112,128]{1,0:T(8,128)S(1)}, f32[112,128]{1,0:T(8,128)S(1)}, u32[]{:S(2)}, u32[]{:S(2)}) collective-permute-start(f32[112,128]{1,0:T(8,128)S(1)} %pad_add_fusion.3), channel_id=1, source_target_pairs={{0,2},{1,3},{2,0},{3,1},{4,6},{5,7},{6,4},{7,5},{8,10},{9,11},{10,... | collective-permute-start | bytes 172040 | tf_op jit(solution)/shard_map/ppermute | solution.py:207
  11.4 0.0 collective-permute-done.1
  11.4 1.6 %collective-permute-done.3 = f32[112,128]{1,0:T(8,128)S(1)} collective-permute-done((f32[112,128]{1,0:T(8,128)S(1)}, f32[112,128]{1,0:T(8,128)S(1)}, u32[]{:S(2)}, u32[]{:S(2)}) %collective-permute-start.3) | collective-permute-done | bytes 57376 | tf_op jit(solution)/shard_map/ppermute | solution.py:207
  13.1 2.2 %collective-permute-done.2 = f32[112,128]{1,0:T(8,128)S(1)} collective-permute-done((f32[112,128]{1,0:T(8,128)S(1)}, f32[112,128]{1,0:T(8,128)S(1)}, u32[]{:S(2)}, u32[]{:S(2)}) %collective-permute-start.2) | collective-permute-done | bytes 57376 | tf_op jit(solution)/shard_map/ppermute | solution.py:207
  15.3 1.3 %collective-permute-start.4 = (f32[112,128]{1,0:T(8,128)S(1)}, f32[112,128]{1,0:T(8,128)S(1)}, u32[]{:S(2)}, u32[]{:S(2)}) collective-permute-start(f32[112,128]{1,0:T(8,128)S(1)} %pad_add_fusion.2), channel_id=1, source_target_pairs={{0,8},{1,9},{2,10},{3,11},{4,12},{5,13},{6,14},{7,15},{8,0},{9,1},... | collective-permute-start | bytes 172040 | tf_op jit(solution)/shard_map/ppermute | solution.py:207
  16.6 1.8 %collective-permute-start.6 = (f32[112,128]{1,0:T(8,128)S(1)}, f32[112,128]{1,0:T(8,128)S(1)}, u32[]{:S(2)}, u32[]{:S(2)}) collective-permute-start(f32[112,128]{1,0:T(8,128)S(1)} %pad_add_fusion.2), channel_id=1, source_target_pairs={{0,72},{1,73},{2,74},{3,75},{4,76},{5,77},{6,78},{7,79},{8,64},{9,... | collective-permute-start | bytes 172040 | tf_op jit(solution)/shard_map/ppermute | solution.py:207
  18.4 0.6 %collective-permute-start.5 = (f32[112,128]{1,0:T(8,128)S(1)}, f32[112,128]{1,0:T(8,128)S(1)}, u32[]{:S(2)}, u32[]{:S(2)}) collective-permute-start(f32[112,128]{1,0:T(8,128)S(1)} %pad_add_fusion.2), channel_id=1, source_target_pairs={{0,64},{1,65},{2,66},{3,67},{4,68},{5,69},{6,70},{7,71},{8,72},{9,... | collective-permute-start | bytes 172040 | tf_op jit(solution)/shard_map/ppermute | solution.py:207
  19.0 0.0 collective-permute-done.4
  19.1 1.8 %collective-permute-done.6 = f32[112,128]{1,0:T(8,128)S(1)} collective-permute-done((f32[112,128]{1,0:T(8,128)S(1)}, f32[112,128]{1,0:T(8,128)S(1)}, u32[]{:S(2)}, u32[]{:S(2)}) %collective-permute-start.6) | collective-permute-done | bytes 57376 | tf_op jit(solution)/shard_map/ppermute | solution.py:207
  20.8 2.5 %collective-permute-done.5 = f32[112,128]{1,0:T(8,128)S(1)} collective-permute-done((f32[112,128]{1,0:T(8,128)S(1)}, f32[112,128]{1,0:T(8,128)S(1)}, u32[]{:S(2)}, u32[]{:S(2)}) %collective-permute-start.5) | collective-permute-done | bytes 57376 | tf_op jit(solution)/shard_map/ppermute | solution.py:207
  23.4 1.7 %collective-permute-start.7 = (f32[112,128]{1,0:T(8,128)S(1)}, f32[112,128]{1,0:T(8,128)S(1)}, u32[]{:S(2)}, u32[]{:S(2)}) collective-permute-start(f32[112,128]{1,0:T(8,128)S(1)} %pad_add_fusion.1), channel_id=1, source_target_pairs={{0,16},{1,17},{2,18},{3,19},{4,20},{5,21},{6,22},{7,23},{8,24},{9,... | collective-permute-start | bytes 172040 | tf_op jit(solution)/shard_map/ppermute | solution.py:207
  25.1 2.3 %collective-permute-start.9 = (f32[112,128]{1,0:T(8,128)S(1)}, f32[112,128]{1,0:T(8,128)S(1)}, u32[]{:S(2)}, u32[]{:S(2)}) collective-permute-start(f32[112,128]{1,0:T(8,128)S(1)} %pad_add_fusion.1), channel_id=1, source_target_pairs={{0,48},{1,49},{2,50},{3,51},{4,52},{5,53},{6,54},{7,55},{8,56},{9,... | collective-permute-start | bytes 172040 | tf_op jit(solution)/shard_map/ppermute | solution.py:207
  27.4 1.1 %collective-permute-start.8 = (f32[112,128]{1,0:T(8,128)S(1)}, f32[112,128]{1,0:T(8,128)S(1)}, u32[]{:S(2)}, u32[]{:S(2)}) collective-permute-start(f32[112,128]{1,0:T(8,128)S(1)} %pad_add_fusion.1), channel_id=1, source_target_pairs={{0,32},{1,33},{2,34},{3,35},{4,36},{5,37},{6,38},{7,39},{8,40},{9,... | collective-permute-start | bytes 172040 | tf_op jit(solution)/shard_map/ppermute | solution.py:207
  28.4 0.0 collective-permute-done.7
  28.5 0.9 %collective-permute-done.9 = f32[112,128]{1,0:T(8,128)S(1)} collective-permute-done((f32[112,128]{1,0:T(8,128)S(1)}, f32[112,128]{1,0:T(8,128)S(1)}, u32[]{:S(2)}, u32[]{:S(2)}) %collective-permute-start.9) | collective-permute-done | bytes 57376 | tf_op jit(solution)/shard_map/ppermute | solution.py:207
  29.4 2.5 %collective-permute-done.8 = f32[112,128]{1,0:T(8,128)S(1)} collective-permute-done((f32[112,128]{1,0:T(8,128)S(1)}, f32[112,128]{1,0:T(8,128)S(1)}, u32[]{:S(2)}, u32[]{:S(2)}) %collective-permute-start.8) | collective-permute-done | bytes 57376 | tf_op jit(solution)/shard_map/ppermute | solution.py:207
  32.0 5.1 %collective-permute-start.10 = (f32[112,128]{1,0:T(8,128)S(1)}, f32[112,128]{1,0:T(8,128)S(1)}, u32[]{:S(2)}, u32[]{:S(2)}) collective-permute-start(f32[112,128]{1,0:T(8,128)S(1)} %pad_add_fusion.refs_1_), channel_id=1, source_target_pairs={{0,4},{1,5},{2,6},{3,7},{4,0},{5,1},{6,2},{7,3},{8,12},{9,13},{10,... | collective-permute-start | bytes 172040 | tf_op jit(solution)/shard_map/ppermute | solution.py:207
  37.1 0.9 %collective-permute-done.10.refs_2_ = f32[112,128]{1,0:T(8,128)S(1)} collective-permute-done((f32[112,128]{1,0:T(8,128)S(1)}, f32[112,128]{1,0:T(8,128)S(1)}, u32[]{:S(2)}, u32[]{:S(2)}) %collective-permute-start.10) | collective-permute-done | bytes 57376 | tf_op jit(solution)/shard_map/ppermute | solution.py:207
  38.0 9.3 %factor.1 = (f32[128,4096]{1,0:T(8,128)}, f32[64,4096]{1,0:T(8,128)}, f32[128,128]{1,0:T(8,128)}, f32[64,128]{1,0:T(8,128)}) custom-call(s32[1]{0:T(128)} %bitcast.core_ref.refs_0_, f32[112,128]{1,0:T(8,128)S(1)} %pad_add_fusion.refs_1_, f32[112,128]{1,0:T(8,128)S(1)} %collective-permute-done.10.refs_2_, f32[128,4096]{1,0:T(8,128)} %refs_3_.1, ...), custom_call_target="tpu_custom_call" | custom-call | tf_op jit(solution)/shard_map/factor/pallas_call | solution.py:385
  (14 shorter events, 0.2 us)
Async XLA Ops:
  4.9 2.4 %collective-permute-start = (f32[112,128]{1,0:T(8,128)S(1)}, f32[112,128]{1,0:T(8,128)S(1)}, u32[]{:S(2)}, u32[]{:S(2)}) collective-permute-start(f32[112,128]{1,0:T(8,128)S(1)} %get-tuple-element.11), channel_id=1, source_target_pairs={{0,4},{1,5},{2,6},{3,7},{4,0},{5,1},{6,2},{7,3},{8,12},{9,13},{10,... | collective-permute-start | bytes 172040 | tf_op jit(solution)/shard_map/ppermute | solution.py:207
  7.4 4.1 %collective-permute-start.1 = (f32[112,128]{1,0:T(8,128)S(1)}, f32[112,128]{1,0:T(8,128)S(1)}, u32[]{:S(2)}, u32[]{:S(2)}) collective-permute-start(f32[112,128]{1,0:T(8,128)S(1)} %pad_add_fusion.3), channel_id=1, source_target_pairs={{0,1},{1,0},{2,3},{3,2},{4,5},{5,4},{6,7},{7,6},{8,9},{9,8},{10,11... | collective-permute-start | bytes 172040 | tf_op jit(solution)/shard_map/ppermute | solution.py:207
  8.8 4.2 %collective-permute-start.3 = (f32[112,128]{1,0:T(8,128)S(1)}, f32[112,128]{1,0:T(8,128)S(1)}, u32[]{:S(2)}, u32[]{:S(2)}) collective-permute-start(f32[112,128]{1,0:T(8,128)S(1)} %pad_add_fusion.3), channel_id=1, source_target_pairs={{0,3},{1,2},{2,1},{3,0},{4,7},{5,6},{6,5},{7,4},{8,11},{9,10},{10,... | collective-permute-start | bytes 172040 | tf_op jit(solution)/shard_map/ppermute | solution.py:207
  10.7 4.5 %collective-permute-start.2 = (f32[112,128]{1,0:T(8,128)S(1)}, f32[112,128]{1,0:T(8,128)S(1)}, u32[]{:S(2)}, u32[]{:S(2)}) collective-permute-start(f32[112,128]{1,0:T(8,128)S(1)} %pad_add_fusion.3), channel_id=1, source_target_pairs={{0,2},{1,3},{2,0},{3,1},{4,6},{5,7},{6,4},{7,5},{8,10},{9,11},{10,... | collective-permute-start | bytes 172040 | tf_op jit(solution)/shard_map/ppermute | solution.py:207
  15.3 3.7 %collective-permute-start.4 = (f32[112,128]{1,0:T(8,128)S(1)}, f32[112,128]{1,0:T(8,128)S(1)}, u32[]{:S(2)}, u32[]{:S(2)}) collective-permute-start(f32[112,128]{1,0:T(8,128)S(1)} %pad_add_fusion.2), channel_id=1, source_target_pairs={{0,8},{1,9},{2,10},{3,11},{4,12},{5,13},{6,14},{7,15},{8,0},{9,1},... | collective-permute-start | bytes 172040 | tf_op jit(solution)/shard_map/ppermute | solution.py:207
  16.6 4.2 %collective-permute-start.6 = (f32[112,128]{1,0:T(8,128)S(1)}, f32[112,128]{1,0:T(8,128)S(1)}, u32[]{:S(2)}, u32[]{:S(2)}) collective-permute-start(f32[112,128]{1,0:T(8,128)S(1)} %pad_add_fusion.2), channel_id=1, source_target_pairs={{0,72},{1,73},{2,74},{3,75},{4,76},{5,77},{6,78},{7,79},{8,64},{9,... | collective-permute-start | bytes 172040 | tf_op jit(solution)/shard_map/ppermute | solution.py:207
  18.4 5.0 %collective-permute-start.5 = (f32[112,128]{1,0:T(8,128)S(1)}, f32[112,128]{1,0:T(8,128)S(1)}, u32[]{:S(2)}, u32[]{:S(2)}) collective-permute-start(f32[112,128]{1,0:T(8,128)S(1)} %pad_add_fusion.2), channel_id=1, source_target_pairs={{0,64},{1,65},{2,66},{3,67},{4,68},{5,69},{6,70},{7,71},{8,72},{9,... | collective-permute-start | bytes 172040 | tf_op jit(solution)/shard_map/ppermute | solution.py:207
  23.4 5.0 %collective-permute-start.7 = (f32[112,128]{1,0:T(8,128)S(1)}, f32[112,128]{1,0:T(8,128)S(1)}, u32[]{:S(2)}, u32[]{:S(2)}) collective-permute-start(f32[112,128]{1,0:T(8,128)S(1)} %pad_add_fusion.1), channel_id=1, source_target_pairs={{0,16},{1,17},{2,18},{3,19},{4,20},{5,21},{6,22},{7,23},{8,24},{9,... | collective-permute-start | bytes 172040 | tf_op jit(solution)/shard_map/ppermute | solution.py:207
  25.1 4.2 %collective-permute-start.9 = (f32[112,128]{1,0:T(8,128)S(1)}, f32[112,128]{1,0:T(8,128)S(1)}, u32[]{:S(2)}, u32[]{:S(2)}) collective-permute-start(f32[112,128]{1,0:T(8,128)S(1)} %pad_add_fusion.1), channel_id=1, source_target_pairs={{0,48},{1,49},{2,50},{3,51},{4,52},{5,53},{6,54},{7,55},{8,56},{9,... | collective-permute-start | bytes 172040 | tf_op jit(solution)/shard_map/ppermute | solution.py:207
  27.4 4.5 %collective-permute-start.8 = (f32[112,128]{1,0:T(8,128)S(1)}, f32[112,128]{1,0:T(8,128)S(1)}, u32[]{:S(2)}, u32[]{:S(2)}) collective-permute-start(f32[112,128]{1,0:T(8,128)S(1)} %pad_add_fusion.1), channel_id=1, source_target_pairs={{0,32},{1,33},{2,34},{3,35},{4,36},{5,37},{6,38},{7,39},{8,40},{9,... | collective-permute-start | bytes 172040 | tf_op jit(solution)/shard_map/ppermute | solution.py:207
  32.0 6.0 %collective-permute-start.10 = (f32[112,128]{1,0:T(8,128)S(1)}, f32[112,128]{1,0:T(8,128)S(1)}, u32[]{:S(2)}, u32[]{:S(2)}) collective-permute-start(f32[112,128]{1,0:T(8,128)S(1)} %pad_add_fusion.refs_1_), channel_id=1, source_target_pairs={{0,4},{1,5},{2,6},{3,7},{4,0},{5,1},{6,2},{7,3},{8,12},{9,13},{10,... | collective-permute-start | bytes 172040 | tf_op jit(solution)/shard_map/ppermute | solution.py:207

commit v4 on v3

--- a/solution.py
+++ b/solution.py
@@ -420,7 +420,7 @@
     total = add_packed(words, keep, exchange(send, 4))
     for masks in ((1, 3, 2), (8, 72, 64), (16, 48, 32)):
         near, wrap, far = (exchange(total, m) for m in masks)
-        total = add_packed(words, total, near, far, wrap)
+        total = add_packed(words, total, wrap, near, far)
     other = exchange(total, 4)
     basis_t, updated, upper, coupling_t = factor(core, total, other, panel, trailing, rows_all)
     return basis_t, upper, coupling_t.T, updated

time: 47.6 us -> 45.8 us (0.962)
  starting transfers between devices: 19.5 us -> 17.6 us
    ppermute x11, starting transfers between devices: 19.5 us -> 17.6 us  [exchange(): return lax.ppermute(value, AXES, [(s, s ^ mask) for s in range(size)])]
where the time goes in v4:
time: 45.8 us; the launch traced here: 45.7 us
  starting transfers between devices  17.6 us (38%)
  Pallas kernels  13.6 us (30%)
  waiting for transfers between devices  13.4 us (29%)
  between operations  0.88 us (2%)
    ppermute x11, starting transfers between devices, exchange(): return lax.ppermute(value, AXES, [(s, s ^ mask) for s in range(size)])  17.6 us
    ppermute x11, waiting for transfers between devices, exchange(): return lax.ppermute(value, AXES, [(s, s ^ mask) for s in range(size)])  13.4 us
    pallas_call x1, Pallas kernels, factor(): pl.pallas_call(lambda *refs: factor_kernel(rows_all, *refs), in_specs=[pl...  9.35 us
    pallas_call x1, Pallas kernels, local_gram(): pl.pallas_call(gram_kernel, in_specs=[pl.BlockSpec(memory_space=pltpu.SME...  4.28 us
  transfers between devices with their start and end apart: 11, of which 8 were waited for; matrix products, arithmetic and copies ran while one was open for 0% of the time, Pallas kernels for 0%

profile of v4, /device:TPU:1, one launch (start us, length us, event | category | flops | bytes accessed | tf_op | source)
XLA Modules:
  0.0 45.7 jit_solution(18388044811931474286)
XLA Ops:
  0.6 4.3 %gram.1 = (f32[112,128]{1,0:T(8,128)S(1)}, f32[112,128]{1,0:T(8,128)S(1)}) custom-call(s32[1]{0:T(128)} %bitcast.core_ref.refs_0_, f32[128,4096]{1,0:T(8,128)} %refs_3_.1, f32[64,4096]{1,0:T(8,128)} %refs_4_.1), custom_call_target="tpu_custom_call" | custom-call | tf_op jit(solution)/shard_map/gram/pallas_call | solution.py:171
  4.9 1.5 %collective-permute-start = (f32[112,128]{1,0:T(8,128)S(1)}, f32[112,128]{1,0:T(8,128)S(1)}, u32[]{:S(2)}, u32[]{:S(2)}) collective-permute-start(f32[112,128]{1,0:T(8,128)S(1)} %get-tuple-element.11), channel_id=1, source_target_pairs={{0,4},{1,5},{2,6},{3,7},{4,0},{5,1},{6,2},{7,3},{8,12},{9,13},{10,... | collective-permute-start | bytes 172040 | tf_op jit(solution)/shard_map/ppermute | solution.py:207
  6.4 0.9 %collective-permute-done = f32[112,128]{1,0:T(8,128)S(1)} collective-permute-done((f32[112,128]{1,0:T(8,128)S(1)}, f32[112,128]{1,0:T(8,128)S(1)}, u32[]{:S(2)}, u32[]{:S(2)}) %collective-permute-start) | collective-permute-done | bytes 57376 | tf_op jit(solution)/shard_map/ppermute | solution.py:207
  7.4 2.9 %collective-permute-start.1 = (f32[112,128]{1,0:T(8,128)S(1)}, f32[112,128]{1,0:T(8,128)S(1)}, u32[]{:S(2)}, u32[]{:S(2)}) collective-permute-start(f32[112,128]{1,0:T(8,128)S(1)} %pad_add_fusion.3), channel_id=1, source_target_pairs={{0,3},{1,2},{2,1},{3,0},{4,7},{5,6},{6,5},{7,4},{8,11},{9,10},{10,... | collective-permute-start | bytes 172040 | tf_op jit(solution)/shard_map/ppermute | solution.py:207
  10.2 0.4 collective-permute-start.3
  10.6 0.3 collective-permute-start.2
  10.9 0.9 %collective-permute-done.1 = f32[112,128]{1,0:T(8,128)S(1)} collective-permute-done((f32[112,128]{1,0:T(8,128)S(1)}, f32[112,128]{1,0:T(8,128)S(1)}, u32[]{:S(2)}, u32[]{:S(2)}) %collective-permute-start.1) | collective-permute-done | bytes 57376 | tf_op jit(solution)/shard_map/ppermute | solution.py:207
  11.8 3.0 %collective-permute-done.3 = f32[112,128]{1,0:T(8,128)S(1)} collective-permute-done((f32[112,128]{1,0:T(8,128)S(1)}, f32[112,128]{1,0:T(8,128)S(1)}, u32[]{:S(2)}, u32[]{:S(2)}) %collective-permute-start.3) | collective-permute-done | bytes 57376 | tf_op jit(solution)/shard_map/ppermute | solution.py:207
  14.8 0.0 collective-permute-done.2
  14.8 2.6 %collective-permute-start.4 = (f32[112,128]{1,0:T(8,128)S(1)}, f32[112,128]{1,0:T(8,128)S(1)}, u32[]{:S(2)}, u32[]{:S(2)}) collective-permute-start(f32[112,128]{1,0:T(8,128)S(1)} %pad_add_fusion.2), channel_id=1, source_target_pairs={{0,72},{1,73},{2,74},{3,75},{4,76},{5,77},{6,78},{7,79},{8,64},{9,... | collective-permute-start | bytes 172040 | tf_op jit(solution)/shard_map/ppermute | solution.py:207
  17.4 0.5 %collective-permute-start.6 = (f32[112,128]{1,0:T(8,128)S(1)}, f32[112,128]{1,0:T(8,128)S(1)}, u32[]{:S(2)}, u32[]{:S(2)}) collective-permute-start(f32[112,128]{1,0:T(8,128)S(1)} %pad_add_fusion.2), channel_id=1, source_target_pairs={{0,64},{1,65},{2,66},{3,67},{4,68},{5,69},{6,70},{7,71},{8,72},{9,... | collective-permute-start | bytes 172040 | tf_op jit(solution)/shard_map/ppermute | solution.py:207
  17.9 0.2 collective-permute-start.5
  18.2 1.0 %collective-permute-done.4 = f32[112,128]{1,0:T(8,128)S(1)} collective-permute-done((f32[112,128]{1,0:T(8,128)S(1)}, f32[112,128]{1,0:T(8,128)S(1)}, u32[]{:S(2)}, u32[]{:S(2)}) %collective-permute-start.4) | collective-permute-done | bytes 57376 | tf_op jit(solution)/shard_map/ppermute | solution.py:207
  19.2 2.9 %collective-permute-done.6 = f32[112,128]{1,0:T(8,128)S(1)} collective-permute-done((f32[112,128]{1,0:T(8,128)S(1)}, f32[112,128]{1,0:T(8,128)S(1)}, u32[]{:S(2)}, u32[]{:S(2)}) %collective-permute-start.6) | collective-permute-done | bytes 57376 | tf_op jit(solution)/shard_map/ppermute | solution.py:207
  22.0 0.0 collective-permute-done.5
  22.1 3.8 %collective-permute-start.7 = (f32[112,128]{1,0:T(8,128)S(1)}, f32[112,128]{1,0:T(8,128)S(1)}, u32[]{:S(2)}, u32[]{:S(2)}) collective-permute-start(f32[112,128]{1,0:T(8,128)S(1)} %pad_add_fusion.1), channel_id=1, source_target_pairs={{0,48},{1,49},{2,50},{3,51},{4,52},{5,53},{6,54},{7,55},{8,56},{9,... | collective-permute-start | bytes 172040 | tf_op jit(solution)/shard_map/ppermute | solution.py:207
  25.9 0.0 collective-permute-start.9
  25.9 0.7 %collective-permute-start.8 = (f32[112,128]{1,0:T(8,128)S(1)}, f32[112,128]{1,0:T(8,128)S(1)}, u32[]{:S(2)}, u32[]{:S(2)}) collective-permute-start(f32[112,128]{1,0:T(8,128)S(1)} %pad_add_fusion.1), channel_id=1, source_target_pairs={{0,16},{1,17},{2,18},{3,19},{4,20},{5,21},{6,22},{7,23},{8,24},{9,... | collective-permute-start | bytes 172040 | tf_op jit(solution)/shard_map/ppermute | solution.py:207
  26.6 0.9 %collective-permute-done.7 = f32[112,128]{1,0:T(8,128)S(1)} collective-permute-done((f32[112,128]{1,0:T(8,128)S(1)}, f32[112,128]{1,0:T(8,128)S(1)}, u32[]{:S(2)}, u32[]{:S(2)}) %collective-permute-start.7) | collective-permute-done | bytes 57376 | tf_op jit(solution)/shard_map/ppermute | solution.py:207
  27.5 3.0 %collective-permute-done.9 = f32[112,128]{1,0:T(8,128)S(1)} collective-permute-done((f32[112,128]{1,0:T(8,128)S(1)}, f32[112,128]{1,0:T(8,128)S(1)}, u32[]{:S(2)}, u32[]{:S(2)}) %collective-permute-start.9) | collective-permute-done | bytes 57376 | tf_op jit(solution)/shard_map/ppermute | solution.py:207
  30.5 0.0 collective-permute-done.8
  30.6 4.7 %collective-permute-start.10 = (f32[112,128]{1,0:T(8,128)S(1)}, f32[112,128]{1,0:T(8,128)S(1)}, u32[]{:S(2)}, u32[]{:S(2)}) collective-permute-start(f32[112,128]{1,0:T(8,128)S(1)} %pad_add_fusion.refs_1_), channel_id=1, source_target_pairs={{0,4},{1,5},{2,6},{3,7},{4,0},{5,1},{6,2},{7,3},{8,12},{9,13},{10,... | collective-permute-start | bytes 172040 | tf_op jit(solution)/shard_map/ppermute | solution.py:207
  35.3 0.9 %collective-permute-done.10.refs_2_ = f32[112,128]{1,0:T(8,128)S(1)} collective-permute-done((f32[112,128]{1,0:T(8,128)S(1)}, f32[112,128]{1,0:T(8,128)S(1)}, u32[]{:S(2)}, u32[]{:S(2)}) %collective-permute-start.10) | collective-permute-done | bytes 57376 | tf_op jit(solution)/shard_map/ppermute | solution.py:207
  36.2 9.3 %factor.1 = (f32[128,4096]{1,0:T(8,128)}, f32[64,4096]{1,0:T(8,128)}, f32[128,128]{1,0:T(8,128)}, f32[64,128]{1,0:T(8,128)}) custom-call(s32[1]{0:T(128)} %bitcast.core_ref.refs_0_, f32[112,128]{1,0:T(8,128)S(1)} %pad_add_fusion.refs_1_, f32[112,128]{1,0:T(8,128)S(1)} %collective-permute-done.10.refs_2_, f32[128,4096]{1,0:T(8,128)} %refs_3_.1, ...), custom_call_target="tpu_custom_call" | custom-call | tf_op jit(solution)/shard_map/factor/pallas_call | solution.py:385
  (14 shorter events, 0.2 us)
Async XLA Ops:
  4.9 2.4 %collective-permute-start = (f32[112,128]{1,0:T(8,128)S(1)}, f32[112,128]{1,0:T(8,128)S(1)}, u32[]{:S(2)}, u32[]{:S(2)}) collective-permute-start(f32[112,128]{1,0:T(8,128)S(1)} %get-tuple-element.11), channel_id=1, source_target_pairs={{0,4},{1,5},{2,6},{3,7},{4,0},{5,1},{6,2},{7,3},{8,12},{9,13},{10,... | collective-permute-start | bytes 172040 | tf_op jit(solution)/shard_map/ppermute | solution.py:207
  7.4 4.5 %collective-permute-start.1 = (f32[112,128]{1,0:T(8,128)S(1)}, f32[112,128]{1,0:T(8,128)S(1)}, u32[]{:S(2)}, u32[]{:S(2)}) collective-permute-start(f32[112,128]{1,0:T(8,128)S(1)} %pad_add_fusion.3), channel_id=1, source_target_pairs={{0,3},{1,2},{2,1},{3,0},{4,7},{5,6},{6,5},{7,4},{8,11},{9,10},{10,... | collective-permute-start | bytes 172040 | tf_op jit(solution)/shard_map/ppermute | solution.py:207
  10.2 4.5 %collective-permute-start.3 = (f32[112,128]{1,0:T(8,128)S(1)}, f32[112,128]{1,0:T(8,128)S(1)}, u32[]{:S(2)}, u32[]{:S(2)}) collective-permute-start(f32[112,128]{1,0:T(8,128)S(1)} %pad_add_fusion.3), channel_id=1, source_target_pairs={{0,2},{1,3},{2,0},{3,1},{4,6},{5,7},{6,4},{7,5},{8,10},{9,11},{10,... | collective-permute-start | bytes 172040 | tf_op jit(solution)/shard_map/ppermute | solution.py:207
  10.6 4.2 %collective-permute-start.2 = (f32[112,128]{1,0:T(8,128)S(1)}, f32[112,128]{1,0:T(8,128)S(1)}, u32[]{:S(2)}, u32[]{:S(2)}) collective-permute-start(f32[112,128]{1,0:T(8,128)S(1)} %pad_add_fusion.3), channel_id=1, source_target_pairs={{0,1},{1,0},{2,3},{3,2},{4,5},{5,4},{6,7},{7,6},{8,9},{9,8},{10,11... | collective-permute-start | bytes 172040 | tf_op jit(solution)/shard_map/ppermute | solution.py:207
  14.8 4.3 %collective-permute-start.4 = (f32[112,128]{1,0:T(8,128)S(1)}, f32[112,128]{1,0:T(8,128)S(1)}, u32[]{:S(2)}, u32[]{:S(2)}) collective-permute-start(f32[112,128]{1,0:T(8,128)S(1)} %pad_add_fusion.2), channel_id=1, source_target_pairs={{0,72},{1,73},{2,74},{3,75},{4,76},{5,77},{6,78},{7,79},{8,64},{9,... | collective-permute-start | bytes 172040 | tf_op jit(solution)/shard_map/ppermute | solution.py:207
  17.4 4.6 %collective-permute-start.6 = (f32[112,128]{1,0:T(8,128)S(1)}, f32[112,128]{1,0:T(8,128)S(1)}, u32[]{:S(2)}, u32[]{:S(2)}) collective-permute-start(f32[112,128]{1,0:T(8,128)S(1)} %pad_add_fusion.2), channel_id=1, source_target_pairs={{0,64},{1,65},{2,66},{3,67},{4,68},{5,69},{6,70},{7,71},{8,72},{9,... | collective-permute-start | bytes 172040 | tf_op jit(solution)/shard_map/ppermute | solution.py:207
  17.9 4.1 %collective-permute-start.5 = (f32[112,128]{1,0:T(8,128)S(1)}, f32[112,128]{1,0:T(8,128)S(1)}, u32[]{:S(2)}, u32[]{:S(2)}) collective-permute-start(f32[112,128]{1,0:T(8,128)S(1)} %pad_add_fusion.2), channel_id=1, source_target_pairs={{0,8},{1,9},{2,10},{3,11},{4,12},{5,13},{6,14},{7,15},{8,0},{9,1},... | collective-permute-start | bytes 172040 | tf_op jit(solution)/shard_map/ppermute | solution.py:207
  22.1 5.4 %collective-permute-start.7 = (f32[112,128]{1,0:T(8,128)S(1)}, f32[112,128]{1,0:T(8,128)S(1)}, u32[]{:S(2)}, u32[]{:S(2)}) collective-permute-start(f32[112,128]{1,0:T(8,128)S(1)} %pad_add_fusion.1), channel_id=1, source_target_pairs={{0,48},{1,49},{2,50},{3,51},{4,52},{5,53},{6,54},{7,55},{8,56},{9,... | collective-permute-start | bytes 172040 | tf_op jit(solution)/shard_map/ppermute | solution.py:207
  25.9 4.5 %collective-permute-start.9 = (f32[112,128]{1,0:T(8,128)S(1)}, f32[112,128]{1,0:T(8,128)S(1)}, u32[]{:S(2)}, u32[]{:S(2)}) collective-permute-start(f32[112,128]{1,0:T(8,128)S(1)} %pad_add_fusion.1), channel_id=1, source_target_pairs={{0,32},{1,33},{2,34},{3,35},{4,36},{5,37},{6,38},{7,39},{8,40},{9,... | collective-permute-start | bytes 172040 | tf_op jit(solution)/shard_map/ppermute | solution.py:207
  25.9 4.5 %collective-permute-start.8 = (f32[112,128]{1,0:T(8,128)S(1)}, f32[112,128]{1,0:T(8,128)S(1)}, u32[]{:S(2)}, u32[]{:S(2)}) collective-permute-start(f32[112,128]{1,0:T(8,128)S(1)} %pad_add_fusion.1), channel_id=1, source_target_pairs={{0,16},{1,17},{2,18},{3,19},{4,20},{5,21},{6,22},{7,23},{8,24},{9,... | collective-permute-start | bytes 172040 | tf_op jit(solution)/shard_map/ppermute | solution.py:207
  30.6 5.6 %collective-permute-start.10 = (f32[112,128]{1,0:T(8,128)S(1)}, f32[112,128]{1,0:T(8,128)S(1)}, u32[]{:S(2)}, u32[]{:S(2)}) collective-permute-start(f32[112,128]{1,0:T(8,128)S(1)} %pad_add_fusion.refs_1_), channel_id=1, source_target_pairs={{0,4},{1,5},{2,6},{3,7},{4,0},{5,1},{6,2},{7,3},{8,12},{9,13},{10,... | collective-permute-start | bytes 172040 | tf_op jit(solution)/shard_map/ppermute | solution.py:207

commit v5 on v4

--- a/solution.py
+++ b/solution.py
@@ -11,7 +11,7 @@
 BF16 = jnp.bfloat16
 CHUNK = 2048
 OUT_CHUNK = 512
-PANEL_COLS = 8
+NEAR = 4
 SMALL = 4e-3
 MAGIC = 1.5 * 2.0**23
 
@@ -27,12 +27,12 @@
 
 
 def snap(x):
-    c = x * 4097.0
+    c = x * (2.0**23 + 1.0)
     return c - (c - x)
 
 
-def power_below(x):
-    p = snap(jnp.exp2(jnp.floor(jnp.log2(jnp.maximum(x, 1e-30)))))
+def power_near(x):
+    p = snap(jnp.maximum(x, 1e-30))
     return p, snap(1.0 / p)
 
 
@@ -81,7 +81,7 @@
     def split(k):
         copies[k][0].wait()
         x = pbuf[k]
-        p, inv = power_below(jnp.max(jnp.abs(x), axis=1, keepdims=True))
+        p, inv = power_near(jnp.max(jnp.abs(x), axis=1, keepdims=True))
         a = x * (inv * 32.0)
         d1 = round_int(a)
         r1 = (a - d1) * 256.0
@@ -207,42 +207,79 @@
     return lax.ppermute(value, AXES, [(s, s ^ mask) for s in range(size)])
 
 
-def chol_inv(s):
-    blocks = len(s)
-    n = 8 * blocks
-    rid, lid = iota((8, n), 0), iota((8, n), 1)
-    w = [jnp.where(lid == rid + 8 * r, 1.0, 0.0) for r in range(blocks)]
-    s = list(s)
-    for first in range(0, n, PANEL_COLS):
-        r0 = first // 8
-        cols = [
-            [jnp.broadcast_to(s[r][:, first + k : first + k + 1], (8, n)) for r in range(r0, blocks)]
-            for k in range(PANEL_COLS)
-        ]
-        scales = []
-        for k in range(PANEL_COLS):
-            pivot = cols[k][0][k : k + 1, :]
-            inv = 1.0 / pivot
-            mult = [c * inv for c in cols[k]]
-            mult[0] = jnp.where(rid > k, mult[0], 0.0)
-            for later in range(k + 1, PANEL_COLS):
-                e = cols[later][0][k : k + 1, :]
-                cols[later] = [c - m * e for c, m in zip(cols[later], mult)]
-            srow, wrow = s[r0][k : k + 1, :], w[r0][k : k + 1, :]
-            for i, m in enumerate(mult):
-                s[r0 + i] = s[r0 + i] - m * srow
-                w[r0 + i] = w[r0 + i] - m * wrow
-            scales.append(lax.rsqrt(pivot))
-        for k, d in enumerate(scales):
-            w[r0] = jnp.where(rid == k, w[r0] * d, w[r0])
-    return w
-
-
 def split3(x):
     x1 = x.astype(BF16)
     rest = x - x1.astype(F32)
     x2 = rest.astype(BF16)
     return x1, x2, (rest - x2.astype(F32)).astype(BF16)
+
+
+def chol_inv(s):
+    blocks = len(s)
+    n = 8 * blocks
+    rid, lid = iota((8, n), 0), iota((8, n), 1)
+    s, w = list(s), [jnp.where(lid == rid + 8 * r, 1.0, 0.0) for r in range(blocks)]
+
+    def spread(r, first):
+        return [jnp.broadcast_to(s[r][:, first + k : first + k + 1], (8, n)) for k in range(8)]
+
+    cols = {r: spread(r, 0) for r in (0, 1)}
+    for r0 in range(blocks):
+        first = 8 * r0
+        near = range(r0, min(r0 + 3, blocks))
+        for r in near:
+            if r not in cols:
+                cols[r] = spread(r, first)
+        ahead = {r: spread(r, first + 8) for r in near if r > r0}
+        edges, invs, srows, wrows, scales = {}, [], [], [], []
+        inv_rows = jnp.zeros((8, n), F32)
+        for k in range(8):
+            pivot = cols[r0][k][k : k + 1, :]
+            inv = 1.0 / pivot
+            mult = {r: cols[r][k] * inv for r in near}
+            mult[r0] = jnp.where(rid > k, mult[r0], 0.0)
+            for later in range(k + 1, 8):
+                edges[k, later] = edge = cols[r0][later][k : k + 1, :]
+                for r in near:
+                    cols[r][later] = cols[r][later] - mult[r] * edge
+            if ahead:
+                for q in range(8):
+                    edge = cols[r0 + 1][k][q : q + 1, :]
+                    for r in ahead:
+                        ahead[r][q] = ahead[r][q] - mult[r] * edge
+            srow, wrow = s[r0][k : k + 1, :], w[r0][k : k + 1, :]
+            for r in near:
+                s[r] = s[r] - mult[r] * srow
+                w[r] = w[r] - mult[r] * wrow
+            inv_rows = jnp.where(rid == k, inv, inv_rows)
+            invs.append(inv)
+            srows.append(srow)
+            wrows.append(wrow)
+            scales.append(lax.rsqrt(pivot))
+        for r in range(r0 + 3, min(r0 + NEAR, blocks)):
+            col = spread(r, first)
+            for k in range(8):
+                mult = col[k] * invs[k]
+                for later in range(k + 1, 8):
+                    col[later] = col[later] - mult * edges[k, later]
+                s[r] = s[r] - mult * srows[k]
+                w[r] = w[r] - mult * wrows[k]
+        if r0 + NEAR < blocks:
+            l1, l2, l3 = split3(s[r0] * inv_rows)
+            r1, r2, r3 = split3(jnp.concatenate([s[r0], w[r0]], axis=1))
+
+            def stack(*parts):
+                return jnp.concatenate([p.astype(F32) for p in parts], axis=0).astype(BF16)
+
+            left, right = stack(l1, l2, l1, l2, l1, l3), stack(r1, r2, r2, r1, r3, r1)
+            update = lax.dot_general(left, right, (((0,), (0,)), ((), ())), preferred_element_type=F32)
+            for r in range(r0 + NEAR, blocks):
+                s[r] = s[r] - update[8 * r : 8 * r + 8, :n]
+                w[r] = w[r] - update[8 * r : 8 * r + 8, n:]
+        for k, d in enumerate(scales):
+            w[r0] = jnp.where(rid == k, w[r0] * d, w[r0])
+        cols = ahead
+    return w
 
 
 def apply_factors(wz, scale, panel, trailing, basis, updated, words, basis_buf, updated_buf, sems):
@@ -300,14 +337,14 @@
     g_hi, g_lo = two_sum(g_hi, g_lo)
 
     diag = jnp.sum(jnp.where(i == j, g_hi, 0.0), axis=0, keepdims=True)
-    pc, inv_pc = power_below(jnp.sqrt(diag))
+    pc, inv_pc = power_near(jnp.sqrt(diag))
     ic = jnp.broadcast_to(inv_pc, (n, n))
     eq = ic * ic.T
     s_hi, s_lo = g_hi * eq, g_lo * eq
 
     w = jnp.concatenate(chol_inv([s_hi[8 * r : 8 * r + 8, :] for r in range(n // 8)]), axis=0)
 
-    qr, inv_qr = power_below(jnp.max(jnp.abs(w), axis=1, keepdims=True))
+    qr, inv_qr = power_near(jnp.max(jnp.abs(w), axis=1, keepdims=True))
     wd = slices(w * (inv_qr * 64.0), None, 3)
     qs = qr * (1.0 / 64.0)
     wt = (wd[0] + wd[1] * 2.0**-8 + wd[2] * 2.0**-16) * qs
@@ -329,7 +366,7 @@
         return nn(wcat[:, 0:width], gcat[(5 - k) * n : (5 - k) * n + width, :])
 
     t_hi, t_lo = weigh([t_level(k) for k in range(6)])
-    tau, inv_tau = power_below(jnp.max(jnp.abs(t_hi), axis=1, keepdims=True))
+    tau, inv_tau = power_near(jnp.max(jnp.abs(t_hi), axis=1, keepdims=True))
     td = slices(t_hi * (inv_tau * 64.0), t_lo * (inv_tau * 64.0), 4)
     for k in range(4):
         tcat[:, (3 - k) * n : (4 - k) * n] = td[k].astype(BF16)

time: 45.8 us -> 44 us (0.961)
  Pallas kernels: 13.6 us -> 11.9 us
    pallas_call x1, Pallas kernels: 9.35 us -> 7.69 us  [factor(): pl.pallas_call(lambda *refs: factor_kernel(rows_all, *refs), in_specs=[pl...]
where the time goes in v5:
time: 44 us; the launch traced here: 43.9 us
  starting transfers between devices  17.7 us (40%)
  waiting for transfers between devices  13.3 us (30%)
  Pallas kernels  11.9 us (27%)
  between operations  0.72 us (2%)
    ppermute x11, starting transfers between devices, exchange(): return lax.ppermute(value, AXES, [(s, s ^ mask) for s in range(size)])  17.7 us
    ppermute x11, waiting for transfers between devices, exchange(): return lax.ppermute(value, AXES, [(s, s ^ mask) for s in range(size)])  13.3 us
    pallas_call x1, Pallas kernels, factor(): pl.pallas_call(lambda *refs: factor_kernel(rows_all, *refs), in_specs=[pl...  7.69 us
    pallas_call x1, Pallas kernels, local_gram(): pl.pallas_call(gram_kernel, in_specs=[pl.BlockSpec(memory_space=pltpu.SME...  4.25 us
  transfers between devices with their start and end apart: 11, of which 8 were waited for; matrix products, arithmetic and copies ran while one was open for 0% of the time, Pallas kernels for 0%

profile of v5, /device:TPU:1, one launch (start us, length us, event | category | flops | bytes accessed | tf_op | source)
XLA Modules:
  0.0 43.9 jit_solution(13050432485116016524)
XLA Ops:
  0.6 4.3 %gram.1 = (f32[112,128]{1,0:T(8,128)S(1)}, f32[112,128]{1,0:T(8,128)S(1)}) custom-call(s32[1]{0:T(128)} %bitcast.core_ref.refs_0_, f32[128,4096]{1,0:T(8,128)} %refs_3_.1, f32[64,4096]{1,0:T(8,128)} %refs_4_.1), custom_call_target="tpu_custom_call" | custom-call | tf_op jit(solution)/shard_map/gram/pallas_call | solution.py:171
  4.9 1.5 %collective-permute-start = (f32[112,128]{1,0:T(8,128)S(1)}, f32[112,128]{1,0:T(8,128)S(1)}, u32[]{:S(2)}, u32[]{:S(2)}) collective-permute-start(f32[112,128]{1,0:T(8,128)S(1)} %get-tuple-element.11), channel_id=1, source_target_pairs={{0,4},{1,5},{2,6},{3,7},{4,0},{5,1},{6,2},{7,3},{8,12},{9,13},{10,... | collective-permute-start | bytes 172040 | tf_op jit(solution)/shard_map/ppermute | solution.py:207
  6.4 0.9 %collective-permute-done = f32[112,128]{1,0:T(8,128)S(1)} collective-permute-done((f32[112,128]{1,0:T(8,128)S(1)}, f32[112,128]{1,0:T(8,128)S(1)}, u32[]{:S(2)}, u32[]{:S(2)}) %collective-permute-start) | collective-permute-done | bytes 57376 | tf_op jit(solution)/shard_map/ppermute | solution.py:207
  7.3 2.9 %collective-permute-start.1 = (f32[112,128]{1,0:T(8,128)S(1)}, f32[112,128]{1,0:T(8,128)S(1)}, u32[]{:S(2)}, u32[]{:S(2)}) collective-permute-start(f32[112,128]{1,0:T(8,128)S(1)} %pad_add_fusion.3), channel_id=1, source_target_pairs={{0,3},{1,2},{2,1},{3,0},{4,7},{5,6},{6,5},{7,4},{8,11},{9,10},{10,... | collective-permute-start | bytes 172040 | tf_op jit(solution)/shard_map/ppermute | solution.py:207
  10.2 0.3 collective-permute-start.3
  10.6 0.3 collective-permute-start.2
  10.9 0.9 %collective-permute-done.1 = f32[112,128]{1,0:T(8,128)S(1)} collective-permute-done((f32[112,128]{1,0:T(8,128)S(1)}, f32[112,128]{1,0:T(8,128)S(1)}, u32[]{:S(2)}, u32[]{:S(2)}) %collective-permute-start.1) | collective-permute-done | bytes 57376 | tf_op jit(solution)/shard_map/ppermute | solution.py:207
  11.8 3.0 %collective-permute-done.3 = f32[112,128]{1,0:T(8,128)S(1)} collective-permute-done((f32[112,128]{1,0:T(8,128)S(1)}, f32[112,128]{1,0:T(8,128)S(1)}, u32[]{:S(2)}, u32[]{:S(2)}) %collective-permute-start.3) | collective-permute-done | bytes 57376 | tf_op jit(solution)/shard_map/ppermute | solution.py:207
  14.8 0.0 collective-permute-done.2
  14.8 2.6 %collective-permute-start.4 = (f32[112,128]{1,0:T(8,128)S(1)}, f32[112,128]{1,0:T(8,128)S(1)}, u32[]{:S(2)}, u32[]{:S(2)}) collective-permute-start(f32[112,128]{1,0:T(8,128)S(1)} %pad_add_fusion.2), channel_id=1, source_target_pairs={{0,72},{1,73},{2,74},{3,75},{4,76},{5,77},{6,78},{7,79},{8,64},{9,... | collective-permute-start | bytes 172040 | tf_op jit(solution)/shard_map/ppermute | solution.py:207
  17.4 0.5 %collective-permute-start.6 = (f32[112,128]{1,0:T(8,128)S(1)}, f32[112,128]{1,0:T(8,128)S(1)}, u32[]{:S(2)}, u32[]{:S(2)}) collective-permute-start(f32[112,128]{1,0:T(8,128)S(1)} %pad_add_fusion.2), channel_id=1, source_target_pairs={{0,64},{1,65},{2,66},{3,67},{4,68},{5,69},{6,70},{7,71},{8,72},{9,... | collective-permute-start | bytes 172040 | tf_op jit(solution)/shard_map/ppermute | solution.py:207
  17.9 0.3 collective-permute-start.5
  18.2 1.0 %collective-permute-done.4 = f32[112,128]{1,0:T(8,128)S(1)} collective-permute-done((f32[112,128]{1,0:T(8,128)S(1)}, f32[112,128]{1,0:T(8,128)S(1)}, u32[]{:S(2)}, u32[]{:S(2)}) %collective-permute-start.4) | collective-permute-done | bytes 57376 | tf_op jit(solution)/shard_map/ppermute | solution.py:207
  19.1 2.9 %collective-permute-done.6 = f32[112,128]{1,0:T(8,128)S(1)} collective-permute-done((f32[112,128]{1,0:T(8,128)S(1)}, f32[112,128]{1,0:T(8,128)S(1)}, u32[]{:S(2)}, u32[]{:S(2)}) %collective-permute-start.6) | collective-permute-done | bytes 57376 | tf_op jit(solution)/shard_map/ppermute | solution.py:207
  22.0 0.0 collective-permute-done.5
  22.1 3.8 %collective-permute-start.7 = (f32[112,128]{1,0:T(8,128)S(1)}, f32[112,128]{1,0:T(8,128)S(1)}, u32[]{:S(2)}, u32[]{:S(2)}) collective-permute-start(f32[112,128]{1,0:T(8,128)S(1)} %pad_add_fusion.1), channel_id=1, source_target_pairs={{0,48},{1,49},{2,50},{3,51},{4,52},{5,53},{6,54},{7,55},{8,56},{9,... | collective-permute-start | bytes 172040 | tf_op jit(solution)/shard_map/ppermute | solution.py:207
  25.9 0.0 collective-permute-start.9
  25.9 0.7 %collective-permute-start.8 = (f32[112,128]{1,0:T(8,128)S(1)}, f32[112,128]{1,0:T(8,128)S(1)}, u32[]{:S(2)}, u32[]{:S(2)}) collective-permute-start(f32[112,128]{1,0:T(8,128)S(1)} %pad_add_fusion.1), channel_id=1, source_target_pairs={{0,16},{1,17},{2,18},{3,19},{4,20},{5,21},{6,22},{7,23},{8,24},{9,... | collective-permute-start | bytes 172040 | tf_op jit(solution)/shard_map/ppermute | solution.py:207
  26.6 0.9 %collective-permute-done.7 = f32[112,128]{1,0:T(8,128)S(1)} collective-permute-done((f32[112,128]{1,0:T(8,128)S(1)}, f32[112,128]{1,0:T(8,128)S(1)}, u32[]{:S(2)}, u32[]{:S(2)}) %collective-permute-start.7) | collective-permute-done | bytes 57376 | tf_op jit(solution)/shard_map/ppermute | solution.py:207
  27.5 3.0 %collective-permute-done.9 = f32[112,128]{1,0:T(8,128)S(1)} collective-permute-done((f32[112,128]{1,0:T(8,128)S(1)}, f32[112,128]{1,0:T(8,128)S(1)}, u32[]{:S(2)}, u32[]{:S(2)}) %collective-permute-start.9) | collective-permute-done | bytes 57376 | tf_op jit(solution)/shard_map/ppermute | solution.py:207
  30.5 0.0 collective-permute-done.8
  30.5 4.7 %collective-permute-start.10 = (f32[112,128]{1,0:T(8,128)S(1)}, f32[112,128]{1,0:T(8,128)S(1)}, u32[]{:S(2)}, u32[]{:S(2)}) collective-permute-start(f32[112,128]{1,0:T(8,128)S(1)} %pad_add_fusion.refs_1_), channel_id=1, source_target_pairs={{0,4},{1,5},{2,6},{3,7},{4,0},{5,1},{6,2},{7,3},{8,12},{9,13},{10,... | collective-permute-start | bytes 172040 | tf_op jit(solution)/shard_map/ppermute | solution.py:207
  35.3 0.9 %collective-permute-done.10.refs_2_ = f32[112,128]{1,0:T(8,128)S(1)} collective-permute-done((f32[112,128]{1,0:T(8,128)S(1)}, f32[112,128]{1,0:T(8,128)S(1)}, u32[]{:S(2)}, u32[]{:S(2)}) %collective-permute-start.10) | collective-permute-done | bytes 57376 | tf_op jit(solution)/shard_map/ppermute | solution.py:207
  36.2 7.7 %factor.1 = (f32[128,4096]{1,0:T(8,128)}, f32[64,4096]{1,0:T(8,128)}, f32[128,128]{1,0:T(8,128)}, f32[64,128]{1,0:T(8,128)}) custom-call(s32[1]{0:T(128)} %bitcast.core_ref.refs_0_, f32[112,128]{1,0:T(8,128)S(1)} %pad_add_fusion.refs_1_, f32[112,128]{1,0:T(8,128)S(1)} %collective-permute-done.10.refs_2_, f32[128,4096]{1,0:T(8,128)} %refs_3_.1, ...), custom_call_target="tpu_custom_call" | custom-call | tf_op jit(solution)/shard_map/factor/pallas_call | solution.py:422
  (14 shorter events, 0.2 us)
Async XLA Ops:
  4.9 2.4 %collective-permute-start = (f32[112,128]{1,0:T(8,128)S(1)}, f32[112,128]{1,0:T(8,128)S(1)}, u32[]{:S(2)}, u32[]{:S(2)}) collective-permute-start(f32[112,128]{1,0:T(8,128)S(1)} %get-tuple-element.11), channel_id=1, source_target_pairs={{0,4},{1,5},{2,6},{3,7},{4,0},{5,1},{6,2},{7,3},{8,12},{9,13},{10,... | collective-permute-start | bytes 172040 | tf_op jit(solution)/shard_map/ppermute | solution.py:207
  7.3 4.5 %collective-permute-start.1 = (f32[112,128]{1,0:T(8,128)S(1)}, f32[112,128]{1,0:T(8,128)S(1)}, u32[]{:S(2)}, u32[]{:S(2)}) collective-permute-start(f32[112,128]{1,0:T(8,128)S(1)} %pad_add_fusion.3), channel_id=1, source_target_pairs={{0,3},{1,2},{2,1},{3,0},{4,7},{5,6},{6,5},{7,4},{8,11},{9,10},{10,... | collective-permute-start | bytes 172040 | tf_op jit(solution)/shard_map/ppermute | solution.py:207
  10.2 4.5 %collective-permute-start.3 = (f32[112,128]{1,0:T(8,128)S(1)}, f32[112,128]{1,0:T(8,128)S(1)}, u32[]{:S(2)}, u32[]{:S(2)}) collective-permute-start(f32[112,128]{1,0:T(8,128)S(1)} %pad_add_fusion.3), channel_id=1, source_target_pairs={{0,2},{1,3},{2,0},{3,1},{4,6},{5,7},{6,4},{7,5},{8,10},{9,11},{10,... | collective-permute-start | bytes 172040 | tf_op jit(solution)/shard_map/ppermute | solution.py:207
  10.6 4.2 %collective-permute-start.2 = (f32[112,128]{1,0:T(8,128)S(1)}, f32[112,128]{1,0:T(8,128)S(1)}, u32[]{:S(2)}, u32[]{:S(2)}) collective-permute-start(f32[112,128]{1,0:T(8,128)S(1)} %pad_add_fusion.3), channel_id=1, source_target_pairs={{0,1},{1,0},{2,3},{3,2},{4,5},{5,4},{6,7},{7,6},{8,9},{9,8},{10,11... | collective-permute-start | bytes 172040 | tf_op jit(solution)/shard_map/ppermute | solution.py:207
  14.8 4.3 %collective-permute-start.4 = (f32[112,128]{1,0:T(8,128)S(1)}, f32[112,128]{1,0:T(8,128)S(1)}, u32[]{:S(2)}, u32[]{:S(2)}) collective-permute-start(f32[112,128]{1,0:T(8,128)S(1)} %pad_add_fusion.2), channel_id=1, source_target_pairs={{0,72},{1,73},{2,74},{3,75},{4,76},{5,77},{6,78},{7,79},{8,64},{9,... | collective-permute-start | bytes 172040 | tf_op jit(solution)/shard_map/ppermute | solution.py:207
  17.4 4.6 %collective-permute-start.6 = (f32[112,128]{1,0:T(8,128)S(1)}, f32[112,128]{1,0:T(8,128)S(1)}, u32[]{:S(2)}, u32[]{:S(2)}) collective-permute-start(f32[112,128]{1,0:T(8,128)S(1)} %pad_add_fusion.2), channel_id=1, source_target_pairs={{0,64},{1,65},{2,66},{3,67},{4,68},{5,69},{6,70},{7,71},{8,72},{9,... | collective-permute-start | bytes 172040 | tf_op jit(solution)/shard_map/ppermute | solution.py:207
  17.9 4.1 %collective-permute-start.5 = (f32[112,128]{1,0:T(8,128)S(1)}, f32[112,128]{1,0:T(8,128)S(1)}, u32[]{:S(2)}, u32[]{:S(2)}) collective-permute-start(f32[112,128]{1,0:T(8,128)S(1)} %pad_add_fusion.2), channel_id=1, source_target_pairs={{0,8},{1,9},{2,10},{3,11},{4,12},{5,13},{6,14},{7,15},{8,0},{9,1},... | collective-permute-start | bytes 172040 | tf_op jit(solution)/shard_map/ppermute | solution.py:207
  22.1 5.4 %collective-permute-start.7 = (f32[112,128]{1,0:T(8,128)S(1)}, f32[112,128]{1,0:T(8,128)S(1)}, u32[]{:S(2)}, u32[]{:S(2)}) collective-permute-start(f32[112,128]{1,0:T(8,128)S(1)} %pad_add_fusion.1), channel_id=1, source_target_pairs={{0,48},{1,49},{2,50},{3,51},{4,52},{5,53},{6,54},{7,55},{8,56},{9,... | collective-permute-start | bytes 172040 | tf_op jit(solution)/shard_map/ppermute | solution.py:207
  25.9 4.5 %collective-permute-start.9 = (f32[112,128]{1,0:T(8,128)S(1)}, f32[112,128]{1,0:T(8,128)S(1)}, u32[]{:S(2)}, u32[]{:S(2)}) collective-permute-start(f32[112,128]{1,0:T(8,128)S(1)} %pad_add_fusion.1), channel_id=1, source_target_pairs={{0,32},{1,33},{2,34},{3,35},{4,36},{5,37},{6,38},{7,39},{8,40},{9,... | collective-permute-start | bytes 172040 | tf_op jit(solution)/shard_map/ppermute | solution.py:207
  25.9 4.5 %collective-permute-start.8 = (f32[112,128]{1,0:T(8,128)S(1)}, f32[112,128]{1,0:T(8,128)S(1)}, u32[]{:S(2)}, u32[]{:S(2)}) collective-permute-start(f32[112,128]{1,0:T(8,128)S(1)} %pad_add_fusion.1), channel_id=1, source_target_pairs={{0,16},{1,17},{2,18},{3,19},{4,20},{5,21},{6,22},{7,23},{8,24},{9,... | collective-permute-start | bytes 172040 | tf_op jit(solution)/shard_map/ppermute | solution.py:207
  30.5 5.6 %collective-permute-start.10 = (f32[112,128]{1,0:T(8,128)S(1)}, f32[112,128]{1,0:T(8,128)S(1)}, u32[]{:S(2)}, u32[]{:S(2)}) collective-permute-start(f32[112,128]{1,0:T(8,128)S(1)} %pad_add_fusion.refs_1_), channel_id=1, source_target_pairs={{0,4},{1,5},{2,6},{3,7},{4,0},{5,1},{6,2},{7,3},{8,12},{9,13},{10,... | collective-permute-start | bytes 172040 | tf_op jit(solution)/shard_map/ppermute | solution.py:207

commit v6 on v5

--- a/solution.py
+++ b/solution.py
@@ -12,7 +12,7 @@
 CHUNK = 2048
 OUT_CHUNK = 512
 NEAR = 4
-SMALL = 4e-3
+SMALL = 2e-2
 MAGIC = 1.5 * 2.0**23
 
 
@@ -389,7 +389,12 @@
     @pl.when(size <= SMALL * SMALL)
     def _():
         fb = f.astype(BF16)
-        v_ref[...] = (jnp.where(i == j, 1.0, 0.0) - f) + (phi(nt(fb, fb)) + nn(fb, fb))
+        f2, square = -phi(nt(fb, fb)), nn(fb, fb)
+        f2b = f2.astype(BF16)
+        ab = jnp.concatenate([fb, f2b], axis=1)
+        ba = jnp.concatenate([f2b, fb], axis=1)
+        third = phi(nt(ab, ba)) + nn(ab, jnp.concatenate([(f2 - square).astype(BF16), fb], axis=0))
+        v_ref[...] = (jnp.where(i == j, 1.0, 0.0) - f) + ((square - f2) + third)
 
     @pl.when(jnp.logical_not(size <= SMALL * SMALL))
     def _():

time: 44 us -> 44.1 us (level)
  no operation moved by 1% of the time
where the time goes in v6:
time: 44.1 us; the launch traced here: 44 us
  starting transfers between devices  17.7 us (40%)
  waiting for transfers between devices  13.3 us (30%)
  Pallas kernels  12.1 us (27%)
  between operations  0.72 us (2%)
    ppermute x11, starting transfers between devices, exchange(): return lax.ppermute(value, AXES, [(s, s ^ mask) for s in range(size)])  17.7 us
    ppermute x11, waiting for transfers between devices, exchange(): return lax.ppermute(value, AXES, [(s, s ^ mask) for s in range(size)])  13.3 us
    pallas_call x1, Pallas kernels, factor(): pl.pallas_call(lambda *refs: factor_kernel(rows_all, *refs), in_specs=[pl...  7.88 us
    pallas_call x1, Pallas kernels, local_gram(): pl.pallas_call(gram_kernel, in_specs=[pl.BlockSpec(memory_space=pltpu.SME...  4.25 us
  transfers between devices with their start and end apart: 11, of which 8 were waited for; matrix products, arithmetic and copies ran while one was open for 0% of the time, Pallas kernels for 0%

profile of v6, /device:TPU:1, one launch (start us, length us, event | category | flops | bytes accessed | tf_op | source)
XLA Modules:
  0.0 44.0 jit_solution(10438428883864453428)
XLA Ops:
  0.6 4.3 %gram.1 = (f32[112,128]{1,0:T(8,128)S(1)}, f32[112,128]{1,0:T(8,128)S(1)}) custom-call(s32[1]{0:T(128)} %bitcast.core_ref.refs_0_, f32[128,4096]{1,0:T(8,128)} %refs_3_.1, f32[64,4096]{1,0:T(8,128)} %refs_4_.1), custom_call_target="tpu_custom_call" | custom-call | tf_op jit(solution)/shard_map/gram/pallas_call | solution.py:171
  4.9 1.5 %collective-permute-start = (f32[112,128]{1,0:T(8,128)S(1)}, f32[112,128]{1,0:T(8,128)S(1)}, u32[]{:S(2)}, u32[]{:S(2)}) collective-permute-start(f32[112,128]{1,0:T(8,128)S(1)} %get-tuple-element.11), channel_id=1, source_target_pairs={{0,4},{1,5},{2,6},{3,7},{4,0},{5,1},{6,2},{7,3},{8,12},{9,13},{10,... | collective-permute-start | bytes 172040 | tf_op jit(solution)/shard_map/ppermute | solution.py:207
  6.4 0.9 %collective-permute-done = f32[112,128]{1,0:T(8,128)S(1)} collective-permute-done((f32[112,128]{1,0:T(8,128)S(1)}, f32[112,128]{1,0:T(8,128)S(1)}, u32[]{:S(2)}, u32[]{:S(2)}) %collective-permute-start) | collective-permute-done | bytes 57376 | tf_op jit(solution)/shard_map/ppermute | solution.py:207
  7.3 2.9 %collective-permute-start.1 = (f32[112,128]{1,0:T(8,128)S(1)}, f32[112,128]{1,0:T(8,128)S(1)}, u32[]{:S(2)}, u32[]{:S(2)}) collective-permute-start(f32[112,128]{1,0:T(8,128)S(1)} %pad_add_fusion.3), channel_id=1, source_target_pairs={{0,3},{1,2},{2,1},{3,0},{4,7},{5,6},{6,5},{7,4},{8,11},{9,10},{10,... | collective-permute-start | bytes 172040 | tf_op jit(solution)/shard_map/ppermute | solution.py:207
  10.2 0.3 collective-permute-start.3
  10.6 0.3 collective-permute-start.2
  10.9 0.9 %collective-permute-done.1 = f32[112,128]{1,0:T(8,128)S(1)} collective-permute-done((f32[112,128]{1,0:T(8,128)S(1)}, f32[112,128]{1,0:T(8,128)S(1)}, u32[]{:S(2)}, u32[]{:S(2)}) %collective-permute-start.1) | collective-permute-done | bytes 57376 | tf_op jit(solution)/shard_map/ppermute | solution.py:207
  11.8 3.0 %collective-permute-done.3 = f32[112,128]{1,0:T(8,128)S(1)} collective-permute-done((f32[112,128]{1,0:T(8,128)S(1)}, f32[112,128]{1,0:T(8,128)S(1)}, u32[]{:S(2)}, u32[]{:S(2)}) %collective-permute-start.3) | collective-permute-done | bytes 57376 | tf_op jit(solution)/shard_map/ppermute | solution.py:207
  14.8 0.0 collective-permute-done.2
  14.8 2.6 %collective-permute-start.4 = (f32[112,128]{1,0:T(8,128)S(1)}, f32[112,128]{1,0:T(8,128)S(1)}, u32[]{:S(2)}, u32[]{:S(2)}) collective-permute-start(f32[112,128]{1,0:T(8,128)S(1)} %pad_add_fusion.2), channel_id=1, source_target_pairs={{0,72},{1,73},{2,74},{3,75},{4,76},{5,77},{6,78},{7,79},{8,64},{9,... | collective-permute-start | bytes 172040 | tf_op jit(solution)/shard_map/ppermute | solution.py:207
  17.4 0.5 %collective-permute-start.6 = (f32[112,128]{1,0:T(8,128)S(1)}, f32[112,128]{1,0:T(8,128)S(1)}, u32[]{:S(2)}, u32[]{:S(2)}) collective-permute-start(f32[112,128]{1,0:T(8,128)S(1)} %pad_add_fusion.2), channel_id=1, source_target_pairs={{0,64},{1,65},{2,66},{3,67},{4,68},{5,69},{6,70},{7,71},{8,72},{9,... | collective-permute-start | bytes 172040 | tf_op jit(solution)/shard_map/ppermute | solution.py:207
  17.9 0.3 collective-permute-start.5
  18.2 1.0 %collective-permute-done.4 = f32[112,128]{1,0:T(8,128)S(1)} collective-permute-done((f32[112,128]{1,0:T(8,128)S(1)}, f32[112,128]{1,0:T(8,128)S(1)}, u32[]{:S(2)}, u32[]{:S(2)}) %collective-permute-start.4) | collective-permute-done | bytes 57376 | tf_op jit(solution)/shard_map/ppermute | solution.py:207
  19.1 2.9 %collective-permute-done.6 = f32[112,128]{1,0:T(8,128)S(1)} collective-permute-done((f32[112,128]{1,0:T(8,128)S(1)}, f32[112,128]{1,0:T(8,128)S(1)}, u32[]{:S(2)}, u32[]{:S(2)}) %collective-permute-start.6) | collective-permute-done | bytes 57376 | tf_op jit(solution)/shard_map/ppermute | solution.py:207
  22.0 0.0 collective-permute-done.5
  22.1 3.8 %collective-permute-start.7 = (f32[112,128]{1,0:T(8,128)S(1)}, f32[112,128]{1,0:T(8,128)S(1)}, u32[]{:S(2)}, u32[]{:S(2)}) collective-permute-start(f32[112,128]{1,0:T(8,128)S(1)} %pad_add_fusion.1), channel_id=1, source_target_pairs={{0,48},{1,49},{2,50},{3,51},{4,52},{5,53},{6,54},{7,55},{8,56},{9,... | collective-permute-start | bytes 172040 | tf_op jit(solution)/shard_map/ppermute | solution.py:207
  25.9 0.0 collective-permute-start.9
  25.9 0.7 %collective-permute-start.8 = (f32[112,128]{1,0:T(8,128)S(1)}, f32[112,128]{1,0:T(8,128)S(1)}, u32[]{:S(2)}, u32[]{:S(2)}) collective-permute-start(f32[112,128]{1,0:T(8,128)S(1)} %pad_add_fusion.1), channel_id=1, source_target_pairs={{0,16},{1,17},{2,18},{3,19},{4,20},{5,21},{6,22},{7,23},{8,24},{9,... | collective-permute-start | bytes 172040 | tf_op jit(solution)/shard_map/ppermute | solution.py:207
  26.6 0.9 %collective-permute-done.7 = f32[112,128]{1,0:T(8,128)S(1)} collective-permute-done((f32[112,128]{1,0:T(8,128)S(1)}, f32[112,128]{1,0:T(8,128)S(1)}, u32[]{:S(2)}, u32[]{:S(2)}) %collective-permute-start.7) | collective-permute-done | bytes 57376 | tf_op jit(solution)/shard_map/ppermute | solution.py:207
  27.5 3.0 %collective-permute-done.9 = f32[112,128]{1,0:T(8,128)S(1)} collective-permute-done((f32[112,128]{1,0:T(8,128)S(1)}, f32[112,128]{1,0:T(8,128)S(1)}, u32[]{:S(2)}, u32[]{:S(2)}) %collective-permute-start.9) | collective-permute-done | bytes 57376 | tf_op jit(solution)/shard_map/ppermute | solution.py:207
  30.5 0.0 collective-permute-done.8
  30.5 4.7 %collective-permute-start.10 = (f32[112,128]{1,0:T(8,128)S(1)}, f32[112,128]{1,0:T(8,128)S(1)}, u32[]{:S(2)}, u32[]{:S(2)}) collective-permute-start(f32[112,128]{1,0:T(8,128)S(1)} %pad_add_fusion.refs_1_), channel_id=1, source_target_pairs={{0,4},{1,5},{2,6},{3,7},{4,0},{5,1},{6,2},{7,3},{8,12},{9,13},{10,... | collective-permute-start | bytes 172040 | tf_op jit(solution)/shard_map/ppermute | solution.py:207
  35.3 0.9 %collective-permute-done.10.refs_2_ = f32[112,128]{1,0:T(8,128)S(1)} collective-permute-done((f32[112,128]{1,0:T(8,128)S(1)}, f32[112,128]{1,0:T(8,128)S(1)}, u32[]{:S(2)}, u32[]{:S(2)}) %collective-permute-start.10) | collective-permute-done | bytes 57376 | tf_op jit(solution)/shard_map/ppermute | solution.py:207
  36.2 7.9 %factor.1 = (f32[128,4096]{1,0:T(8,128)}, f32[64,4096]{1,0:T(8,128)}, f32[128,128]{1,0:T(8,128)}, f32[64,128]{1,0:T(8,128)}) custom-call(s32[1]{0:T(128)} %bitcast.core_ref.refs_0_, f32[112,128]{1,0:T(8,128)S(1)} %pad_add_fusion.refs_1_, f32[112,128]{1,0:T(8,128)S(1)} %collective-permute-done.10.refs_2_, f32[128,4096]{1,0:T(8,128)} %refs_3_.1, ...), custom_call_target="tpu_custom_call" | custom-call | tf_op jit(solution)/shard_map/factor/pallas_call | solution.py:427
  (14 shorter events, 0.2 us)
Async XLA Ops:
  4.9 2.4 %collective-permute-start = (f32[112,128]{1,0:T(8,128)S(1)}, f32[112,128]{1,0:T(8,128)S(1)}, u32[]{:S(2)}, u32[]{:S(2)}) collective-permute-start(f32[112,128]{1,0:T(8,128)S(1)} %get-tuple-element.11), channel_id=1, source_target_pairs={{0,4},{1,5},{2,6},{3,7},{4,0},{5,1},{6,2},{7,3},{8,12},{9,13},{10,... | collective-permute-start | bytes 172040 | tf_op jit(solution)/shard_map/ppermute | solution.py:207
  7.3 4.5 %collective-permute-start.1 = (f32[112,128]{1,0:T(8,128)S(1)}, f32[112,128]{1,0:T(8,128)S(1)}, u32[]{:S(2)}, u32[]{:S(2)}) collective-permute-start(f32[112,128]{1,0:T(8,128)S(1)} %pad_add_fusion.3), channel_id=1, source_target_pairs={{0,3},{1,2},{2,1},{3,0},{4,7},{5,6},{6,5},{7,4},{8,11},{9,10},{10,... | collective-permute-start | bytes 172040 | tf_op jit(solution)/shard_map/ppermute | solution.py:207
  10.2 4.5 %collective-permute-start.3 = (f32[112,128]{1,0:T(8,128)S(1)}, f32[112,128]{1,0:T(8,128)S(1)}, u32[]{:S(2)}, u32[]{:S(2)}) collective-permute-start(f32[112,128]{1,0:T(8,128)S(1)} %pad_add_fusion.3), channel_id=1, source_target_pairs={{0,2},{1,3},{2,0},{3,1},{4,6},{5,7},{6,4},{7,5},{8,10},{9,11},{10,... | collective-permute-start | bytes 172040 | tf_op jit(solution)/shard_map/ppermute | solution.py:207
  10.6 4.2 %collective-permute-start.2 = (f32[112,128]{1,0:T(8,128)S(1)}, f32[112,128]{1,0:T(8,128)S(1)}, u32[]{:S(2)}, u32[]{:S(2)}) collective-permute-start(f32[112,128]{1,0:T(8,128)S(1)} %pad_add_fusion.3), channel_id=1, source_target_pairs={{0,1},{1,0},{2,3},{3,2},{4,5},{5,4},{6,7},{7,6},{8,9},{9,8},{10,11... | collective-permute-start | bytes 172040 | tf_op jit(solution)/shard_map/ppermute | solution.py:207
  14.8 4.3 %collective-permute-start.4 = (f32[112,128]{1,0:T(8,128)S(1)}, f32[112,128]{1,0:T(8,128)S(1)}, u32[]{:S(2)}, u32[]{:S(2)}) collective-permute-start(f32[112,128]{1,0:T(8,128)S(1)} %pad_add_fusion.2), channel_id=1, source_target_pairs={{0,72},{1,73},{2,74},{3,75},{4,76},{5,77},{6,78},{7,79},{8,64},{9,... | collective-permute-start | bytes 172040 | tf_op jit(solution)/shard_map/ppermute | solution.py:207
  17.4 4.6 %collective-permute-start.6 = (f32[112,128]{1,0:T(8,128)S(1)}, f32[112,128]{1,0:T(8,128)S(1)}, u32[]{:S(2)}, u32[]{:S(2)}) collective-permute-start(f32[112,128]{1,0:T(8,128)S(1)} %pad_add_fusion.2), channel_id=1, source_target_pairs={{0,64},{1,65},{2,66},{3,67},{4,68},{5,69},{6,70},{7,71},{8,72},{9,... | collective-permute-start | bytes 172040 | tf_op jit(solution)/shard_map/ppermute | solution.py:207
  17.9 4.1 %collective-permute-start.5 = (f32[112,128]{1,0:T(8,128)S(1)}, f32[112,128]{1,0:T(8,128)S(1)}, u32[]{:S(2)}, u32[]{:S(2)}) collective-permute-start(f32[112,128]{1,0:T(8,128)S(1)} %pad_add_fusion.2), channel_id=1, source_target_pairs={{0,8},{1,9},{2,10},{3,11},{4,12},{5,13},{6,14},{7,15},{8,0},{9,1},... | collective-permute-start | bytes 172040 | tf_op jit(solution)/shard_map/ppermute | solution.py:207
  22.1 5.4 %collective-permute-start.7 = (f32[112,128]{1,0:T(8,128)S(1)}, f32[112,128]{1,0:T(8,128)S(1)}, u32[]{:S(2)}, u32[]{:S(2)}) collective-permute-start(f32[112,128]{1,0:T(8,128)S(1)} %pad_add_fusion.1), channel_id=1, source_target_pairs={{0,48},{1,49},{2,50},{3,51},{4,52},{5,53},{6,54},{7,55},{8,56},{9,... | collective-permute-start | bytes 172040 | tf_op jit(solution)/shard_map/ppermute | solution.py:207
  25.9 4.5 %collective-permute-start.9 = (f32[112,128]{1,0:T(8,128)S(1)}, f32[112,128]{1,0:T(8,128)S(1)}, u32[]{:S(2)}, u32[]{:S(2)}) collective-permute-start(f32[112,128]{1,0:T(8,128)S(1)} %pad_add_fusion.1), channel_id=1, source_target_pairs={{0,32},{1,33},{2,34},{3,35},{4,36},{5,37},{6,38},{7,39},{8,40},{9,... | collective-permute-start | bytes 172040 | tf_op jit(solution)/shard_map/ppermute | solution.py:207
  25.9 4.5 %collective-permute-start.8 = (f32[112,128]{1,0:T(8,128)S(1)}, f32[112,128]{1,0:T(8,128)S(1)}, u32[]{:S(2)}, u32[]{:S(2)}) collective-permute-start(f32[112,128]{1,0:T(8,128)S(1)} %pad_add_fusion.1), channel_id=1, source_target_pairs={{0,16},{1,17},{2,18},{3,19},{4,20},{5,21},{6,22},{7,23},{8,24},{9,... | collective-permute-start | bytes 172040 | tf_op jit(solution)/shard_map/ppermute | solution.py:207
  30.5 5.6 %collective-permute-start.10 = (f32[112,128]{1,0:T(8,128)S(1)}, f32[112,128]{1,0:T(8,128)S(1)}, u32[]{:S(2)}, u32[]{:S(2)}) collective-permute-start(f32[112,128]{1,0:T(8,128)S(1)} %pad_add_fusion.refs_1_), channel_id=1, source_target_pairs={{0,4},{1,5},{2,6},{3,7},{4,0},{5,1},{6,2},{7,3},{8,12},{9,13},{10,... | collective-permute-start | bytes 172040 | tf_op jit(solution)/shard_map/ppermute | solution.py:207

commit v7 on v6

--- a/solution.py
+++ b/solution.py
@@ -9,7 +9,7 @@
 HIGHEST = lax.Precision.HIGHEST
 F32 = jnp.float32
 BF16 = jnp.bfloat16
-CHUNK = 2048
+CHUNKS = 4
 OUT_CHUNK = 512
 NEAR = 4
 SMALL = 2e-2
@@ -63,13 +63,13 @@
     return lax.broadcasted_iota(jnp.int32, shape, axis)
 
 
-def gram_kernel(core_ref, panel, trail, keep_ref, send_ref, pbuf, tbuf, ops, hi_ref, lo_ref, mix_ref, ca_ref, ac_ref, sems):
+def gram_kernel(core_ref, panel, trail, keep_ref, send_ref, pbuf, tbuf, ops, sems):
     n, rows = panel.shape
     t = trail.shape[0]
-    steps = rows // CHUNK
+    width = rows // CHUNKS
     copies = []
-    for k in range(steps):
-        at = pl.ds(k * CHUNK, CHUNK)
+    for k in range(CHUNKS):
+        at = pl.ds(k * width, width)
         pair = (
             pltpu.make_async_copy(panel.at[:, at], pbuf.at[k], sems.at[0, k]),
             pltpu.make_async_copy(trail.at[:, at], tbuf.at[k], sems.at[1, k]),
@@ -78,16 +78,22 @@
             copy.start()
         copies.append(pair)
 
+    top = jnp.zeros((n, 128), F32)
+    for k in range(CHUNKS):
+        copies[k][0].wait()
+        x = jnp.abs(pbuf[k])
+        for q in range(0, width, 128):
+            top = jnp.maximum(top, x[:, q : q + 128])
+    for k in range(CHUNKS):
+        copies[k][1].wait()
+    p, inv = power_near(jnp.max(top, axis=1, keepdims=True))
+
     def split(k):
-        copies[k][0].wait()
-        x = pbuf[k]
-        p, inv = power_near(jnp.max(jnp.abs(x), axis=1, keepdims=True))
-        a = x * (inv * 32.0)
+        a = pbuf[k] * (inv * 32.0)
         d1 = round_int(a)
         r1 = (a - d1) * 256.0
         d2 = round_int(r1)
         d3 = (r1 - d2) * 256.0
-        copies[k][1].wait()
         c = tbuf[k]
         c1 = c.astype(BF16)
         rc = c - c1.astype(F32)
@@ -97,38 +103,26 @@
         for part in (c3, d1, d2, d3, c1, c2):
             ops[k, at : at + part.shape[0], :] = part.astype(BF16)
             at += part.shape[0]
-        return p
-
-    def product(k, p):
-        left = nt(ops[k, 0 : t + 2 * n, :], ops[k, t : t + 2 * n, :])
-        right = nt(ops[k, t : t + 3 * n, :], ops[k, t + 2 * n :, :])
-        c3d1, left = left[:t, :n], left[t:, :]
-        row = jnp.broadcast_to(p * (1.0 / 32.0), (n, n))
-        col = row.T
-        scale = row * col
-        h, e = two_sum(left[:n, :n], (left[:n, n:] + left[n:, :n]) * 2.0**-8)
-        e = e + (left[n:, n:] * 2.0**-16 + right[2 * n :, :n] * 2.0**-32)
-        mix = (right[:n, :n] * 2.0**-16 + right[n : 2 * n, :n] * 2.0**-24) * scale
-        ac = right[2 * n :, n : n + t] * 2.0**-16 + right[n : 2 * n, n + t :] * 2.0**-8
-        ac = ac + (right[n : 2 * n, n : n + t] * 2.0**-8 + right[:n, n + t :])
-        ac = (ac + right[:n, n : n + t]) * row[:, :t]
-        ca = c3d1 * col[:t, :]
-        if k == 0:
-            hi_ref[...], lo_ref[...] = h * scale, e * scale
-            mix_ref[...], ca_ref[...], ac_ref[...] = mix, ca, ac
-        else:
-            hi, err = two_sum(hi_ref[...], h * scale)
-            hi_ref[...] = hi
-            lo_ref[...] += err + e * scale
-            mix_ref[...] += mix
-            ca_ref[...] += ca
-            ac_ref[...] += ac
-
-    p = split(0)
-    for k in range(steps):
-        following = split(k + 1) if k + 1 < steps else None
-        product(k, p)
-        p = following
+
+    left, right = None, None
+    split(0)
+    for k in range(CHUNKS):
+        if k + 1 < CHUNKS:
+            split(k + 1)
+        l = nt(ops[k, 0 : t + 2 * n, :], ops[k, t : t + 2 * n, :])
+        r = nt(ops[k, t : t + 3 * n, :], ops[k, t + 2 * n :, :])
+        left, right = (l, r) if left is None else (left + l, right + r)
+
+    c3d1, left = left[:t, :n], left[t:, :]
+    row = jnp.broadcast_to(p * (1.0 / 32.0), (n, n))
+    col = row.T
+    scale = row * col
+    h, e = two_sum(left[:n, :n], (left[:n, n:] + left[n:, :n]) * 2.0**-8)
+    e = e + (left[n:, n:] * 2.0**-16 + right[2 * n :, :n] * 2.0**-32)
+    mix = right[:n, :n] * 2.0**-16 + right[n : 2 * n, :n] * 2.0**-24
+    ac = right[2 * n :, n : n + t] * 2.0**-16 + right[n : 2 * n, n + t :] * 2.0**-8
+    ac = ac + (right[n : 2 * n, n : n + t] * 2.0**-8 + right[:n, n + t :])
+    ca = (c3d1 + (ac + right[:n, n : n + t]).T) * col[:t, :]
 
     core = core_ref[0]
     half = n // 2
@@ -140,11 +134,9 @@
         diag = jnp.sum(jnp.where(i == j - half, bottom, 0.0), axis=0, keepdims=True)
         return body, jnp.broadcast_to(diag, (8, n))
 
-    mix = mix_ref[...]
-    hi, lo = two_sum(hi_ref[...], lo_ref[...] + (mix + mix.T))
+    hi, lo = two_sum(h * scale, (e + (mix + mix.T)) * scale)
     hi_body, hi_diag = fold(hi)
     lo_body, lo_diag = fold(lo)
-    ca = ca_ref[...] + ac_ref[...].T
     q = half // 2
     tq = t // 2
 
@@ -165,7 +157,7 @@
 def local_gram(core, panel, trailing):
     n, rows = panel.shape
     t = trailing.shape[0]
-    steps = rows // CHUNK
+    width = rows // CHUNKS
     out = jax.ShapeDtypeStruct((n // 2 + 16 + t // 2, n), F32)
     vmem, hbm = pl.BlockSpec(memory_space=pltpu.VMEM), pl.BlockSpec(memory_space=pltpu.HBM)
     return pl.pallas_call(
@@ -174,15 +166,10 @@
         out_specs=[vmem, vmem],
         out_shape=[out, out],
         scratch_shapes=[
-            pltpu.VMEM((steps, n, CHUNK), F32),
-            pltpu.VMEM((steps, t, CHUNK), F32),
-            pltpu.VMEM((steps, 3 * (n + t), CHUNK), BF16),
-            pltpu.VMEM((n, n), F32),
-            pltpu.VMEM((n, n), F32),
-            pltpu.VMEM((n, n), F32),
-            pltpu.VMEM((t, n), F32),
-            pltpu.VMEM((n, t), F32),
-            pltpu.SemaphoreType.DMA((2, steps)),
+            pltpu.VMEM((CHUNKS, n, width), F32),
+            pltpu.VMEM((CHUNKS, t, width), F32),
+            pltpu.VMEM((CHUNKS, 3 * (n + t), width), BF16),
+            pltpu.SemaphoreType.DMA((2, CHUNKS)),
         ],
         compiler_params=pltpu.CompilerParams(vmem_limit_bytes=32 << 20),
         name="gram",

time: 44.1 us -> 43.9 us (level)
  no operation moved by 1% of the time
where the time goes in v7:
time: 43.9 us; the launch traced here: 43.8 us
  starting transfers between devices  17.7 us (40%)
  waiting for transfers between devices  13.4 us (31%)
  Pallas kernels  11.9 us (27%)
  between operations  0.72 us (2%)
    ppermute x11, starting transfers between devices, exchange(): return lax.ppermute(value, AXES, [(s, s ^ mask) for s in range(size)])  17.7 us
    ppermute x11, waiting for transfers between devices, exchange(): return lax.ppermute(value, AXES, [(s, s ^ mask) for s in range(size)])  13.4 us
    pallas_call x1, Pallas kernels, factor(): pl.pallas_call(lambda *refs: factor_kernel(rows_all, *refs), in_specs=[pl...  7.88 us
    pallas_call x1, Pallas kernels, local_gram(): pl.pallas_call(gram_kernel, in_specs=[pl.BlockSpec(memory_space=pltpu.SME...  3.99 us
  transfers between devices with their start and end apart: 11, of which 8 were waited for; matrix products, arithmetic and copies ran while one was open for 0% of the time, Pallas kernels for 0%

profile of v7, /device:TPU:1, one launch (start us, length us, event | category | flops | bytes accessed | tf_op | source)
XLA Modules:
  0.0 43.8 jit_solution(10581272374838384567)
XLA Ops:
  0.6 4.0 %gram.1 = (f32[112,128]{1,0:T(8,128)S(1)}, f32[112,128]{1,0:T(8,128)S(1)}) custom-call(s32[1]{0:T(128)} %bitcast.core_ref.refs_0_, f32[128,4096]{1,0:T(8,128)} %refs_3_.1, f32[64,4096]{1,0:T(8,128)} %refs_4_.1), custom_call_target="tpu_custom_call" | custom-call | tf_op jit(solution)/shard_map/gram/pallas_call | solution.py:163
  4.6 1.5 %collective-permute-start = (f32[112,128]{1,0:T(8,128)S(1)}, f32[112,128]{1,0:T(8,128)S(1)}, u32[]{:S(2)}, u32[]{:S(2)}) collective-permute-start(f32[112,128]{1,0:T(8,128)S(1)} %get-tuple-element.11), channel_id=1, source_target_pairs={{0,4},{1,5},{2,6},{3,7},{4,0},{5,1},{6,2},{7,3},{8,12},{9,13},{10,... | collective-permute-start | bytes 172040 | tf_op jit(solution)/shard_map/ppermute | solution.py:194
  6.1 0.9 %collective-permute-done = f32[112,128]{1,0:T(8,128)S(1)} collective-permute-done((f32[112,128]{1,0:T(8,128)S(1)}, f32[112,128]{1,0:T(8,128)S(1)}, u32[]{:S(2)}, u32[]{:S(2)}) %collective-permute-start) | collective-permute-done | bytes 57376 | tf_op jit(solution)/shard_map/ppermute | solution.py:194
  7.1 2.9 %collective-permute-start.1 = (f32[112,128]{1,0:T(8,128)S(1)}, f32[112,128]{1,0:T(8,128)S(1)}, u32[]{:S(2)}, u32[]{:S(2)}) collective-permute-start(f32[112,128]{1,0:T(8,128)S(1)} %pad_add_fusion.3), channel_id=1, source_target_pairs={{0,3},{1,2},{2,1},{3,0},{4,7},{5,6},{6,5},{7,4},{8,11},{9,10},{10,... | collective-permute-start | bytes 172040 | tf_op jit(solution)/shard_map/ppermute | solution.py:194
  10.0 0.3 collective-permute-start.3
  10.3 0.3 collective-permute-start.2
  10.6 0.9 %collective-permute-done.1 = f32[112,128]{1,0:T(8,128)S(1)} collective-permute-done((f32[112,128]{1,0:T(8,128)S(1)}, f32[112,128]{1,0:T(8,128)S(1)}, u32[]{:S(2)}, u32[]{:S(2)}) %collective-permute-start.1) | collective-permute-done | bytes 57376 | tf_op jit(solution)/shard_map/ppermute | solution.py:194
  11.5 3.0 %collective-permute-done.3 = f32[112,128]{1,0:T(8,128)S(1)} collective-permute-done((f32[112,128]{1,0:T(8,128)S(1)}, f32[112,128]{1,0:T(8,128)S(1)}, u32[]{:S(2)}, u32[]{:S(2)}) %collective-permute-start.3) | collective-permute-done | bytes 57376 | tf_op jit(solution)/shard_map/ppermute | solution.py:194
  14.5 0.0 collective-permute-done.2
  14.6 2.6 %collective-permute-start.4 = (f32[112,128]{1,0:T(8,128)S(1)}, f32[112,128]{1,0:T(8,128)S(1)}, u32[]{:S(2)}, u32[]{:S(2)}) collective-permute-start(f32[112,128]{1,0:T(8,128)S(1)} %pad_add_fusion.2), channel_id=1, source_target_pairs={{0,72},{1,73},{2,74},{3,75},{4,76},{5,77},{6,78},{7,79},{8,64},{9,... | collective-permute-start | bytes 172040 | tf_op jit(solution)/shard_map/ppermute | solution.py:194
  17.1 0.5 %collective-permute-start.6 = (f32[112,128]{1,0:T(8,128)S(1)}, f32[112,128]{1,0:T(8,128)S(1)}, u32[]{:S(2)}, u32[]{:S(2)}) collective-permute-start(f32[112,128]{1,0:T(8,128)S(1)} %pad_add_fusion.2), channel_id=1, source_target_pairs={{0,64},{1,65},{2,66},{3,67},{4,68},{5,69},{6,70},{7,71},{8,72},{9,... | collective-permute-start | bytes 172040 | tf_op jit(solution)/shard_map/ppermute | solution.py:194
  17.6 0.3 collective-permute-start.5
  17.9 1.0 %collective-permute-done.4 = f32[112,128]{1,0:T(8,128)S(1)} collective-permute-done((f32[112,128]{1,0:T(8,128)S(1)}, f32[112,128]{1,0:T(8,128)S(1)}, u32[]{:S(2)}, u32[]{:S(2)}) %collective-permute-start.4) | collective-permute-done | bytes 57376 | tf_op jit(solution)/shard_map/ppermute | solution.py:194
  18.9 2.9 %collective-permute-done.6 = f32[112,128]{1,0:T(8,128)S(1)} collective-permute-done((f32[112,128]{1,0:T(8,128)S(1)}, f32[112,128]{1,0:T(8,128)S(1)}, u32[]{:S(2)}, u32[]{:S(2)}) %collective-permute-start.6) | collective-permute-done | bytes 57376 | tf_op jit(solution)/shard_map/ppermute | solution.py:194
  21.8 0.0 collective-permute-done.5
  21.8 3.8 %collective-permute-start.7 = (f32[112,128]{1,0:T(8,128)S(1)}, f32[112,128]{1,0:T(8,128)S(1)}, u32[]{:S(2)}, u32[]{:S(2)}) collective-permute-start(f32[112,128]{1,0:T(8,128)S(1)} %pad_add_fusion.1), channel_id=1, source_target_pairs={{0,48},{1,49},{2,50},{3,51},{4,52},{5,53},{6,54},{7,55},{8,56},{9,... | collective-permute-start | bytes 172040 | tf_op jit(solution)/shard_map/ppermute | solution.py:194
  25.7 0.0 collective-permute-start.9
  25.7 0.7 %collective-permute-start.8 = (f32[112,128]{1,0:T(8,128)S(1)}, f32[112,128]{1,0:T(8,128)S(1)}, u32[]{:S(2)}, u32[]{:S(2)}) collective-permute-start(f32[112,128]{1,0:T(8,128)S(1)} %pad_add_fusion.1), channel_id=1, source_target_pairs={{0,16},{1,17},{2,18},{3,19},{4,20},{5,21},{6,22},{7,23},{8,24},{9,... | collective-permute-start | bytes 172040 | tf_op jit(solution)/shard_map/ppermute | solution.py:194
  26.3 0.9 %collective-permute-done.7 = f32[112,128]{1,0:T(8,128)S(1)} collective-permute-done((f32[112,128]{1,0:T(8,128)S(1)}, f32[112,128]{1,0:T(8,128)S(1)}, u32[]{:S(2)}, u32[]{:S(2)}) %collective-permute-start.7) | collective-permute-done | bytes 57376 | tf_op jit(solution)/shard_map/ppermute | solution.py:194
  27.2 3.0 %collective-permute-done.9 = f32[112,128]{1,0:T(8,128)S(1)} collective-permute-done((f32[112,128]{1,0:T(8,128)S(1)}, f32[112,128]{1,0:T(8,128)S(1)}, u32[]{:S(2)}, u32[]{:S(2)}) %collective-permute-start.9) | collective-permute-done | bytes 57376 | tf_op jit(solution)/shard_map/ppermute | solution.py:194
  30.2 0.0 collective-permute-done.8
  30.3 4.7 %collective-permute-start.10 = (f32[112,128]{1,0:T(8,128)S(1)}, f32[112,128]{1,0:T(8,128)S(1)}, u32[]{:S(2)}, u32[]{:S(2)}) collective-permute-start(f32[112,128]{1,0:T(8,128)S(1)} %pad_add_fusion.refs_1_), channel_id=1, source_target_pairs={{0,4},{1,5},{2,6},{3,7},{4,0},{5,1},{6,2},{7,3},{8,12},{9,13},{10,... | collective-permute-start | bytes 172040 | tf_op jit(solution)/shard_map/ppermute | solution.py:194
  35.0 0.9 %collective-permute-done.10.refs_2_ = f32[112,128]{1,0:T(8,128)S(1)} collective-permute-done((f32[112,128]{1,0:T(8,128)S(1)}, f32[112,128]{1,0:T(8,128)S(1)}, u32[]{:S(2)}, u32[]{:S(2)}) %collective-permute-start.10) | collective-permute-done | bytes 57376 | tf_op jit(solution)/shard_map/ppermute | solution.py:194
  35.9 7.9 %factor.1 = (f32[128,4096]{1,0:T(8,128)}, f32[64,4096]{1,0:T(8,128)}, f32[128,128]{1,0:T(8,128)}, f32[64,128]{1,0:T(8,128)}) custom-call(s32[1]{0:T(128)} %bitcast.core_ref.refs_0_, f32[112,128]{1,0:T(8,128)S(1)} %pad_add_fusion.refs_1_, f32[112,128]{1,0:T(8,128)S(1)} %collective-permute-done.10.refs_2_, f32[128,4096]{1,0:T(8,128)} %refs_3_.1, ...), custom_call_target="tpu_custom_call" | custom-call | tf_op jit(solution)/shard_map/factor/pallas_call | solution.py:414
  (14 shorter events, 0.2 us)
Async XLA Ops:
  4.6 2.4 %collective-permute-start = (f32[112,128]{1,0:T(8,128)S(1)}, f32[112,128]{1,0:T(8,128)S(1)}, u32[]{:S(2)}, u32[]{:S(2)}) collective-permute-start(f32[112,128]{1,0:T(8,128)S(1)} %get-tuple-element.11), channel_id=1, source_target_pairs={{0,4},{1,5},{2,6},{3,7},{4,0},{5,1},{6,2},{7,3},{8,12},{9,13},{10,... | collective-permute-start | bytes 172040 | tf_op jit(solution)/shard_map/ppermute | solution.py:194
  7.1 4.5 %collective-permute-start.1 = (f32[112,128]{1,0:T(8,128)S(1)}, f32[112,128]{1,0:T(8,128)S(1)}, u32[]{:S(2)}, u32[]{:S(2)}) collective-permute-start(f32[112,128]{1,0:T(8,128)S(1)} %pad_add_fusion.3), channel_id=1, source_target_pairs={{0,3},{1,2},{2,1},{3,0},{4,7},{5,6},{6,5},{7,4},{8,11},{9,10},{10,... | collective-permute-start | bytes 172040 | tf_op jit(solution)/shard_map/ppermute | solution.py:194
  10.0 4.5 %collective-permute-start.3 = (f32[112,128]{1,0:T(8,128)S(1)}, f32[112,128]{1,0:T(8,128)S(1)}, u32[]{:S(2)}, u32[]{:S(2)}) collective-permute-start(f32[112,128]{1,0:T(8,128)S(1)} %pad_add_fusion.3), channel_id=1, source_target_pairs={{0,2},{1,3},{2,0},{3,1},{4,6},{5,7},{6,4},{7,5},{8,10},{9,11},{10,... | collective-permute-start | bytes 172040 | tf_op jit(solution)/shard_map/ppermute | solution.py:194
  10.3 4.2 %collective-permute-start.2 = (f32[112,128]{1,0:T(8,128)S(1)}, f32[112,128]{1,0:T(8,128)S(1)}, u32[]{:S(2)}, u32[]{:S(2)}) collective-permute-start(f32[112,128]{1,0:T(8,128)S(1)} %pad_add_fusion.3), channel_id=1, source_target_pairs={{0,1},{1,0},{2,3},{3,2},{4,5},{5,4},{6,7},{7,6},{8,9},{9,8},{10,11... | collective-permute-start | bytes 172040 | tf_op jit(solution)/shard_map/ppermute | solution.py:194
  14.6 4.3 %collective-permute-start.4 = (f32[112,128]{1,0:T(8,128)S(1)}, f32[112,128]{1,0:T(8,128)S(1)}, u32[]{:S(2)}, u32[]{:S(2)}) collective-permute-start(f32[112,128]{1,0:T(8,128)S(1)} %pad_add_fusion.2), channel_id=1, source_target_pairs={{0,72},{1,73},{2,74},{3,75},{4,76},{5,77},{6,78},{7,79},{8,64},{9,... | collective-permute-start | bytes 172040 | tf_op jit(solution)/shard_map/ppermute | solution.py:194
  17.1 4.6 %collective-permute-start.6 = (f32[112,128]{1,0:T(8,128)S(1)}, f32[112,128]{1,0:T(8,128)S(1)}, u32[]{:S(2)}, u32[]{:S(2)}) collective-permute-start(f32[112,128]{1,0:T(8,128)S(1)} %pad_add_fusion.2), channel_id=1, source_target_pairs={{0,64},{1,65},{2,66},{3,67},{4,68},{5,69},{6,70},{7,71},{8,72},{9,... | collective-permute-start | bytes 172040 | tf_op jit(solution)/shard_map/ppermute | solution.py:194
  17.6 4.1 %collective-permute-start.5 = (f32[112,128]{1,0:T(8,128)S(1)}, f32[112,128]{1,0:T(8,128)S(1)}, u32[]{:S(2)}, u32[]{:S(2)}) collective-permute-start(f32[112,128]{1,0:T(8,128)S(1)} %pad_add_fusion.2), channel_id=1, source_target_pairs={{0,8},{1,9},{2,10},{3,11},{4,12},{5,13},{6,14},{7,15},{8,0},{9,1},... | collective-permute-start | bytes 172040 | tf_op jit(solution)/shard_map/ppermute | solution.py:194
  21.8 5.4 %collective-permute-start.7 = (f32[112,128]{1,0:T(8,128)S(1)}, f32[112,128]{1,0:T(8,128)S(1)}, u32[]{:S(2)}, u32[]{:S(2)}) collective-permute-start(f32[112,128]{1,0:T(8,128)S(1)} %pad_add_fusion.1), channel_id=1, source_target_pairs={{0,48},{1,49},{2,50},{3,51},{4,52},{5,53},{6,54},{7,55},{8,56},{9,... | collective-permute-start | bytes 172040 | tf_op jit(solution)/shard_map/ppermute | solution.py:194
  25.7 4.5 %collective-permute-start.9 = (f32[112,128]{1,0:T(8,128)S(1)}, f32[112,128]{1,0:T(8,128)S(1)}, u32[]{:S(2)}, u32[]{:S(2)}) collective-permute-start(f32[112,128]{1,0:T(8,128)S(1)} %pad_add_fusion.1), channel_id=1, source_target_pairs={{0,32},{1,33},{2,34},{3,35},{4,36},{5,37},{6,38},{7,39},{8,40},{9,... | collective-permute-start | bytes 172040 | tf_op jit(solution)/shard_map/ppermute | solution.py:194
  25.7 4.5 %collective-permute-start.8 = (f32[112,128]{1,0:T(8,128)S(1)}, f32[112,128]{1,0:T(8,128)S(1)}, u32[]{:S(2)}, u32[]{:S(2)}) collective-permute-start(f32[112,128]{1,0:T(8,128)S(1)} %pad_add_fusion.1), channel_id=1, source_target_pairs={{0,16},{1,17},{2,18},{3,19},{4,20},{5,21},{6,22},{7,23},{8,24},{9,... | collective-permute-start | bytes 172040 | tf_op jit(solution)/shard_map/ppermute | solution.py:194
  30.3 5.6 %collective-permute-start.10 = (f32[112,128]{1,0:T(8,128)S(1)}, f32[112,128]{1,0:T(8,128)S(1)}, u32[]{:S(2)}, u32[]{:S(2)}) collective-permute-start(f32[112,128]{1,0:T(8,128)S(1)} %pad_add_fusion.refs_1_), channel_id=1, source_target_pairs={{0,4},{1,5},{2,6},{3,7},{4,0},{5,1},{6,2},{7,3},{8,12},{9,13},{10,... | collective-permute-start | bytes 172040 | tf_op jit(solution)/shard_map/ppermute | solution.py:194

commit v8 on v7

--- a/solution.py
+++ b/solution.py
@@ -310,26 +310,31 @@
     i, j = iota((n, n), 0), iota((n, n), 1)
     hi_, hj_ = iota((half, n), 0), iota((half, n), 1)
 
-    def unfold(start):
-        body = jnp.concatenate([a[start : start + q, :], b[start : start + q, :]], axis=0)
-        diag = jnp.broadcast_to(a[start + q : start + q + 1, :], (half, n))
-        top = jnp.where((hj_ < half) & (hi_ >= hj_), pltpu.roll(body, half, 1), 0.0)
-        keep = jnp.where((hj_ < half) | (hi_ < hj_ - half), body, 0.0)
+    def unfold(packed, diag_row):
+        diag = jnp.broadcast_to(diag_row, (half, n))
+        top = jnp.where((hj_ < half) & (hi_ >= hj_), pltpu.roll(packed, half, 1), 0.0)
+        keep = jnp.where((hj_ < half) | (hi_ < hj_ - half), packed, 0.0)
         bottom = jnp.where(hi_ == hj_ - half, diag, keep)
         part = jnp.concatenate([top, bottom], axis=0)
         return jnp.where(i == j, part, part + part.T)
 
-    g_hi, g_lo = unfold(0), unfold(q + 8)
+    def packed(start):
+        return jnp.concatenate([a[start : start + q, :], b[start : start + q, :]], axis=0), a[start + q : start + q + 1, :]
+
+    hi_body, hi_diag = packed(0)
+    lo_body, lo_diag = packed(q + 8)
     ca = jnp.concatenate([a[2 * q + 16 :, :], b[2 * q + 16 :, :]], axis=0)
-    g_hi, g_lo = two_sum(g_hi, g_lo)
+    hi_body, lo_body = two_sum(hi_body, lo_body)
+    hi_diag, lo_diag = two_sum(hi_diag, lo_diag)
+    g_hi, g_lo = unfold(hi_body, hi_diag), unfold(lo_body, lo_diag)
+    w = jnp.concatenate(chol_inv([g_hi[8 * r : 8 * r + 8, :] for r in range(n // 8)]), axis=0)
 
     diag = jnp.sum(jnp.where(i == j, g_hi, 0.0), axis=0, keepdims=True)
     pc, inv_pc = power_near(jnp.sqrt(diag))
     ic = jnp.broadcast_to(inv_pc, (n, n))
     eq = ic * ic.T
     s_hi, s_lo = g_hi * eq, g_lo * eq
-
-    w = jnp.concatenate(chol_inv([s_hi[8 * r : 8 * r + 8, :] for r in range(n // 8)]), axis=0)
+    w = w * jnp.broadcast_to(pc, (n, n))
 
     qr, inv_qr = power_near(jnp.max(jnp.abs(w), axis=1, keepdims=True))
     wd = slices(w * (inv_qr * 64.0), None, 3)
@@ -397,7 +402,7 @@
     wide = nn(v, jnp.concatenate([wt, t_true, y], axis=1), precision=HIGHEST)
     w_new = wide[:, :n] * ic
     root = jnp.sqrt(jnp.float32(rows_all))
-    upper_ref[...] = jnp.where(i <= j, wide[:, n : 2 * n] / root, 0.0)
+    upper_ref[...] = jnp.where(i <= j, wide[:, n : 2 * n] * (1.0 / root), 0.0)
     coupling_t = wide[:, 2 * n :].T
     coup_ref[...] = coupling_t
     wz = jnp.concatenate([w_new, nn(coupling_t, w_new, precision=HIGHEST)], axis=0)

time: 43.9 us -> 43.9 us (level)
  no operation moved by 1% of the time
where the time goes in v8:
time: 43.9 us; the launch traced here: 43.8 us
  starting transfers between devices  17.7 us (40%)
  waiting for transfers between devices  13.4 us (31%)
  Pallas kernels  11.8 us (27%)
  between operations  0.72 us (2%)
    ppermute x11, starting transfers between devices, exchange(): return lax.ppermute(value, AXES, [(s, s ^ mask) for s in range(size)])  17.7 us
    ppermute x11, waiting for transfers between devices, exchange(): return lax.ppermute(value, AXES, [(s, s ^ mask) for s in range(size)])  13.4 us
    pallas_call x1, Pallas kernels, factor(): pl.pallas_call(lambda *refs: factor_kernel(rows_all, *refs), in_specs=[pl...  7.85 us
    pallas_call x1, Pallas kernels, local_gram(): pl.pallas_call(gram_kernel, in_specs=[pl.BlockSpec(memory_space=pltpu.SME...  3.99 us
  transfers between devices with their start and end apart: 11, of which 8 were waited for; matrix products, arithmetic and copies ran while one was open for 0% of the time, Pallas kernels for 0%

profile of v8, /device:TPU:1, one launch (start us, length us, event | category | flops | bytes accessed | tf_op | source)
XLA Modules:
  0.0 43.8 jit_solution(16976541142738330311)
XLA Ops:
  0.6 4.0 %gram.1 = (f32[112,128]{1,0:T(8,128)S(1)}, f32[112,128]{1,0:T(8,128)S(1)}) custom-call(s32[1]{0:T(128)} %bitcast.core_ref.refs_0_, f32[128,4096]{1,0:T(8,128)} %refs_3_.1, f32[64,4096]{1,0:T(8,128)} %refs_4_.1), custom_call_target="tpu_custom_call" | custom-call | tf_op jit(solution)/shard_map/gram/pallas_call | solution.py:163
  4.6 1.5 %collective-permute-start = (f32[112,128]{1,0:T(8,128)S(1)}, f32[112,128]{1,0:T(8,128)S(1)}, u32[]{:S(2)}, u32[]{:S(2)}) collective-permute-start(f32[112,128]{1,0:T(8,128)S(1)} %get-tuple-element.11), channel_id=1, source_target_pairs={{0,4},{1,5},{2,6},{3,7},{4,0},{5,1},{6,2},{7,3},{8,12},{9,13},{10,... | collective-permute-start | bytes 172040 | tf_op jit(solution)/shard_map/ppermute | solution.py:194
  6.1 0.9 %collective-permute-done = f32[112,128]{1,0:T(8,128)S(1)} collective-permute-done((f32[112,128]{1,0:T(8,128)S(1)}, f32[112,128]{1,0:T(8,128)S(1)}, u32[]{:S(2)}, u32[]{:S(2)}) %collective-permute-start) | collective-permute-done | bytes 57376 | tf_op jit(solution)/shard_map/ppermute | solution.py:194
  7.1 2.9 %collective-permute-start.1 = (f32[112,128]{1,0:T(8,128)S(1)}, f32[112,128]{1,0:T(8,128)S(1)}, u32[]{:S(2)}, u32[]{:S(2)}) collective-permute-start(f32[112,128]{1,0:T(8,128)S(1)} %pad_add_fusion.3), channel_id=1, source_target_pairs={{0,3},{1,2},{2,1},{3,0},{4,7},{5,6},{6,5},{7,4},{8,11},{9,10},{10,... | collective-permute-start | bytes 172040 | tf_op jit(solution)/shard_map/ppermute | solution.py:194
  10.0 0.3 collective-permute-start.3
  10.3 0.3 collective-permute-start.2
  10.6 0.9 %collective-permute-done.1 = f32[112,128]{1,0:T(8,128)S(1)} collective-permute-done((f32[112,128]{1,0:T(8,128)S(1)}, f32[112,128]{1,0:T(8,128)S(1)}, u32[]{:S(2)}, u32[]{:S(2)}) %collective-permute-start.1) | collective-permute-done | bytes 57376 | tf_op jit(solution)/shard_map/ppermute | solution.py:194
  11.5 3.0 %collective-permute-done.3 = f32[112,128]{1,0:T(8,128)S(1)} collective-permute-done((f32[112,128]{1,0:T(8,128)S(1)}, f32[112,128]{1,0:T(8,128)S(1)}, u32[]{:S(2)}, u32[]{:S(2)}) %collective-permute-start.3) | collective-permute-done | bytes 57376 | tf_op jit(solution)/shard_map/ppermute | solution.py:194
  14.5 0.0 collective-permute-done.2
  14.6 2.6 %collective-permute-start.4 = (f32[112,128]{1,0:T(8,128)S(1)}, f32[112,128]{1,0:T(8,128)S(1)}, u32[]{:S(2)}, u32[]{:S(2)}) collective-permute-start(f32[112,128]{1,0:T(8,128)S(1)} %pad_add_fusion.2), channel_id=1, source_target_pairs={{0,72},{1,73},{2,74},{3,75},{4,76},{5,77},{6,78},{7,79},{8,64},{9,... | collective-permute-start | bytes 172040 | tf_op jit(solution)/shard_map/ppermute | solution.py:194
  17.1 0.5 %collective-permute-start.6 = (f32[112,128]{1,0:T(8,128)S(1)}, f32[112,128]{1,0:T(8,128)S(1)}, u32[]{:S(2)}, u32[]{:S(2)}) collective-permute-start(f32[112,128]{1,0:T(8,128)S(1)} %pad_add_fusion.2), channel_id=1, source_target_pairs={{0,64},{1,65},{2,66},{3,67},{4,68},{5,69},{6,70},{7,71},{8,72},{9,... | collective-permute-start | bytes 172040 | tf_op jit(solution)/shard_map/ppermute | solution.py:194
  17.6 0.3 collective-permute-start.5
  17.9 1.0 %collective-permute-done.4 = f32[112,128]{1,0:T(8,128)S(1)} collective-permute-done((f32[112,128]{1,0:T(8,128)S(1)}, f32[112,128]{1,0:T(8,128)S(1)}, u32[]{:S(2)}, u32[]{:S(2)}) %collective-permute-start.4) | collective-permute-done | bytes 57376 | tf_op jit(solution)/shard_map/ppermute | solution.py:194
  18.9 2.9 %collective-permute-done.6 = f32[112,128]{1,0:T(8,128)S(1)} collective-permute-done((f32[112,128]{1,0:T(8,128)S(1)}, f32[112,128]{1,0:T(8,128)S(1)}, u32[]{:S(2)}, u32[]{:S(2)}) %collective-permute-start.6) | collective-permute-done | bytes 57376 | tf_op jit(solution)/shard_map/ppermute | solution.py:194
  21.8 0.0 collective-permute-done.5
  21.8 3.8 %collective-permute-start.7 = (f32[112,128]{1,0:T(8,128)S(1)}, f32[112,128]{1,0:T(8,128)S(1)}, u32[]{:S(2)}, u32[]{:S(2)}) collective-permute-start(f32[112,128]{1,0:T(8,128)S(1)} %pad_add_fusion.1), channel_id=1, source_target_pairs={{0,48},{1,49},{2,50},{3,51},{4,52},{5,53},{6,54},{7,55},{8,56},{9,... | collective-permute-start | bytes 172040 | tf_op jit(solution)/shard_map/ppermute | solution.py:194
  25.7 0.0 collective-permute-start.9
  25.7 0.7 %collective-permute-start.8 = (f32[112,128]{1,0:T(8,128)S(1)}, f32[112,128]{1,0:T(8,128)S(1)}, u32[]{:S(2)}, u32[]{:S(2)}) collective-permute-start(f32[112,128]{1,0:T(8,128)S(1)} %pad_add_fusion.1), channel_id=1, source_target_pairs={{0,16},{1,17},{2,18},{3,19},{4,20},{5,21},{6,22},{7,23},{8,24},{9,... | collective-permute-start | bytes 172040 | tf_op jit(solution)/shard_map/ppermute | solution.py:194
  26.3 0.9 %collective-permute-done.7 = f32[112,128]{1,0:T(8,128)S(1)} collective-permute-done((f32[112,128]{1,0:T(8,128)S(1)}, f32[112,128]{1,0:T(8,128)S(1)}, u32[]{:S(2)}, u32[]{:S(2)}) %collective-permute-start.7) | collective-permute-done | bytes 57376 | tf_op jit(solution)/shard_map/ppermute | solution.py:194
  27.2 3.0 %collective-permute-done.9 = f32[112,128]{1,0:T(8,128)S(1)} collective-permute-done((f32[112,128]{1,0:T(8,128)S(1)}, f32[112,128]{1,0:T(8,128)S(1)}, u32[]{:S(2)}, u32[]{:S(2)}) %collective-permute-start.9) | collective-permute-done | bytes 57376 | tf_op jit(solution)/shard_map/ppermute | solution.py:194
  30.2 0.0 collective-permute-done.8
  30.3 4.7 %collective-permute-start.10 = (f32[112,128]{1,0:T(8,128)S(1)}, f32[112,128]{1,0:T(8,128)S(1)}, u32[]{:S(2)}, u32[]{:S(2)}) collective-permute-start(f32[112,128]{1,0:T(8,128)S(1)} %pad_add_fusion.refs_1_), channel_id=1, source_target_pairs={{0,4},{1,5},{2,6},{3,7},{4,0},{5,1},{6,2},{7,3},{8,12},{9,13},{10,... | collective-permute-start | bytes 172040 | tf_op jit(solution)/shard_map/ppermute | solution.py:194
  35.0 0.9 %collective-permute-done.10.refs_2_ = f32[112,128]{1,0:T(8,128)S(1)} collective-permute-done((f32[112,128]{1,0:T(8,128)S(1)}, f32[112,128]{1,0:T(8,128)S(1)}, u32[]{:S(2)}, u32[]{:S(2)}) %collective-permute-start.10) | collective-permute-done | bytes 57376 | tf_op jit(solution)/shard_map/ppermute | solution.py:194
  35.9 7.9 %factor.1 = (f32[128,4096]{1,0:T(8,128)}, f32[64,4096]{1,0:T(8,128)}, f32[128,128]{1,0:T(8,128)}, f32[64,128]{1,0:T(8,128)}) custom-call(s32[1]{0:T(128)} %bitcast.core_ref.refs_0_, f32[112,128]{1,0:T(8,128)S(1)} %pad_add_fusion.refs_1_, f32[112,128]{1,0:T(8,128)S(1)} %collective-permute-done.10.refs_2_, f32[128,4096]{1,0:T(8,128)} %refs_3_.1, ...), custom_call_target="tpu_custom_call" | custom-call | tf_op jit(solution)/shard_map/factor/pallas_call | solution.py:419
  (14 shorter events, 0.2 us)
Async XLA Ops:
  4.6 2.4 %collective-permute-start = (f32[112,128]{1,0:T(8,128)S(1)}, f32[112,128]{1,0:T(8,128)S(1)}, u32[]{:S(2)}, u32[]{:S(2)}) collective-permute-start(f32[112,128]{1,0:T(8,128)S(1)} %get-tuple-element.11), channel_id=1, source_target_pairs={{0,4},{1,5},{2,6},{3,7},{4,0},{5,1},{6,2},{7,3},{8,12},{9,13},{10,... | collective-permute-start | bytes 172040 | tf_op jit(solution)/shard_map/ppermute | solution.py:194
  7.1 4.5 %collective-permute-start.1 = (f32[112,128]{1,0:T(8,128)S(1)}, f32[112,128]{1,0:T(8,128)S(1)}, u32[]{:S(2)}, u32[]{:S(2)}) collective-permute-start(f32[112,128]{1,0:T(8,128)S(1)} %pad_add_fusion.3), channel_id=1, source_target_pairs={{0,3},{1,2},{2,1},{3,0},{4,7},{5,6},{6,5},{7,4},{8,11},{9,10},{10,... | collective-permute-start | bytes 172040 | tf_op jit(solution)/shard_map/ppermute | solution.py:194
  10.0 4.5 %collective-permute-start.3 = (f32[112,128]{1,0:T(8,128)S(1)}, f32[112,128]{1,0:T(8,128)S(1)}, u32[]{:S(2)}, u32[]{:S(2)}) collective-permute-start(f32[112,128]{1,0:T(8,128)S(1)} %pad_add_fusion.3), channel_id=1, source_target_pairs={{0,2},{1,3},{2,0},{3,1},{4,6},{5,7},{6,4},{7,5},{8,10},{9,11},{10,... | collective-permute-start | bytes 172040 | tf_op jit(solution)/shard_map/ppermute | solution.py:194
  10.3 4.2 %collective-permute-start.2 = (f32[112,128]{1,0:T(8,128)S(1)}, f32[112,128]{1,0:T(8,128)S(1)}, u32[]{:S(2)}, u32[]{:S(2)}) collective-permute-start(f32[112,128]{1,0:T(8,128)S(1)} %pad_add_fusion.3), channel_id=1, source_target_pairs={{0,1},{1,0},{2,3},{3,2},{4,5},{5,4},{6,7},{7,6},{8,9},{9,8},{10,11... | collective-permute-start | bytes 172040 | tf_op jit(solution)/shard_map/ppermute | solution.py:194
  14.6 4.3 %collective-permute-start.4 = (f32[112,128]{1,0:T(8,128)S(1)}, f32[112,128]{1,0:T(8,128)S(1)}, u32[]{:S(2)}, u32[]{:S(2)}) collective-permute-start(f32[112,128]{1,0:T(8,128)S(1)} %pad_add_fusion.2), channel_id=1, source_target_pairs={{0,72},{1,73},{2,74},{3,75},{4,76},{5,77},{6,78},{7,79},{8,64},{9,... | collective-permute-start | bytes 172040 | tf_op jit(solution)/shard_map/ppermute | solution.py:194
  17.1 4.6 %collective-permute-start.6 = (f32[112,128]{1,0:T(8,128)S(1)}, f32[112,128]{1,0:T(8,128)S(1)}, u32[]{:S(2)}, u32[]{:S(2)}) collective-permute-start(f32[112,128]{1,0:T(8,128)S(1)} %pad_add_fusion.2), channel_id=1, source_target_pairs={{0,64},{1,65},{2,66},{3,67},{4,68},{5,69},{6,70},{7,71},{8,72},{9,... | collective-permute-start | bytes 172040 | tf_op jit(solution)/shard_map/ppermute | solution.py:194
  17.6 4.1 %collective-permute-start.5 = (f32[112,128]{1,0:T(8,128)S(1)}, f32[112,128]{1,0:T(8,128)S(1)}, u32[]{:S(2)}, u32[]{:S(2)}) collective-permute-start(f32[112,128]{1,0:T(8,128)S(1)} %pad_add_fusion.2), channel_id=1, source_target_pairs={{0,8},{1,9},{2,10},{3,11},{4,12},{5,13},{6,14},{7,15},{8,0},{9,1},... | collective-permute-start | bytes 172040 | tf_op jit(solution)/shard_map/ppermute | solution.py:194
  21.8 5.4 %collective-permute-start.7 = (f32[112,128]{1,0:T(8,128)S(1)}, f32[112,128]{1,0:T(8,128)S(1)}, u32[]{:S(2)}, u32[]{:S(2)}) collective-permute-start(f32[112,128]{1,0:T(8,128)S(1)} %pad_add_fusion.1), channel_id=1, source_target_pairs={{0,48},{1,49},{2,50},{3,51},{4,52},{5,53},{6,54},{7,55},{8,56},{9,... | collective-permute-start | bytes 172040 | tf_op jit(solution)/shard_map/ppermute | solution.py:194
  25.7 4.5 %collective-permute-start.9 = (f32[112,128]{1,0:T(8,128)S(1)}, f32[112,128]{1,0:T(8,128)S(1)}, u32[]{:S(2)}, u32[]{:S(2)}) collective-permute-start(f32[112,128]{1,0:T(8,128)S(1)} %pad_add_fusion.1), channel_id=1, source_target_pairs={{0,32},{1,33},{2,34},{3,35},{4,36},{5,37},{6,38},{7,39},{8,40},{9,... | collective-permute-start | bytes 172040 | tf_op jit(solution)/shard_map/ppermute | solution.py:194
  25.7 4.5 %collective-permute-start.8 = (f32[112,128]{1,0:T(8,128)S(1)}, f32[112,128]{1,0:T(8,128)S(1)}, u32[]{:S(2)}, u32[]{:S(2)}) collective-permute-start(f32[112,128]{1,0:T(8,128)S(1)} %pad_add_fusion.1), channel_id=1, source_target_pairs={{0,16},{1,17},{2,18},{3,19},{4,20},{5,21},{6,22},{7,23},{8,24},{9,... | collective-permute-start | bytes 172040 | tf_op jit(solution)/shard_map/ppermute | solution.py:194
  30.3 5.6 %collective-permute-start.10 = (f32[112,128]{1,0:T(8,128)S(1)}, f32[112,128]{1,0:T(8,128)S(1)}, u32[]{:S(2)}, u32[]{:S(2)}) collective-permute-start(f32[112,128]{1,0:T(8,128)S(1)} %pad_add_fusion.refs_1_), channel_id=1, source_target_pairs={{0,4},{1,5},{2,6},{3,7},{4,0},{5,1},{6,2},{7,3},{8,12},{9,13},{10,... | collective-permute-start | bytes 172040 | tf_op jit(solution)/shard_map/ppermute | solution.py:194

commit v9 on v8

--- a/solution.py
+++ b/solution.py
@@ -292,8 +292,8 @@
 
 
 def factor_kernel(
-    rows_all, core_ref, own_ref, other_ref, panel, trailing, basis, updated, upper_ref, coup_ref,
-    wcat, gcat, tcat, v_ref, panel_buf, trail_buf, in_sems, words, basis_buf, updated_buf, out_sems,
+    rows_all, core_ref, own_ref, other_ref, panel, trailing, basis, updated, upper, coup,
+    upper_ref, coup_ref, small_sems, wcat, gcat, tcat, v_ref, panel_buf, trail_buf, in_sems, words, basis_buf, updated_buf, out_sems,
 ):
     loads = (
         pltpu.make_async_copy(panel, panel_buf, in_sems.at[0]),
@@ -405,10 +405,18 @@
     upper_ref[...] = jnp.where(i <= j, wide[:, n : 2 * n] * (1.0 / root), 0.0)
     coupling_t = wide[:, 2 * n :].T
     coup_ref[...] = coupling_t
+    stores = (
+        pltpu.make_async_copy(upper_ref, upper, small_sems.at[0]),
+        pltpu.make_async_copy(coup_ref, coup, small_sems.at[1]),
+    )
+    for store in stores:
+        store.start()
     wz = jnp.concatenate([w_new, nn(coupling_t, w_new, precision=HIGHEST)], axis=0)
     for load in loads:
         load.wait()
     apply_factors(wz, root, panel_buf, trail_buf, basis, updated, words, basis_buf, updated_buf, out_sems)
+    for store in stores:
+        store.wait()
 
 
 def factor(core, own, other, panel, trailing, rows_all):
@@ -419,7 +427,7 @@
     return pl.pallas_call(
         lambda *refs: factor_kernel(rows_all, *refs),
         in_specs=[pl.BlockSpec(memory_space=pltpu.SMEM), vmem, vmem, hbm, hbm],
-        out_specs=[hbm, hbm, vmem, vmem],
+        out_specs=[hbm] * 4,
         out_shape=[
             jax.ShapeDtypeStruct((n, rows), F32),
             jax.ShapeDtypeStruct((t, rows), F32),
@@ -427,6 +435,9 @@
             jax.ShapeDtypeStruct((t, n), F32),
         ],
         scratch_shapes=[
+            pltpu.VMEM((n, n), F32),
+            pltpu.VMEM((t, n), F32),
+            pltpu.SemaphoreType.DMA((2,)),
             pltpu.VMEM((n, 3 * n), BF16),
             pltpu.VMEM((6 * n, n), BF16),
             pltpu.VMEM((n, 4 * n), BF16),

time: 43.9 us -> 43.3 us (0.986)
  Pallas kernels: 11.8 us -> 11.2 us
    pallas_call x1, Pallas kernels: 7.85 us -> 7.23 us  [factor(): pl.pallas_call(lambda *refs: factor_kernel(rows_all, *refs), in_specs=[pl...]
where the time goes in v9:
time: 43.3 us; the launch traced here: 43.1 us
  starting transfers between devices  17.7 us (41%)
  waiting for transfers between devices  13.4 us (31%)
  Pallas kernels  11.2 us (26%)
  between operations  0.72 us (2%)
    ppermute x11, starting transfers between devices, exchange(): return lax.ppermute(value, AXES, [(s, s ^ mask) for s in range(size)])  17.7 us
    ppermute x11, waiting for transfers between devices, exchange(): return lax.ppermute(value, AXES, [(s, s ^ mask) for s in range(size)])  13.4 us
    pallas_call x1, Pallas kernels, factor(): pl.pallas_call(lambda *refs: factor_kernel(rows_all, *refs), in_specs=[pl...  7.23 us
    pallas_call x1, Pallas kernels, local_gram(): pl.pallas_call(gram_kernel, in_specs=[pl.BlockSpec(memory_space=pltpu.SME...  3.99 us
  transfers between devices with their start and end apart: 11, of which 8 were waited for; matrix products, arithmetic and copies ran while one was open for 0% of the time, Pallas kernels for 0%

profile of v9, /device:TPU:1, one launch (start us, length us, event | category | flops | bytes accessed | tf_op | source)
XLA Modules:
  0.0 43.1 jit_solution(7084944933450465748)
XLA Ops:
  0.6 4.0 %gram.1 = (f32[112,128]{1,0:T(8,128)S(1)}, f32[112,128]{1,0:T(8,128)S(1)}) custom-call(s32[1]{0:T(128)} %bitcast.core_ref.refs_0_, f32[128,4096]{1,0:T(8,128)} %refs_3_.1, f32[64,4096]{1,0:T(8,128)} %refs_4_.1), custom_call_target="tpu_custom_call" | custom-call | tf_op jit(solution)/shard_map/gram/pallas_call | solution.py:163
  4.6 1.5 %collective-permute-start = (f32[112,128]{1,0:T(8,128)S(1)}, f32[112,128]{1,0:T(8,128)S(1)}, u32[]{:S(2)}, u32[]{:S(2)}) collective-permute-start(f32[112,128]{1,0:T(8,128)S(1)} %get-tuple-element.11), channel_id=1, source_target_pairs={{0,4},{1,5},{2,6},{3,7},{4,0},{5,1},{6,2},{7,3},{8,12},{9,13},{10,... | collective-permute-start | bytes 172040 | tf_op jit(solution)/shard_map/ppermute | solution.py:194
  6.1 0.9 %collective-permute-done = f32[112,128]{1,0:T(8,128)S(1)} collective-permute-done((f32[112,128]{1,0:T(8,128)S(1)}, f32[112,128]{1,0:T(8,128)S(1)}, u32[]{:S(2)}, u32[]{:S(2)}) %collective-permute-start) | collective-permute-done | bytes 57376 | tf_op jit(solution)/shard_map/ppermute | solution.py:194
  7.1 2.9 %collective-permute-start.1 = (f32[112,128]{1,0:T(8,128)S(1)}, f32[112,128]{1,0:T(8,128)S(1)}, u32[]{:S(2)}, u32[]{:S(2)}) collective-permute-start(f32[112,128]{1,0:T(8,128)S(1)} %pad_add_fusion.3), channel_id=1, source_target_pairs={{0,3},{1,2},{2,1},{3,0},{4,7},{5,6},{6,5},{7,4},{8,11},{9,10},{10,... | collective-permute-start | bytes 172040 | tf_op jit(solution)/shard_map/ppermute | solution.py:194
  10.0 0.3 collective-permute-start.3
  10.3 0.3 collective-permute-start.2
  10.6 0.9 %collective-permute-done.1 = f32[112,128]{1,0:T(8,128)S(1)} collective-permute-done((f32[112,128]{1,0:T(8,128)S(1)}, f32[112,128]{1,0:T(8,128)S(1)}, u32[]{:S(2)}, u32[]{:S(2)}) %collective-permute-start.1) | collective-permute-done | bytes 57376 | tf_op jit(solution)/shard_map/ppermute | solution.py:194
  11.5 3.0 %collective-permute-done.3 = f32[112,128]{1,0:T(8,128)S(1)} collective-permute-done((f32[112,128]{1,0:T(8,128)S(1)}, f32[112,128]{1,0:T(8,128)S(1)}, u32[]{:S(2)}, u32[]{:S(2)}) %collective-permute-start.3) | collective-permute-done | bytes 57376 | tf_op jit(solution)/shard_map/ppermute | solution.py:194
  14.5 0.0 collective-permute-done.2
  14.6 2.6 %collective-permute-start.4 = (f32[112,128]{1,0:T(8,128)S(1)}, f32[112,128]{1,0:T(8,128)S(1)}, u32[]{:S(2)}, u32[]{:S(2)}) collective-permute-start(f32[112,128]{1,0:T(8,128)S(1)} %pad_add_fusion.2), channel_id=1, source_target_pairs={{0,72},{1,73},{2,74},{3,75},{4,76},{5,77},{6,78},{7,79},{8,64},{9,... | collective-permute-start | bytes 172040 | tf_op jit(solution)/shard_map/ppermute | solution.py:194
  17.1 0.5 %collective-permute-start.6 = (f32[112,128]{1,0:T(8,128)S(1)}, f32[112,128]{1,0:T(8,128)S(1)}, u32[]{:S(2)}, u32[]{:S(2)}) collective-permute-start(f32[112,128]{1,0:T(8,128)S(1)} %pad_add_fusion.2), channel_id=1, source_target_pairs={{0,64},{1,65},{2,66},{3,67},{4,68},{5,69},{6,70},{7,71},{8,72},{9,... | collective-permute-start | bytes 172040 | tf_op jit(solution)/shard_map/ppermute | solution.py:194
  17.6 0.3 collective-permute-start.5
  17.9 1.0 %collective-permute-done.4 = f32[112,128]{1,0:T(8,128)S(1)} collective-permute-done((f32[112,128]{1,0:T(8,128)S(1)}, f32[112,128]{1,0:T(8,128)S(1)}, u32[]{:S(2)}, u32[]{:S(2)}) %collective-permute-start.4) | collective-permute-done | bytes 57376 | tf_op jit(solution)/shard_map/ppermute | solution.py:194
  18.9 2.9 %collective-permute-done.6 = f32[112,128]{1,0:T(8,128)S(1)} collective-permute-done((f32[112,128]{1,0:T(8,128)S(1)}, f32[112,128]{1,0:T(8,128)S(1)}, u32[]{:S(2)}, u32[]{:S(2)}) %collective-permute-start.6) | collective-permute-done | bytes 57376 | tf_op jit(solution)/shard_map/ppermute | solution.py:194
  21.8 0.0 collective-permute-done.5
  21.8 3.8 %collective-permute-start.7 = (f32[112,128]{1,0:T(8,128)S(1)}, f32[112,128]{1,0:T(8,128)S(1)}, u32[]{:S(2)}, u32[]{:S(2)}) collective-permute-start(f32[112,128]{1,0:T(8,128)S(1)} %pad_add_fusion.1), channel_id=1, source_target_pairs={{0,48},{1,49},{2,50},{3,51},{4,52},{5,53},{6,54},{7,55},{8,56},{9,... | collective-permute-start | bytes 172040 | tf_op jit(solution)/shard_map/ppermute | solution.py:194
  25.7 0.0 collective-permute-start.9
  25.7 0.7 %collective-permute-start.8 = (f32[112,128]{1,0:T(8,128)S(1)}, f32[112,128]{1,0:T(8,128)S(1)}, u32[]{:S(2)}, u32[]{:S(2)}) collective-permute-start(f32[112,128]{1,0:T(8,128)S(1)} %pad_add_fusion.1), channel_id=1, source_target_pairs={{0,16},{1,17},{2,18},{3,19},{4,20},{5,21},{6,22},{7,23},{8,24},{9,... | collective-permute-start | bytes 172040 | tf_op jit(solution)/shard_map/ppermute | solution.py:194
  26.3 0.9 %collective-permute-done.7 = f32[112,128]{1,0:T(8,128)S(1)} collective-permute-done((f32[112,128]{1,0:T(8,128)S(1)}, f32[112,128]{1,0:T(8,128)S(1)}, u32[]{:S(2)}, u32[]{:S(2)}) %collective-permute-start.7) | collective-permute-done | bytes 57376 | tf_op jit(solution)/shard_map/ppermute | solution.py:194
  27.2 3.0 %collective-permute-done.9 = f32[112,128]{1,0:T(8,128)S(1)} collective-permute-done((f32[112,128]{1,0:T(8,128)S(1)}, f32[112,128]{1,0:T(8,128)S(1)}, u32[]{:S(2)}, u32[]{:S(2)}) %collective-permute-start.9) | collective-permute-done | bytes 57376 | tf_op jit(solution)/shard_map/ppermute | solution.py:194
  30.2 0.0 collective-permute-done.8
  30.3 4.7 %collective-permute-start.10 = (f32[112,128]{1,0:T(8,128)S(1)}, f32[112,128]{1,0:T(8,128)S(1)}, u32[]{:S(2)}, u32[]{:S(2)}) collective-permute-start(f32[112,128]{1,0:T(8,128)S(1)} %pad_add_fusion.refs_1_), channel_id=1, source_target_pairs={{0,4},{1,5},{2,6},{3,7},{4,0},{5,1},{6,2},{7,3},{8,12},{9,13},{10,... | collective-permute-start | bytes 172040 | tf_op jit(solution)/shard_map/ppermute | solution.py:194
  35.0 0.9 %collective-permute-done.10.refs_2_ = f32[112,128]{1,0:T(8,128)S(1)} collective-permute-done((f32[112,128]{1,0:T(8,128)S(1)}, f32[112,128]{1,0:T(8,128)S(1)}, u32[]{:S(2)}, u32[]{:S(2)}) %collective-permute-start.10) | collective-permute-done | bytes 57376 | tf_op jit(solution)/shard_map/ppermute | solution.py:194
  35.9 7.2 %factor.1 = (f32[128,4096]{1,0:T(8,128)}, f32[64,4096]{1,0:T(8,128)}, f32[128,128]{1,0:T(8,128)}, f32[64,128]{1,0:T(8,128)}) custom-call(s32[1]{0:T(128)} %bitcast.core_ref.refs_0_, f32[112,128]{1,0:T(8,128)S(1)} %pad_add_fusion.refs_1_, f32[112,128]{1,0:T(8,128)S(1)} %collective-permute-done.10.refs_2_, f32[128,4096]{1,0:T(8,128)} %refs_3_.1, ...), custom_call_target="tpu_custom_call" | custom-call | tf_op jit(solution)/shard_map/factor/pallas_call | solution.py:427
  (14 shorter events, 0.2 us)
Async XLA Ops:
  4.6 2.4 %collective-permute-start = (f32[112,128]{1,0:T(8,128)S(1)}, f32[112,128]{1,0:T(8,128)S(1)}, u32[]{:S(2)}, u32[]{:S(2)}) collective-permute-start(f32[112,128]{1,0:T(8,128)S(1)} %get-tuple-element.11), channel_id=1, source_target_pairs={{0,4},{1,5},{2,6},{3,7},{4,0},{5,1},{6,2},{7,3},{8,12},{9,13},{10,... | collective-permute-start | bytes 172040 | tf_op jit(solution)/shard_map/ppermute | solution.py:194
  7.1 4.5 %collective-permute-start.1 = (f32[112,128]{1,0:T(8,128)S(1)}, f32[112,128]{1,0:T(8,128)S(1)}, u32[]{:S(2)}, u32[]{:S(2)}) collective-permute-start(f32[112,128]{1,0:T(8,128)S(1)} %pad_add_fusion.3), channel_id=1, source_target_pairs={{0,3},{1,2},{2,1},{3,0},{4,7},{5,6},{6,5},{7,4},{8,11},{9,10},{10,... | collective-permute-start | bytes 172040 | tf_op jit(solution)/shard_map/ppermute | solution.py:194
  10.0 4.5 %collective-permute-start.3 = (f32[112,128]{1,0:T(8,128)S(1)}, f32[112,128]{1,0:T(8,128)S(1)}, u32[]{:S(2)}, u32[]{:S(2)}) collective-permute-start(f32[112,128]{1,0:T(8,128)S(1)} %pad_add_fusion.3), channel_id=1, source_target_pairs={{0,2},{1,3},{2,0},{3,1},{4,6},{5,7},{6,4},{7,5},{8,10},{9,11},{10,... | collective-permute-start | bytes 172040 | tf_op jit(solution)/shard_map/ppermute | solution.py:194
  10.3 4.2 %collective-permute-start.2 = (f32[112,128]{1,0:T(8,128)S(1)}, f32[112,128]{1,0:T(8,128)S(1)}, u32[]{:S(2)}, u32[]{:S(2)}) collective-permute-start(f32[112,128]{1,0:T(8,128)S(1)} %pad_add_fusion.3), channel_id=1, source_target_pairs={{0,1},{1,0},{2,3},{3,2},{4,5},{5,4},{6,7},{7,6},{8,9},{9,8},{10,11... | collective-permute-start | bytes 172040 | tf_op jit(solution)/shard_map/ppermute | solution.py:194
  14.6 4.3 %collective-permute-start.4 = (f32[112,128]{1,0:T(8,128)S(1)}, f32[112,128]{1,0:T(8,128)S(1)}, u32[]{:S(2)}, u32[]{:S(2)}) collective-permute-start(f32[112,128]{1,0:T(8,128)S(1)} %pad_add_fusion.2), channel_id=1, source_target_pairs={{0,72},{1,73},{2,74},{3,75},{4,76},{5,77},{6,78},{7,79},{8,64},{9,... | collective-permute-start | bytes 172040 | tf_op jit(solution)/shard_map/ppermute | solution.py:194
  17.1 4.6 %collective-permute-start.6 = (f32[112,128]{1,0:T(8,128)S(1)}, f32[112,128]{1,0:T(8,128)S(1)}, u32[]{:S(2)}, u32[]{:S(2)}) collective-permute-start(f32[112,128]{1,0:T(8,128)S(1)} %pad_add_fusion.2), channel_id=1, source_target_pairs={{0,64},{1,65},{2,66},{3,67},{4,68},{5,69},{6,70},{7,71},{8,72},{9,... | collective-permute-start | bytes 172040 | tf_op jit(solution)/shard_map/ppermute | solution.py:194
  17.6 4.1 %collective-permute-start.5 = (f32[112,128]{1,0:T(8,128)S(1)}, f32[112,128]{1,0:T(8,128)S(1)}, u32[]{:S(2)}, u32[]{:S(2)}) collective-permute-start(f32[112,128]{1,0:T(8,128)S(1)} %pad_add_fusion.2), channel_id=1, source_target_pairs={{0,8},{1,9},{2,10},{3,11},{4,12},{5,13},{6,14},{7,15},{8,0},{9,1},... | collective-permute-start | bytes 172040 | tf_op jit(solution)/shard_map/ppermute | solution.py:194
  21.8 5.4 %collective-permute-start.7 = (f32[112,128]{1,0:T(8,128)S(1)}, f32[112,128]{1,0:T(8,128)S(1)}, u32[]{:S(2)}, u32[]{:S(2)}) collective-permute-start(f32[112,128]{1,0:T(8,128)S(1)} %pad_add_fusion.1), channel_id=1, source_target_pairs={{0,48},{1,49},{2,50},{3,51},{4,52},{5,53},{6,54},{7,55},{8,56},{9,... | collective-permute-start | bytes 172040 | tf_op jit(solution)/shard_map/ppermute | solution.py:194
  25.7 4.5 %collective-permute-start.9 = (f32[112,128]{1,0:T(8,128)S(1)}, f32[112,128]{1,0:T(8,128)S(1)}, u32[]{:S(2)}, u32[]{:S(2)}) collective-permute-start(f32[112,128]{1,0:T(8,128)S(1)} %pad_add_fusion.1), channel_id=1, source_target_pairs={{0,32},{1,33},{2,34},{3,35},{4,36},{5,37},{6,38},{7,39},{8,40},{9,... | collective-permute-start | bytes 172040 | tf_op jit(solution)/shard_map/ppermute | solution.py:194
  25.7 4.5 %collective-permute-start.8 = (f32[112,128]{1,0:T(8,128)S(1)}, f32[112,128]{1,0:T(8,128)S(1)}, u32[]{:S(2)}, u32[]{:S(2)}) collective-permute-start(f32[112,128]{1,0:T(8,128)S(1)} %pad_add_fusion.1), channel_id=1, source_target_pairs={{0,16},{1,17},{2,18},{3,19},{4,20},{5,21},{6,22},{7,23},{8,24},{9,... | collective-permute-start | bytes 172040 | tf_op jit(solution)/shard_map/ppermute | solution.py:194
  30.3 5.6 %collective-permute-start.10 = (f32[112,128]{1,0:T(8,128)S(1)}, f32[112,128]{1,0:T(8,128)S(1)}, u32[]{:S(2)}, u32[]{:S(2)}) collective-permute-start(f32[112,128]{1,0:T(8,128)S(1)} %pad_add_fusion.refs_1_), channel_id=1, source_target_pairs={{0,4},{1,5},{2,6},{3,7},{4,0},{5,1},{6,2},{7,3},{8,12},{9,13},{10,... | collective-permute-start | bytes 172040 | tf_op jit(solution)/shard_map/ppermute | solution.py:194

commit v10 on v9

--- a/solution.py
+++ b/solution.py
@@ -74,9 +74,10 @@
             pltpu.make_async_copy(panel.at[:, at], pbuf.at[k], sems.at[0, k]),
             pltpu.make_async_copy(trail.at[:, at], tbuf.at[k], sems.at[1, k]),
         )
-        for copy in pair:
-            copy.start()
         copies.append(pair)
+    for which in range(2):
+        for pair in copies:
+            pair[which].start()
 
     top = jnp.zeros((n, 128), F32)
     for k in range(CHUNKS):
@@ -84,9 +85,9 @@
         x = jnp.abs(pbuf[k])
         for q in range(0, width, 128):
             top = jnp.maximum(top, x[:, q : q + 128])
+    p, inv = power_near(jnp.max(top, axis=1, keepdims=True))
     for k in range(CHUNKS):
         copies[k][1].wait()
-    p, inv = power_near(jnp.max(top, axis=1, keepdims=True))
 
     def split(k):
         a = pbuf[k] * (inv * 32.0)

time: 43.3 us -> 43.1 us (level)
  no operation moved by 1% of the time
where the time goes in v10:
time: 43.1 us; the launch traced here: 43 us
  starting transfers between devices  17.6 us (41%)
  waiting for transfers between devices  13.4 us (31%)
  Pallas kernels  11.1 us (26%)
  between operations  0.72 us (2%)
    ppermute x11, starting transfers between devices, exchange(): return lax.ppermute(value, AXES, [(s, s ^ mask) for s in range(size)])  17.6 us
    ppermute x11, waiting for transfers between devices, exchange(): return lax.ppermute(value, AXES, [(s, s ^ mask) for s in range(size)])  13.4 us
    pallas_call x1, Pallas kernels, factor(): pl.pallas_call(lambda *refs: factor_kernel(rows_all, *refs), in_specs=[pl...  7.23 us
    pallas_call x1, Pallas kernels, local_gram(): pl.pallas_call(gram_kernel, in_specs=[pl.BlockSpec(memory_space=pltpu.SME...  3.87 us
  transfers between devices with their start and end apart: 11, of which 8 were waited for; matrix products, arithmetic and copies ran while one was open for 0% of the time, Pallas kernels for 0%

profile of v10, /device:TPU:1, one launch (start us, length us, event | category | flops | bytes accessed | tf_op | source)
XLA Modules:
  0.0 43.0 jit_solution(891414222097779908)
XLA Ops:
  0.6 3.9 %gram.1 = (f32[112,128]{1,0:T(8,128)S(1)}, f32[112,128]{1,0:T(8,128)S(1)}) custom-call(s32[1]{0:T(128)} %bitcast.core_ref.refs_0_, f32[128,4096]{1,0:T(8,128)} %refs_3_.1, f32[64,4096]{1,0:T(8,128)} %refs_4_.1), custom_call_target="tpu_custom_call" | custom-call | tf_op jit(solution)/shard_map/gram/pallas_call | solution.py:164
  4.5 1.5 %collective-permute-start = (f32[112,128]{1,0:T(8,128)S(1)}, f32[112,128]{1,0:T(8,128)S(1)}, u32[]{:S(2)}, u32[]{:S(2)}) collective-permute-start(f32[112,128]{1,0:T(8,128)S(1)} %get-tuple-element.11), channel_id=1, source_target_pairs={{0,4},{1,5},{2,6},{3,7},{4,0},{5,1},{6,2},{7,3},{8,12},{9,13},{10,... | collective-permute-start | bytes 172040 | tf_op jit(solution)/shard_map/ppermute | solution.py:195
  6.0 0.9 %collective-permute-done = f32[112,128]{1,0:T(8,128)S(1)} collective-permute-done((f32[112,128]{1,0:T(8,128)S(1)}, f32[112,128]{1,0:T(8,128)S(1)}, u32[]{:S(2)}, u32[]{:S(2)}) %collective-permute-start) | collective-permute-done | bytes 57376 | tf_op jit(solution)/shard_map/ppermute | solution.py:195
  6.9 2.9 %collective-permute-start.1 = (f32[112,128]{1,0:T(8,128)S(1)}, f32[112,128]{1,0:T(8,128)S(1)}, u32[]{:S(2)}, u32[]{:S(2)}) collective-permute-start(f32[112,128]{1,0:T(8,128)S(1)} %pad_add_fusion.3), channel_id=1, source_target_pairs={{0,3},{1,2},{2,1},{3,0},{4,7},{5,6},{6,5},{7,4},{8,11},{9,10},{10,... | collective-permute-start | bytes 172040 | tf_op jit(solution)/shard_map/ppermute | solution.py:195
  9.8 0.3 collective-permute-start.3
  10.2 0.3 collective-permute-start.2
  10.5 0.9 %collective-permute-done.1 = f32[112,128]{1,0:T(8,128)S(1)} collective-permute-done((f32[112,128]{1,0:T(8,128)S(1)}, f32[112,128]{1,0:T(8,128)S(1)}, u32[]{:S(2)}, u32[]{:S(2)}) %collective-permute-start.1) | collective-permute-done | bytes 57376 | tf_op jit(solution)/shard_map/ppermute | solution.py:195
  11.4 3.0 %collective-permute-done.3 = f32[112,128]{1,0:T(8,128)S(1)} collective-permute-done((f32[112,128]{1,0:T(8,128)S(1)}, f32[112,128]{1,0:T(8,128)S(1)}, u32[]{:S(2)}, u32[]{:S(2)}) %collective-permute-start.3) | collective-permute-done | bytes 57376 | tf_op jit(solution)/shard_map/ppermute | solution.py:195
  14.4 0.0 collective-permute-done.2
  14.4 2.6 %collective-permute-start.4 = (f32[112,128]{1,0:T(8,128)S(1)}, f32[112,128]{1,0:T(8,128)S(1)}, u32[]{:S(2)}, u32[]{:S(2)}) collective-permute-start(f32[112,128]{1,0:T(8,128)S(1)} %pad_add_fusion.2), channel_id=1, source_target_pairs={{0,72},{1,73},{2,74},{3,75},{4,76},{5,77},{6,78},{7,79},{8,64},{9,... | collective-permute-start | bytes 172040 | tf_op jit(solution)/shard_map/ppermute | solution.py:195
  17.0 0.5 %collective-permute-start.6 = (f32[112,128]{1,0:T(8,128)S(1)}, f32[112,128]{1,0:T(8,128)S(1)}, u32[]{:S(2)}, u32[]{:S(2)}) collective-permute-start(f32[112,128]{1,0:T(8,128)S(1)} %pad_add_fusion.2), channel_id=1, source_target_pairs={{0,64},{1,65},{2,66},{3,67},{4,68},{5,69},{6,70},{7,71},{8,72},{9,... | collective-permute-start | bytes 172040 | tf_op jit(solution)/shard_map/ppermute | solution.py:195
  17.5 0.3 collective-permute-start.5
  17.8 1.0 %collective-permute-done.4 = f32[112,128]{1,0:T(8,128)S(1)} collective-permute-done((f32[112,128]{1,0:T(8,128)S(1)}, f32[112,128]{1,0:T(8,128)S(1)}, u32[]{:S(2)}, u32[]{:S(2)}) %collective-permute-start.4) | collective-permute-done | bytes 57376 | tf_op jit(solution)/shard_map/ppermute | solution.py:195
  18.8 2.9 %collective-permute-done.6 = f32[112,128]{1,0:T(8,128)S(1)} collective-permute-done((f32[112,128]{1,0:T(8,128)S(1)}, f32[112,128]{1,0:T(8,128)S(1)}, u32[]{:S(2)}, u32[]{:S(2)}) %collective-permute-start.6) | collective-permute-done | bytes 57376 | tf_op jit(solution)/shard_map/ppermute | solution.py:195
  21.6 0.0 collective-permute-done.5
  21.7 3.8 %collective-permute-start.7 = (f32[112,128]{1,0:T(8,128)S(1)}, f32[112,128]{1,0:T(8,128)S(1)}, u32[]{:S(2)}, u32[]{:S(2)}) collective-permute-start(f32[112,128]{1,0:T(8,128)S(1)} %pad_add_fusion.1), channel_id=1, source_target_pairs={{0,48},{1,49},{2,50},{3,51},{4,52},{5,53},{6,54},{7,55},{8,56},{9,... | collective-permute-start | bytes 172040 | tf_op jit(solution)/shard_map/ppermute | solution.py:195
  25.5 0.0 collective-permute-start.9
  25.5 0.7 %collective-permute-start.8 = (f32[112,128]{1,0:T(8,128)S(1)}, f32[112,128]{1,0:T(8,128)S(1)}, u32[]{:S(2)}, u32[]{:S(2)}) collective-permute-start(f32[112,128]{1,0:T(8,128)S(1)} %pad_add_fusion.1), channel_id=1, source_target_pairs={{0,16},{1,17},{2,18},{3,19},{4,20},{5,21},{6,22},{7,23},{8,24},{9,... | collective-permute-start | bytes 172040 | tf_op jit(solution)/shard_map/ppermute | solution.py:195
  26.2 0.9 %collective-permute-done.7 = f32[112,128]{1,0:T(8,128)S(1)} collective-permute-done((f32[112,128]{1,0:T(8,128)S(1)}, f32[112,128]{1,0:T(8,128)S(1)}, u32[]{:S(2)}, u32[]{:S(2)}) %collective-permute-start.7) | collective-permute-done | bytes 57376 | tf_op jit(solution)/shard_map/ppermute | solution.py:195
  27.1 3.0 %collective-permute-done.9 = f32[112,128]{1,0:T(8,128)S(1)} collective-permute-done((f32[112,128]{1,0:T(8,128)S(1)}, f32[112,128]{1,0:T(8,128)S(1)}, u32[]{:S(2)}, u32[]{:S(2)}) %collective-permute-start.9) | collective-permute-done | bytes 57376 | tf_op jit(solution)/shard_map/ppermute | solution.py:195
  30.1 0.0 collective-permute-done.8
  30.1 4.7 %collective-permute-start.10 = (f32[112,128]{1,0:T(8,128)S(1)}, f32[112,128]{1,0:T(8,128)S(1)}, u32[]{:S(2)}, u32[]{:S(2)}) collective-permute-start(f32[112,128]{1,0:T(8,128)S(1)} %pad_add_fusion.refs_1_), channel_id=1, source_target_pairs={{0,4},{1,5},{2,6},{3,7},{4,0},{5,1},{6,2},{7,3},{8,12},{9,13},{10,... | collective-permute-start | bytes 172040 | tf_op jit(solution)/shard_map/ppermute | solution.py:195
  34.9 0.9 %collective-permute-done.10.refs_2_ = f32[112,128]{1,0:T(8,128)S(1)} collective-permute-done((f32[112,128]{1,0:T(8,128)S(1)}, f32[112,128]{1,0:T(8,128)S(1)}, u32[]{:S(2)}, u32[]{:S(2)}) %collective-permute-start.10) | collective-permute-done | bytes 57376 | tf_op jit(solution)/shard_map/ppermute | solution.py:195
  35.8 7.2 %factor.1 = (f32[128,4096]{1,0:T(8,128)}, f32[64,4096]{1,0:T(8,128)}, f32[128,128]{1,0:T(8,128)}, f32[64,128]{1,0:T(8,128)}) custom-call(s32[1]{0:T(128)} %bitcast.core_ref.refs_0_, f32[112,128]{1,0:T(8,128)S(1)} %pad_add_fusion.refs_1_, f32[112,128]{1,0:T(8,128)S(1)} %collective-permute-done.10.refs_2_, f32[128,4096]{1,0:T(8,128)} %refs_3_.1, ...), custom_call_target="tpu_custom_call" | custom-call | tf_op jit(solution)/shard_map/factor/pallas_call | solution.py:428
  (14 shorter events, 0.2 us)
Async XLA Ops:
  4.5 2.4 %collective-permute-start = (f32[112,128]{1,0:T(8,128)S(1)}, f32[112,128]{1,0:T(8,128)S(1)}, u32[]{:S(2)}, u32[]{:S(2)}) collective-permute-start(f32[112,128]{1,0:T(8,128)S(1)} %get-tuple-element.11), channel_id=1, source_target_pairs={{0,4},{1,5},{2,6},{3,7},{4,0},{5,1},{6,2},{7,3},{8,12},{9,13},{10,... | collective-permute-start | bytes 172040 | tf_op jit(solution)/shard_map/ppermute | solution.py:195
  6.9 4.5 %collective-permute-start.1 = (f32[112,128]{1,0:T(8,128)S(1)}, f32[112,128]{1,0:T(8,128)S(1)}, u32[]{:S(2)}, u32[]{:S(2)}) collective-permute-start(f32[112,128]{1,0:T(8,128)S(1)} %pad_add_fusion.3), channel_id=1, source_target_pairs={{0,3},{1,2},{2,1},{3,0},{4,7},{5,6},{6,5},{7,4},{8,11},{9,10},{10,... | collective-permute-start | bytes 172040 | tf_op jit(solution)/shard_map/ppermute | solution.py:195
  9.8 4.5 %collective-permute-start.3 = (f32[112,128]{1,0:T(8,128)S(1)}, f32[112,128]{1,0:T(8,128)S(1)}, u32[]{:S(2)}, u32[]{:S(2)}) collective-permute-start(f32[112,128]{1,0:T(8,128)S(1)} %pad_add_fusion.3), channel_id=1, source_target_pairs={{0,2},{1,3},{2,0},{3,1},{4,6},{5,7},{6,4},{7,5},{8,10},{9,11},{10,... | collective-permute-start | bytes 172040 | tf_op jit(solution)/shard_map/ppermute | solution.py:195
  10.2 4.2 %collective-permute-start.2 = (f32[112,128]{1,0:T(8,128)S(1)}, f32[112,128]{1,0:T(8,128)S(1)}, u32[]{:S(2)}, u32[]{:S(2)}) collective-permute-start(f32[112,128]{1,0:T(8,128)S(1)} %pad_add_fusion.3), channel_id=1, source_target_pairs={{0,1},{1,0},{2,3},{3,2},{4,5},{5,4},{6,7},{7,6},{8,9},{9,8},{10,11... | collective-permute-start | bytes 172040 | tf_op jit(solution)/shard_map/ppermute | solution.py:195
  14.4 4.3 %collective-permute-start.4 = (f32[112,128]{1,0:T(8,128)S(1)}, f32[112,128]{1,0:T(8,128)S(1)}, u32[]{:S(2)}, u32[]{:S(2)}) collective-permute-start(f32[112,128]{1,0:T(8,128)S(1)} %pad_add_fusion.2), channel_id=1, source_target_pairs={{0,72},{1,73},{2,74},{3,75},{4,76},{5,77},{6,78},{7,79},{8,64},{9,... | collective-permute-start | bytes 172040 | tf_op jit(solution)/shard_map/ppermute | solution.py:195
  17.0 4.6 %collective-permute-start.6 = (f32[112,128]{1,0:T(8,128)S(1)}, f32[112,128]{1,0:T(8,128)S(1)}, u32[]{:S(2)}, u32[]{:S(2)}) collective-permute-start(f32[112,128]{1,0:T(8,128)S(1)} %pad_add_fusion.2), channel_id=1, source_target_pairs={{0,64},{1,65},{2,66},{3,67},{4,68},{5,69},{6,70},{7,71},{8,72},{9,... | collective-permute-start | bytes 172040 | tf_op jit(solution)/shard_map/ppermute | solution.py:195
  17.5 4.1 %collective-permute-start.5 = (f32[112,128]{1,0:T(8,128)S(1)}, f32[112,128]{1,0:T(8,128)S(1)}, u32[]{:S(2)}, u32[]{:S(2)}) collective-permute-start(f32[112,128]{1,0:T(8,128)S(1)} %pad_add_fusion.2), channel_id=1, source_target_pairs={{0,8},{1,9},{2,10},{3,11},{4,12},{5,13},{6,14},{7,15},{8,0},{9,1},... | collective-permute-start | bytes 172040 | tf_op jit(solution)/shard_map/ppermute | solution.py:195
  21.7 5.4 %collective-permute-start.7 = (f32[112,128]{1,0:T(8,128)S(1)}, f32[112,128]{1,0:T(8,128)S(1)}, u32[]{:S(2)}, u32[]{:S(2)}) collective-permute-start(f32[112,128]{1,0:T(8,128)S(1)} %pad_add_fusion.1), channel_id=1, source_target_pairs={{0,48},{1,49},{2,50},{3,51},{4,52},{5,53},{6,54},{7,55},{8,56},{9,... | collective-permute-start | bytes 172040 | tf_op jit(solution)/shard_map/ppermute | solution.py:195
  25.5 4.5 %collective-permute-start.9 = (f32[112,128]{1,0:T(8,128)S(1)}, f32[112,128]{1,0:T(8,128)S(1)}, u32[]{:S(2)}, u32[]{:S(2)}) collective-permute-start(f32[112,128]{1,0:T(8,128)S(1)} %pad_add_fusion.1), channel_id=1, source_target_pairs={{0,32},{1,33},{2,34},{3,35},{4,36},{5,37},{6,38},{7,39},{8,40},{9,... | collective-permute-start | bytes 172040 | tf_op jit(solution)/shard_map/ppermute | solution.py:195
  25.5 4.5 %collective-permute-start.8 = (f32[112,128]{1,0:T(8,128)S(1)}, f32[112,128]{1,0:T(8,128)S(1)}, u32[]{:S(2)}, u32[]{:S(2)}) collective-permute-start(f32[112,128]{1,0:T(8,128)S(1)} %pad_add_fusion.1), channel_id=1, source_target_pairs={{0,16},{1,17},{2,18},{3,19},{4,20},{5,21},{6,22},{7,23},{8,24},{9,... | collective-permute-start | bytes 172040 | tf_op jit(solution)/shard_map/ppermute | solution.py:195
  30.1 5.6 %collective-permute-start.10 = (f32[112,128]{1,0:T(8,128)S(1)}, f32[112,128]{1,0:T(8,128)S(1)}, u32[]{:S(2)}, u32[]{:S(2)}) collective-permute-start(f32[112,128]{1,0:T(8,128)S(1)} %pad_add_fusion.refs_1_), channel_id=1, source_target_pairs={{0,4},{1,5},{2,6},{3,7},{4,0},{5,1},{6,2},{7,3},{8,12},{9,13},{10,... | collective-permute-start | bytes 172040 | tf_op jit(solution)/shard_map/ppermute | solution.py:195
